TPU v7x, 256 devices: a whole 4x4x8 slice. The times are simulated.
256 devices in a mesh: row: 4 (over x), col: 16 (over z, core), depth: 4 (over y).
Axes of the slice: x: 4, y: 4, z: 8, core: 2. Of those that a mesh axis runs over, the one named last changes fastest.
Arguments:
- blocks: bfloat16 [512, 16, 128, 128], P(('row', 'col'), 'depth'), may hold values from -2 to 2
- block_cols: int32 [512, 16], replicated, may hold values from 0 to 511, as said below
- product_cols: int32 [512, 24], P(('row', 'col')), may hold values from 0 to 511, as said below
Outputs:
- purified: bfloat16 [512, 24, 128, 128], P(('row', 'col'), 'depth')
Inputs may be any that keep to these rules, and one draw needn't show every extreme that they name: `block_cols`: the 16 entries of a block row i are distinct, each within 8 of i counted cyclically modulo 512. `product_cols`: the 24 entries of a block row i are distinct, each within 16 of i counted cyclically modulo 512.
All inputs are finite; a program needn't handle non-finite values.
Results may differ from a plain program's by a relative error of at most 0.015.
Values may be sent and summed in bfloat16 or wider, within the bound.
A program may use at most 128 MiB of HBM per device.

v0:
```python
import math

import jax
import jax.numpy as jnp
from jax import lax
from jax.sharding import PartitionSpec as P


def shifted(value, axis, steps):
    count = lax.axis_size(axis)
    pairs = [(source, (source + steps) % count) for source in range(count)]
    return lax.ppermute(value, axis, pairs)


def pick_blocks(block_cols, inner_rows, local_rows, targets, fill_count):
    cols_of = block_cols[inner_rows]
    matches = cols_of[:, :, :, None] == targets[:, None, None, :]
    has_match = jnp.any(matches, axis=2)
    slot_ids = jnp.arange(fill_count, dtype=jnp.int32)[None, None, :, None]
    position = jnp.sum(jnp.where(matches, slot_ids, 0), axis=2)
    block_index = local_rows[:, :, None] * fill_count + position
    return (block_index, has_match)


def stacked_product(left_blocks, block_index, has_match, flat_blocks, slot_groups):
    row_count = left_blocks.shape[0]
    slot_total = left_blocks.shape[1]
    edge = left_blocks.shape[2]
    group_rows = math.gcd(row_count, 2)
    groups = row_count // group_rows
    left_group = left_blocks.reshape((groups, group_rows) + left_blocks.shape[1:])
    index_group = block_index.reshape((groups, group_rows) + block_index.shape[1:])
    match_group = has_match.reshape((groups, group_rows) + has_match.shape[1:])

    def one_group(group_items):
        left_part, index_part, match_part = group_items
        picked = flat_blocks[index_part]
        picked = jnp.where(match_part[:, :, :, None, None], picked, jnp.zeros((), jnp.bfloat16))
        target_count = picked.shape[2]
        left_split = left_part.reshape(
            group_rows, slot_groups, slot_total // slot_groups, edge, edge
        )
        picked_split = picked.reshape(
            group_rows, slot_groups, slot_total // slot_groups, target_count, edge, edge
        )
        partial_value = jnp.einsum(
            "rgsab,rgstbc->rgtac", left_split, picked_split, preferred_element_type=jnp.float32
        )
        return partial_value[:, 0]

    result = lax.map(one_group, (left_group, index_group, match_group))
    return result.reshape((row_count,) + result.shape[2:])


def local(blocks, block_cols, product_cols):
    row_count = blocks.shape[0]
    slot_count = blocks.shape[1]
    block_edge = blocks.shape[2]
    fill_count = block_cols.shape[1]
    order_total = row_count * lax.axis_size(("row", "col"))
    row_place = lax.axis_index(("row", "col"))
    depth_index = lax.axis_index("depth")
    depth_count = lax.axis_size("depth")
    pieces = []
    full_rows = lax.all_gather(blocks, "depth", axis=1, tiled=True)
    for offset in (2, 1, 0, -1, -2):
        pieces.append(full_rows if offset == 0 else shifted(full_rows, ("row", "col"), offset))
    extended = jnp.concatenate(pieces, axis=0)
    flat_blocks = extended.reshape(5 * row_count * fill_count, block_edge, block_edge)
    start_row = (row_place - 2) * row_count
    own_cols = lax.dynamic_slice_in_dim(block_cols, row_place * row_count, row_count, 0)
    target_share = product_cols.shape[1] // depth_count
    inner_rows = lax.dynamic_slice_in_dim(own_cols, depth_index * slot_count, slot_count, 1)
    local_rows = (inner_rows - start_row) % order_total
    block_index, has_match = pick_blocks(
        block_cols, inner_rows, local_rows, product_cols, fill_count
    )
    partial_value = stacked_product(blocks, block_index, has_match, flat_blocks, 1)
    square = lax.psum_scatter(
        partial_value.astype(jnp.bfloat16), "depth", scatter_dimension=1, tiled=True
    )
    inner_second = lax.dynamic_slice_in_dim(
        product_cols, depth_index * target_share, target_share, 1
    )
    local_second = (inner_second - start_row) % order_total
    index_second, match_second = pick_blocks(
        block_cols, inner_second, local_second, product_cols, fill_count
    )
    partial_second = stacked_product(square, index_second, match_second, flat_blocks, 1)
    cubed = lax.psum_scatter(
        partial_second.astype(jnp.bfloat16), "depth", scatter_dimension=1, tiled=True
    ).astype(jnp.float32)
    return (3.0 * square.astype(jnp.float32) - 2.0 * cubed).astype(jnp.bfloat16)


def solution(mesh):
    placed = (P(("row", "col"), "depth", None, None), P(), P(("row", "col"), None))
    return jax.shard_map(
        local,
        mesh=mesh,
        in_specs=placed,
        out_specs=P(("row", "col"), "depth", None, None),
        check_vma=False,
    )
```

profile of v0, /device:TPU:8, one launch (start us, length us, event | category | flops | bytes accessed | tf_op | source)
XLA Modules:
  0.0 786.6 jit_solution(5029403357316123950)
XLA Ops:
  7.3 55.0 %all-gather.2.cloned.1.call-done = bf16[8,16,128,128]{3,2,1,0:T(8,128)(2,1)} async-done(((bf16[8,4,128,128]{3,2,1,0:T(8,128)(2,1)}), bf16[8,16,128,128]{3,2,1,0:T(8,128)(2,1)}) %all-gather.2.cloned.1.call-update) | async-done | bytes 4194320 | tf_op jit(solution)/shard_map/all_gather | solution.py:65
  62.3 1.6 collective-permute-start
  63.8 5.1 collective-permute-start.2
  69.5 0.9 copy.33
  70.6 0.8 fusion.25
  72.0 0.8 fusion.21
  72.8 0.8 compare_reduce_fusion.1
  73.8 85.7 %collective-permute-done = bf16[8,16,128,128]{3,2,1,0:T(8,128)(2,1)} collective-permute-done((bf16[8,16,128,128]{3,2,1,0:T(8,128)(2,1)}, bf16[8,16,128,128]{3,2,1,0:T(8,128)(2,1)}, u32[]{:S(2)}, u32[]{:S(2)}) %collective-permute-start) | collective-permute-done | bytes 4194336 | tf_op jit(solution)/shard_map/ppermute | solution.py:12
  159.4 2.5 constant_dynamic-update-slice_fusion.4
  161.9 41.6 %collective-permute-done.1 = bf16[8,16,128,128]{3,2,1,0:T(8,128)(2,1)} collective-permute-done((bf16[8,16,128,128]{3,2,1,0:T(8,128)(2,1)}, bf16[8,16,128,128]{3,2,1,0:T(8,128)(2,1)}, u32[]{:S(2)}, u32[]{:S(2)}) %collective-permute-start.1) | collective-permute-done | bytes 4194336 | tf_op jit(solution)/shard_map/ppermute | solution.py:12
  203.5 3.0 constant_dynamic-update-slice_fusion.3
  207.2 3.0 constant_dynamic-update-slice_fusion.1
  210.2 3.0 constant_dynamic-update-slice_fusion
  213.3 4.6 broadcast.70.clone
  217.9 4.2 copy-done
  222.1 118.4 %while.20 = (s32[]{:T(128)}, bf16[4,2,24,128,128]{3,4,2,1,0:T(8,128)(2,1)}, pred[4,2,4,24]{3,2,1,0:T(4,128)(4,1)S(1)}, s32[4,2,4,24]{3,2,1,0:T(4,128)S(1)}, bf16...) while((s32[]{:T(128)}, bf16[4,2,24,128,128]{3,4,2,1,0:T(8,128)(2,1)}, ...), condition=%wide.region_3.4_spmd, body=%wide.region_2.3_spmd.sunk | while | flops 808453696 | bytes 34875924 | solution.py:51
  222.2 14.9 %gather_fusion = bf16[192,128,128]{2,1,0:T(8,128)(2,1)} fusion(bf16[640,128,128]{2,1,0:T(8,128)(2,1)} %get-tuple-element.217, s32[1024]{0:T(1024)S(1)} %pad_clamp_fusion.6), kind=kCustom, calls=%fused_computation.clone.1 | custom fusion | bytes 12583680 | tf_op jit(solution)/shard_map/while/body/eval_jaxpr/gather | solution.py:37
  237.2 8.6 %copy.61 = bf16[2,4,24,128,128]{3,4,1,2,0:T(8,128)(2,1)} copy(bf16[2,4,24,128,128]{4,3,2,1,0:T(8,128)(2,1)} %bitcast.88) | data formatting | bytes 12582912 | tf_op jit(solution)/shard_map/while/body/eval_jaxpr/gather | solution.py:37
  245.9 5.8 bitcast_dynamic-update-slice_fusion.4
  251.8 14.9 %gather_fusion = bf16[192,128,128]{2,1,0:T(8,128)(2,1)} fusion(bf16[640,128,128]{2,1,0:T(8,128)(2,1)} %get-tuple-element.217, s32[1024]{0:T(1024)S(1)} %pad_clamp_fusion.6), kind=kCustom, calls=%fused_computation.clone.1 | custom fusion | bytes 12583680 | tf_op jit(solution)/shard_map/while/body/eval_jaxpr/gather | solution.py:37
  266.7 8.6 %copy.61 = bf16[2,4,24,128,128]{3,4,1,2,0:T(8,128)(2,1)} copy(bf16[2,4,24,128,128]{4,3,2,1,0:T(8,128)(2,1)} %bitcast.88) | data formatting | bytes 12582912 | tf_op jit(solution)/shard_map/while/body/eval_jaxpr/gather | solution.py:37
  275.5 5.9 bitcast_dynamic-update-slice_fusion.4
  281.4 14.9 %gather_fusion = bf16[192,128,128]{2,1,0:T(8,128)(2,1)} fusion(bf16[640,128,128]{2,1,0:T(8,128)(2,1)} %get-tuple-element.217, s32[1024]{0:T(1024)S(1)} %pad_clamp_fusion.6), kind=kCustom, calls=%fused_computation.clone.1 | custom fusion | bytes 12583680 | tf_op jit(solution)/shard_map/while/body/eval_jaxpr/gather | solution.py:37
  296.4 8.6 %copy.61 = bf16[2,4,24,128,128]{3,4,1,2,0:T(8,128)(2,1)} copy(bf16[2,4,24,128,128]{4,3,2,1,0:T(8,128)(2,1)} %bitcast.88) | data formatting | bytes 12582912 | tf_op jit(solution)/shard_map/while/body/eval_jaxpr/gather | solution.py:37
  305.1 5.8 bitcast_dynamic-update-slice_fusion.4
  311.0 14.9 %gather_fusion = bf16[192,128,128]{2,1,0:T(8,128)(2,1)} fusion(bf16[640,128,128]{2,1,0:T(8,128)(2,1)} %get-tuple-element.217, s32[1024]{0:T(1024)S(1)} %pad_clamp_fusion.6), kind=kCustom, calls=%fused_computation.clone.1 | custom fusion | bytes 12583680 | tf_op jit(solution)/shard_map/while/body/eval_jaxpr/gather | solution.py:37
  326.0 8.6 %copy.61 = bf16[2,4,24,128,128]{3,4,1,2,0:T(8,128)(2,1)} copy(bf16[2,4,24,128,128]{4,3,2,1,0:T(8,128)(2,1)} %bitcast.88) | data formatting | bytes 12582912 | tf_op jit(solution)/shard_map/while/body/eval_jaxpr/gather | solution.py:37
  334.7 5.8 bitcast_dynamic-update-slice_fusion.4
  340.5 8.6 %copy.35 = bf16[4,2,24,128,128]{4,3,2,1,0:T(8,128)(2,1)} copy(bf16[4,2,24,128,128]{3,4,2,1,0:T(8,128)(2,1)} %get-tuple-element.69) | data formatting | bytes 12582912 | tf_op jit(solution)/shard_map/convert_element_type | solution.py:80
  351.9 126.9 %all-reduce.5.cloned.1.call-done = bf16[8,24,128,128]{3,2,1,0:T(8,128)(2,1)} async-done(((bf16[8,24,128,128]{3,2,1,0:T(8,128)(2,1)}), bf16[8,24,128,128]{3,2,1,0:T(8,128)(2,1)}) %all-reduce.5.cloned.1.call-update) | async-done | bytes 6291472
  478.8 1.5 constant_dynamic-slice_fusion.3
  480.3 4.2 broadcast.70
  484.5 150.9 %while.21 = (s32[]{:T(128)}, bf16[4,2,24,128,128]{3,4,2,1,0:T(8,128)(2,1)}, pred[4,2,6,24]{3,2,1,0:T(8,128)(4,1)S(1)}, s32[4,2,6,24]{3,1,0,2:T(2,128)S(1)}, bf16...) while((s32[]{:T(128)}, bf16[4,2,24,128,128]{3,4,2,1,0:T(8,128)(2,1)}, ...), condition=%wide.region_8.9_spmd, body=%wide.region_7.8_spmd.sunk | while | flops 1212680064 | bytes 50746580 | solution.py:51
  484.6 17.3 %gather_fusion.1 = bf16[288,128,128]{2,1,0:T(8,128)(2,1)} fusion(bf16[640,128,128]{2,1,0:T(8,128)(2,1)} %get-tuple-element.238, s32[1024]{0:T(1024)S(1)} %pad_clamp_fusion.7), kind=kCustom, calls=%fused_computation.1.clone.1 | custom fusion | bytes 18875520 | tf_op jit(solution)/shard_map/while/body/eval_jaxpr/gather | solution.py:37
  501.9 12.7 %copy.64 = bf16[2,6,24,128,128]{3,4,1,2,0:T(8,128)(2,1)} copy(bf16[2,6,24,128,128]{4,3,2,1,0:T(8,128)(2,1)} %bitcast.87) | data formatting | bytes 18874368 | tf_op jit(solution)/shard_map/while/body/eval_jaxpr/gather | solution.py:37
  514.7 7.5 bitcast_dynamic-update-slice_fusion.5
  522.3 17.3 %gather_fusion.1 = bf16[288,128,128]{2,1,0:T(8,128)(2,1)} fusion(bf16[640,128,128]{2,1,0:T(8,128)(2,1)} %get-tuple-element.238, s32[1024]{0:T(1024)S(1)} %pad_clamp_fusion.7), kind=kCustom, calls=%fused_computation.1.clone.1 | custom fusion | bytes 18875520 | tf_op jit(solution)/shard_map/while/body/eval_jaxpr/gather | solution.py:37
  539.6 12.7 %copy.64 = bf16[2,6,24,128,128]{3,4,1,2,0:T(8,128)(2,1)} copy(bf16[2,6,24,128,128]{4,3,2,1,0:T(8,128)(2,1)} %bitcast.87) | data formatting | bytes 18874368 | tf_op jit(solution)/shard_map/while/body/eval_jaxpr/gather | solution.py:37
  552.4 7.5 bitcast_dynamic-update-slice_fusion.5
  560.0 17.3 %gather_fusion.1 = bf16[288,128,128]{2,1,0:T(8,128)(2,1)} fusion(bf16[640,128,128]{2,1,0:T(8,128)(2,1)} %get-tuple-element.238, s32[1024]{0:T(1024)S(1)} %pad_clamp_fusion.7), kind=kCustom, calls=%fused_computation.1.clone.1 | custom fusion | bytes 18875520 | tf_op jit(solution)/shard_map/while/body/eval_jaxpr/gather | solution.py:37
  577.3 12.7 %copy.64 = bf16[2,6,24,128,128]{3,4,1,2,0:T(8,128)(2,1)} copy(bf16[2,6,24,128,128]{4,3,2,1,0:T(8,128)(2,1)} %bitcast.87) | data formatting | bytes 18874368 | tf_op jit(solution)/shard_map/while/body/eval_jaxpr/gather | solution.py:37
  590.1 7.6 bitcast_dynamic-update-slice_fusion.5
  597.8 17.3 %gather_fusion.1 = bf16[288,128,128]{2,1,0:T(8,128)(2,1)} fusion(bf16[640,128,128]{2,1,0:T(8,128)(2,1)} %get-tuple-element.238, s32[1024]{0:T(1024)S(1)} %pad_clamp_fusion.7), kind=kCustom, calls=%fused_computation.1.clone.1 | custom fusion | bytes 18875520 | tf_op jit(solution)/shard_map/while/body/eval_jaxpr/gather | solution.py:37
  615.1 12.7 %copy.64 = bf16[2,6,24,128,128]{3,4,1,2,0:T(8,128)(2,1)} copy(bf16[2,6,24,128,128]{4,3,2,1,0:T(8,128)(2,1)} %bitcast.87) | data formatting | bytes 18874368 | tf_op jit(solution)/shard_map/while/body/eval_jaxpr/gather | solution.py:37
  627.9 7.5 bitcast_dynamic-update-slice_fusion.5
  635.4 8.6 %copy.41 = bf16[4,2,24,128,128]{4,3,2,1,0:T(8,128)(2,1)} copy(bf16[4,2,24,128,128]{3,4,2,1,0:T(8,128)(2,1)} %get-tuple-element.70) | data formatting | bytes 12582912 | tf_op jit(solution)/shard_map/convert_element_type | solution.py:91
  644.1 132.2 %all-reduce.7.cloned.1.call-done = bf16[8,24,128,128]{3,2,1,0:T(8,128)(2,1)} async-done(((bf16[8,24,128,128]{3,2,1,0:T(8,128)(2,1)}), bf16[8,24,128,128]{3,2,1,0:T(8,128)(2,1)}) %all-reduce.7.cloned.1.call-update) | async-done | bytes 6291472
  776.2 3.9 subtract_convert_fusion
  (76 shorter events, 6.6 us)
Async XLA Ops:
  6.5 55.7 %all-gather.2.cloned.1.call-start = ((), (), s32[]{:S(2)}) async-start(), calls=%async_computation | async-start | bytes 5242880 | tf_op jit(solution)/shard_map/all_gather | solution.py:65
  7.3 471.5 %all-reduce.5.cloned.1.call-start = ((), (), s32[]{:S(2)}) async-start(), calls=%async_computation.1 | async-start | bytes 12582912
  62.3 97.2 %collective-permute-start = (bf16[8,16,128,128]{3,2,1,0:T(8,128)(2,1)}, bf16[8,16,128,128]{3,2,1,0:T(8,128)(2,1)}, u32[]{:S(2)}, u32[]{:S(2)}) collective-permute-start(bf16[8,16,128,128]{3,2,1,0:T(8,128)(2,1)} %all-gather.2.cloned.1.call-done), channel_id=1, source_target_pairs={{0,8},{4,12},{8,16},{12,20},{16,24},{20,28},{24,32},{28,36},{32,40... | collective-permute-start | bytes 12582920 | tf_op jit(solution)/shard_map/ppermute | solution.py:12
  63.8 139.7 %collective-permute-start.1 = (bf16[8,16,128,128]{3,2,1,0:T(8,128)(2,1)}, bf16[8,16,128,128]{3,2,1,0:T(8,128)(2,1)}, u32[]{:S(2)}, u32[]{:S(2)}) collective-permute-start(bf16[8,16,128,128]{3,2,1,0:T(8,128)(2,1)} %all-gather.2.cloned.1.call-done), channel_id=1, source_target_pairs={{0,4},{4,8},{8,12},{12,16},{16,20},{20,24},{24,28},{28,32},{32,36}... | collective-permute-start | bytes 12582920 | tf_op jit(solution)/shard_map/ppermute | solution.py:12
  63.8 143.3 %collective-permute-start.2 = (bf16[8,16,128,128]{3,2,1,0:T(8,128)(2,1)}, bf16[8,16,128,128]{3,2,1,0:T(8,128)(2,1)}, u32[]{:S(2)}, u32[]{:S(2)}) collective-permute-start(bf16[8,16,128,128]{3,2,1,0:T(8,128)(2,1)} %all-gather.2.cloned.1.call-done), channel_id=1, source_target_pairs={{0,252},{4,0},{8,4},{12,8},{16,12},{20,16},{24,20},{28,24},{32,28}... | collective-permute-start | bytes 12582920 | tf_op jit(solution)/shard_map/ppermute | solution.py:12
  68.9 141.3 %collective-permute-start.3 = (bf16[8,16,128,128]{3,2,1,0:T(8,128)(2,1)}, bf16[8,16,128,128]{3,2,1,0:T(8,128)(2,1)}, u32[]{:S(2)}, u32[]{:S(2)}) collective-permute-start(bf16[8,16,128,128]{3,2,1,0:T(8,128)(2,1)} %all-gather.2.cloned.1.call-done), channel_id=1, source_target_pairs={{0,248},{4,252},{8,0},{12,4},{16,8},{20,12},{24,16},{28,20},{32,24... | collective-permute-start | bytes 12582920 | tf_op jit(solution)/shard_map/ppermute | solution.py:12
  73.8 132.8 %copy-start.1 = (bf16[8,16,128,128]{3,2,1,0:T(8,128)(2,1)S(1)}, bf16[8,16,128,128]{3,2,1,0:T(8,128)(2,1)}, u32[]{:S(2)}) copy-start(bf16[8,16,128,128]{3,2,1,0:T(8,128)(2,1)} %all-gather.2.cloned.1.call-done) | copy-start | bytes 12582916
  213.3 8.8 %copy-start = (bf16[40,16,128,128]{3,2,1,0:T(8,128)(2,1)}, bf16[40,16,128,128]{3,2,1,0:T(8,128)(2,1)S(1)}, u32[]{:S(2)}) copy-start(bf16[40,16,128,128]{3,2,1,0:T(8,128)(2,1)S(1)} %constant_dynamic-update-slice_fusion) | copy-start | bytes 62914564
  349.1 0.9 copy-start.2
  349.1 1.2 copy-start.3
  349.2 427.1 %all-reduce.7.cloned.1.call-start = ((), (), s32[]{:S(2)}) async-start(), calls=%async_computation.2 | async-start | bytes 12582912
Sparse Core Ops, SparseCore 0:
  9.2 53.0 all-gather.1
  349.3 129.4 all-reduce.4
  644.2 132.0 all-reduce.6
where the time goes:
time: 792 us; the launch traced here: 787 us
  waiting for transfers between devices  442 us (56%)
  local copies, waits for them, and re-layouts  263 us (33%)
  matrix products  53.4 us (7%)
  between operations  13.9 us (2%)
    unnamed x5, waiting for transfers between devices  260 us
    gather x16, local copies, waits for them, and re-layouts, one_group(): picked = flat_blocks[index_part]  214 us
    ppermute x4, waiting for transfers between devices, shifted(): return lax.ppermute(value, axis, pairs)  127 us
    all_gather x1, waiting for transfers between devices, local(): full_rows = lax.all_gather(blocks, 'depth', axis=1, tiled=True)  55 us
    dot_general x8, matrix products, one_group(): jnp.einsum('rgsab,rgstbc->rgtac', left_split, picked_split, preferred_ele...  53.4 us
    unnamed x15, local copies, waits for them, and re-layouts  16.3 us
  transfers between devices with their start and end apart: 7, of which 5 were waited for; matrix products, arithmetic and copies ran while one was open for 2% of the time, Pallas kernels for 0%

commit v1 on v0

v1 whole, which is shorter than its diff:
```python
import functools

import jax
import jax.numpy as jnp
from jax import lax
from jax.experimental import pallas as pl
from jax.experimental.pallas import tpu as pltpu
from jax.sharding import PartitionSpec as P


def shifted(value, axis, steps):
    count = lax.axis_size(axis)
    pairs = [(source, (source + steps) % count) for source in range(count)]
    return lax.ppermute(value, axis, pairs)


def block_table(block_cols, rows, targets, start_row, order_total, fill_count, miss):
    cols_of = block_cols[rows]
    matches = cols_of[:, None, :, :] == targets[:, :, None, None]
    has_match = jnp.any(matches, axis=3)
    slot_ids = jnp.arange(fill_count, dtype=jnp.int32)[None, None, None, :]
    position = jnp.sum(jnp.where(matches, slot_ids, 0), axis=3)
    local_rows = (rows - start_row) % order_total
    flat = local_rows[:, None, :] * fill_count + position
    flat = jnp.clip(flat, 0, miss)
    return jnp.where(has_match, flat, miss).astype(jnp.int32)


def product_kernel(n_out, n_inner, final, idx_ref, left_ref, halo_ref, *rest):
    if final:
        own_ref, out_ref = rest
    else:
        (out_ref,) = rest
    edge = left_ref.shape[-1]

    def body(item, carry):
        row = item // n_out
        col = item % n_out
        acc = jnp.zeros((edge, edge), jnp.float32)
        for inner in range(n_inner):
            pick = idx_ref[item * n_inner + inner]
            acc += jnp.dot(
                left_ref[row, inner], halo_ref[pick], preferred_element_type=jnp.float32
            )
        if final:
            value = 3.0 * own_ref[row, col].astype(jnp.float32) - 2.0 * acc
        else:
            value = acc
        out_ref[row, col] = value.astype(out_ref.dtype)
        return carry

    lax.fori_loop(0, left_ref.shape[0] * n_out, body, 0)


def block_products(table, left, halo, own=None):
    rows, n_inner, edge = left.shape[0], left.shape[1], left.shape[2]
    n_out = table.shape[1]
    final = own is not None
    operands = [table.reshape(-1), left, halo] + ([own] if final else [])
    vmem = pl.BlockSpec(memory_space=pltpu.VMEM)
    flops = 2 * rows * n_out * n_inner * edge ** 3
    moved = sum(int(x.size) * x.dtype.itemsize for x in operands) + rows * n_out * edge * edge * 2
    return pl.pallas_call(
        functools.partial(product_kernel, n_out, n_inner, final),
        out_shape=jax.ShapeDtypeStruct((rows, n_out, edge, edge), jnp.bfloat16),
        in_specs=[pl.BlockSpec(memory_space=pltpu.SMEM)] + [vmem] * (len(operands) - 1),
        out_specs=vmem,
        compiler_params=pltpu.CompilerParams(vmem_limit_bytes=60 * 1024 * 1024),
        cost_estimate=pl.CostEstimate(flops=flops, transcendentals=0, bytes_accessed=moved),
    )(*operands)


def local(blocks, block_cols, product_cols):
    row_count = blocks.shape[0]
    block_edge = blocks.shape[2]
    fill_count = block_cols.shape[1]
    order_total = row_count * lax.axis_size(("row", "col"))
    row_place = lax.axis_index(("row", "col"))
    depth_index = lax.axis_index("depth")
    depth_count = lax.axis_size("depth")
    target_share = product_cols.shape[1] // depth_count
    zero = jnp.zeros((1, block_edge, block_edge), blocks.dtype)

    full_rows = lax.all_gather(blocks, "depth", axis=1, tiled=True)
    near = {offset: shifted(full_rows, ("row", "col"), offset) for offset in (2, 1, -1, -2)}
    near[0] = full_rows

    def halo_of(reach):
        pieces = [near[offset] for offset in range(reach, -reach - 1, -1)]
        flat = jnp.concatenate(pieces, axis=0).reshape(-1, block_edge, block_edge)
        return jnp.concatenate([flat, zero], axis=0)

    own_cols = lax.dynamic_slice_in_dim(block_cols, row_place * row_count, row_count, 0)
    own_targets = lax.dynamic_slice_in_dim(
        product_cols, depth_index * target_share, target_share, 1
    )

    halo_first = halo_of(1)
    table_first = block_table(
        block_cols, own_cols, own_targets, (row_place - 1) * row_count, order_total,
        fill_count, halo_first.shape[0] - 1,
    )
    square = block_products(table_first, full_rows, halo_first)

    square_rows = lax.all_gather(square, "depth", axis=1, tiled=True)
    halo_second = halo_of(2)
    table_second = block_table(
        block_cols, product_cols, own_targets, (row_place - 2) * row_count, order_total,
        fill_count, halo_second.shape[0] - 1,
    )
    return block_products(table_second, square_rows, halo_second, own=square)


def solution(mesh):
    placed = (P(("row", "col"), "depth", None, None), P(), P(("row", "col"), None))
    return jax.shard_map(
        local,
        mesh=mesh,
        in_specs=placed,
        out_specs=P(("row", "col"), "depth", None, None),
        check_vma=False,
    )
```

time: 792 us -> 303 us (0.38)
  waiting for transfers between devices: 442 us -> 186 us
  local copies, waits for them, and re-layouts: 263 us -> 32.7 us
  matrix products: 53.4 us -> 0 us
  Pallas kernels: 0 us -> 49.2 us
    unnamed x5 -> x2, waiting for transfers between devices: 260 us -> 0.73 us
    gather x19 -> x3, local copies, waits for them, and re-layouts: 215 us -> 1.41 us  [block_table(): cols_of = block_cols[rows]]
    dot_general x8 -> x0, matrix products: 53.4 us -> none  [one_group(): jnp.einsum('rgsab,rgstbc->rgtac', left_split, picked_split, preferred_ele...]
    pallas_call x0 -> x2, Pallas kernels: none -> 49.2 us  [block_products(): pl.pallas_call(functools.partial(product_kernel, n_out, n_inner, final),...]
    convert_element_type x2 -> x0, local copies, waits for them, and re-layouts: 17.2 us -> none  [the longest x1 8.62 us: local(): partial_second.astype(jnp.bfloat16)]
    concatenate x1 -> x3, local copies, waits for them, and re-layouts: 3.03 us -> 19 us  [the longest x2 15.9 us: halo_of(): return jnp.concatenate([flat, zero], axis=0)]
    another operation x2 -> x0, local copies, waits for them, and re-layouts: 8.81 us -> none
    unnamed x15 -> x7, local copies, waits for them, and re-layouts: 16.3 us -> 10 us
  transfers between devices with their start and end apart: 7 -> 6, of which waited for: 5 -> 3; matrix products, arithmetic and copies ran while one was open for 2% -> 10% of each run, Pallas kernels for 0% -> 0%
where the time goes in v1:
time: 303 us; the launch traced here: 302 us
  waiting for transfers between devices  186 us (61%)
  Pallas kernels  49.2 us (16%)
  local copies, waits for them, and re-layouts  32.7 us (11%)
  between operations  13.5 us (4%)
  starting transfers between devices  10.5 us (3%)
  other arithmetic  10 us (3%)
    ppermute x4, waiting for transfers between devices, shifted(): return lax.ppermute(value, axis, pairs)  130 us
    all_gather x1, waiting for transfers between devices, local(): full_rows = lax.all_gather(blocks, 'depth', axis=1, tiled=True)  55 us
    pallas_call x2, Pallas kernels, block_products(): pl.pallas_call(functools.partial(product_kernel, n_out, n_inner, final),...  49.2 us
    concatenate x2, local copies, waits for them, and re-layouts, halo_of(): return jnp.concatenate([flat, zero], axis=0)  15.9 us
    ppermute x4, starting transfers between devices, shifted(): return lax.ppermute(value, axis, pairs)  10.5 us
    unnamed x7, local copies, waits for them, and re-layouts  10 us
    concatenate x1, other arithmetic, halo_of(): flat = jnp.concatenate(pieces, axis=0).reshape(-1, block_edge, block_edge)  6.98 us
  transfers between devices with their start and end apart: 6, of which 3 were waited for; matrix products, arithmetic and copies ran while one was open for 10% of the time, Pallas kernels for 0%

profile of v1, /device:TPU:8, one launch (start us, length us, event | category | flops | bytes accessed | tf_op | source)
XLA Modules:
  0.0 301.6 jit_solution(12747522720571843212)
XLA Ops:
  6.5 0.0 all-gather.3.cloned.1.call-start
  6.5 0.7 all-gather.3.cloned.1.call-update
  7.3 0.0 all-gather.5.cloned.1.call-start
  7.3 55.0 %all-gather.3.cloned.1.call-done.left_ref = bf16[8,16,128,128]{3,2,1,0:T(8,128)(2,1)} async-done(((bf16[8,4,128,128]{3,2,1,0:T(8,128)(2,1)}), bf16[8,16,128,128]{3,2,1,0:T(8,128)(2,1)}) %all-gather.3.cloned.1.call-update) | async-done | bytes 4194320 | tf_op jit(solution)/shard_map/all_gather | solution.py:84
  62.3 0.0 collective-permute-start
  62.3 5.1 %collective-permute-start.1 = (bf16[8,16,128,128]{3,2,1,0:T(8,128)(2,1)}, bf16[8,16,128,128]{3,2,1,0:T(8,128)(2,1)}, u32[]{:S(2)}, u32[]{:S(2)}) collective-permute-start(bf16[8,16,128,128]{3,2,1,0:T(8,128)(2,1)} %all-gather.3.cloned.1.call-done.left_ref), channel_id=1, source_target_pairs={{0,252},{4,0},{8,4},{12,8},{16,12},{20,16},{24,20},{28,24},{32,28}... | collective-permute-start | bytes 12582920 | tf_op jit(solution)/shard_map/ppermute | solution.py:14
  67.3 0.9 copy.17
  68.2 0.1 reshape.45
  68.3 0.7 fusion.3
  69.0 0.1 reshape.37
  69.1 0.6 gather_fusion.1
  69.8 0.8 constant_dynamic-slice_fusion
  70.5 1.0 compare_reduce_fusion
  71.5 1.0 fusion.1
  72.5 0.7 select_n.60.idx_ref
  73.2 40.7 %collective-permute-done = bf16[8,16,128,128]{3,2,1,0:T(8,128)(2,1)} collective-permute-done((bf16[8,16,128,128]{3,2,1,0:T(8,128)(2,1)}, bf16[8,16,128,128]{3,2,1,0:T(8,128)(2,1)}, u32[]{:S(2)}, u32[]{:S(2)}) %collective-permute-start) | collective-permute-done | bytes 4194336 | tf_op jit(solution)/shard_map/ppermute | solution.py:14
  113.8 0.0 collective-permute-done.1
  113.8 7.0 %pad_maximum_fusion = bf16[24,16,128,128]{3,2,1,0:T(8,128)(2,1)S(1)} fusion(bf16[8,16,128,128]{3,2,1,0:T(8,128)(2,1)} %collective-permute-done.1, bf16[8,16,128,128]{3,2,1,0:T(8,128)(2,1)} %all-gather.3.cloned.1.call-done.left_ref, bf16[8,16,128,128]{3,2,1,0:T(8,128)(2,1)} %collective-permute-done), kind=kLoop, calls=%fused_computation.2 | loop fusion | flops 12582912 | bytes 25165824 | tf_op jit(solution)/shard_map/concatenate | solution.py:90
  120.8 6.1 %concatenate.13.halo_ref = bf16[385,128,128]{2,1,0:T(8,128)(2,1)} pad(bf16[384,128,128]{2,1,0:T(8,128)(2,1)S(1)} %bitcast.4, bf16[]{:T(256)} %constant.64.clone.1), padding=0_1x0_0x0_0 | pad | bytes 25198594 | tf_op jit(solution)/shard_map/concatenate | solution.py:91
  127.0 21.2 %shard_map.37.rest_0_ = bf16[8,6,128,128]{3,2,1,0:T(8,128)(2,1)} custom-call(s32[768]{0:T(1024)} %select_n.60.idx_ref, bf16[8,16,128,128]{3,2,1,0:T(8,128)(2,1)} %all-gather.3.cloned.1.call-done.left_ref, bf16[385,128,128]{2,1,0:T(8,128)(2,1)} %concatenate.13.halo_ref), custom_call_target="tpu_custom_call" | custom-call | flops 3221225472 | bytes 18385920 | tf_op jit(solution)/shard_map/pallas_call | solution.py:63
  148.2 0.0 all-gather.5.cloned.1.call-update
  148.2 0.1 collective-permute-start.2
  148.3 5.3 %collective-permute-start.3 = (bf16[8,16,128,128]{3,2,1,0:T(8,128)(2,1)}, bf16[8,16,128,128]{3,2,1,0:T(8,128)(2,1)}, u32[]{:S(2)}, u32[]{:S(2)}) collective-permute-start(bf16[8,16,128,128]{3,2,1,0:T(8,128)(2,1)} %all-gather.3.cloned.1.call-done.left_ref), channel_id=1, source_target_pairs={{0,248},{4,252},{8,0},{12,4},{16,8},{20,12},{24,16},{28,20},{32,24... | collective-permute-start | bytes 12582920 | tf_op jit(solution)/shard_map/ppermute | solution.py:14
  153.6 0.7 gather_fusion
  154.3 0.1 copy.18
  154.4 0.2 compare_reduce_fusion.1
  154.6 0.2 fusion
  154.8 0.7 select_n.54.idx_ref
  155.4 0.0 copy-start
  155.4 89.3 %collective-permute-done.2 = bf16[8,16,128,128]{3,2,1,0:T(8,128)(2,1)} collective-permute-done((bf16[8,16,128,128]{3,2,1,0:T(8,128)(2,1)}, bf16[8,16,128,128]{3,2,1,0:T(8,128)(2,1)}, u32[]{:S(2)}, u32[]{:S(2)}) %collective-permute-start.2) | collective-permute-done | bytes 4194336 | tf_op jit(solution)/shard_map/ppermute | solution.py:14
  244.8 2.5 constant_dynamic-update-slice_fusion.4
  247.3 3.0 %constant_dynamic-update-slice_fusion.3 = bf16[40,16,128,128]{3,2,1,0:T(8,128)(2,1)S(1)} fusion(bf16[40,16,128,128]{3,2,1,0:T(8,128)(2,1)S(1)} %constant_dynamic-update-slice_fusion.4, bf16[8,16,128,128]{3,2,1,0:T(8,128)(2,1)} %collective-permute-done), kind=kLoop, calls=%fused_computation.16 | loop fusion | bytes 8388608
  250.3 0.0 copy-done
  250.3 0.6 constant_dynamic-update-slice_fusion.2
  250.9 3.0 %constant_dynamic-update-slice_fusion.1 = bf16[40,16,128,128]{3,2,1,0:T(8,128)(2,1)S(1)} fusion(bf16[40,16,128,128]{3,2,1,0:T(8,128)(2,1)S(1)} %constant_dynamic-update-slice_fusion.2, bf16[8,16,128,128]{3,2,1,0:T(8,128)(2,1)} %collective-permute-done.1), kind=kLoop, calls=%fused_computation.14 | loop fusion | bytes 8388608
  253.9 0.0 collective-permute-done.3
  253.9 3.0 %constant_dynamic-update-slice_fusion = bf16[40,16,128,128]{3,2,1,0:T(8,128)(2,1)S(1)} fusion(bf16[40,16,128,128]{3,2,1,0:T(8,128)(2,1)S(1)} %constant_dynamic-update-slice_fusion.1, bf16[8,16,128,128]{3,2,1,0:T(8,128)(2,1)} %collective-permute-done.3), kind=kLoop, calls=%fused_computation.13 | loop fusion | bytes 8388608 | tf_op jit(solution)/shard_map/concatenate | solution.py:90
  257.0 9.8 %concatenate.15.halo_ref = bf16[641,128,128]{2,1,0:T(8,128)(2,1)} pad(bf16[640,128,128]{2,1,0:T(8,128)(2,1)S(1)} %bitcast.5, bf16[]{:T(256)} %constant.64.clone.1), padding=0_1x0_0x0_0 | pad | bytes 41975808 | tf_op jit(solution)/shard_map/concatenate | solution.py:91
  266.8 0.0 all-gather.5.cloned.1.call-done.left_ref
  266.8 28.0 %shard_map.38 = bf16[8,6,128,128]{3,2,1,0:T(8,128)(2,1)} custom-call(s32[1152]{0:T(1024)} %select_n.54.idx_ref, bf16[8,24,128,128]{3,2,1,0:T(8,128)(2,1)} %all-gather.5.cloned.1.call-done.left_ref, bf16[641,128,128]{2,1,0:T(8,128)(2,1)} %concatenate.15.halo_ref, bf16[8,6,128,128]{3,2,1,0:T(8,128)(2,1)} %shard_map.37.rest_0_), custom_call_target="tpu_custom_call" | custom-call | flops 4831838208 | bytes 30446080 | tf_op jit(solution)/shard_map/pallas_call | solution.py:63
  (4 shorter events, 0.1 us)
Async XLA Ops:
  6.5 55.7 %all-gather.3.cloned.1.call-start = ((), (), s32[]{:S(2)}) async-start(), calls=%async_computation | async-start | bytes 5242880 | tf_op jit(solution)/shard_map/all_gather | solution.py:84
  7.3 259.5 %all-gather.5.cloned.1.call-start = ((), (), s32[]{:S(2)}) async-start(), calls=%async_computation.1 | async-start | bytes 7864320 | tf_op jit(solution)/shard_map/all_gather | solution.py:105
  62.3 51.6 %collective-permute-start = (bf16[8,16,128,128]{3,2,1,0:T(8,128)(2,1)}, bf16[8,16,128,128]{3,2,1,0:T(8,128)(2,1)}, u32[]{:S(2)}, u32[]{:S(2)}) collective-permute-start(bf16[8,16,128,128]{3,2,1,0:T(8,128)(2,1)} %all-gather.3.cloned.1.call-done.left_ref), channel_id=1, source_target_pairs={{0,4},{4,8},{8,12},{12,16},{16,20},{20,24},{24,28},{28,32},{32,36}... | collective-permute-start | bytes 12582920 | tf_op jit(solution)/shard_map/ppermute | solution.py:14
  62.3 51.6 %collective-permute-start.1 = (bf16[8,16,128,128]{3,2,1,0:T(8,128)(2,1)}, bf16[8,16,128,128]{3,2,1,0:T(8,128)(2,1)}, u32[]{:S(2)}, u32[]{:S(2)}) collective-permute-start(bf16[8,16,128,128]{3,2,1,0:T(8,128)(2,1)} %all-gather.3.cloned.1.call-done.left_ref), channel_id=1, source_target_pairs={{0,252},{4,0},{8,4},{12,8},{16,12},{20,16},{24,20},{28,24},{32,28}... | collective-permute-start | bytes 12582920 | tf_op jit(solution)/shard_map/ppermute | solution.py:14
  148.2 96.6 %collective-permute-start.2 = (bf16[8,16,128,128]{3,2,1,0:T(8,128)(2,1)}, bf16[8,16,128,128]{3,2,1,0:T(8,128)(2,1)}, u32[]{:S(2)}, u32[]{:S(2)}) collective-permute-start(bf16[8,16,128,128]{3,2,1,0:T(8,128)(2,1)} %all-gather.3.cloned.1.call-done.left_ref), channel_id=1, source_target_pairs={{0,8},{4,12},{8,16},{12,20},{16,24},{20,28},{24,32},{28,36},{32,40... | collective-permute-start | bytes 12582920 | tf_op jit(solution)/shard_map/ppermute | solution.py:14
  148.3 105.7 %collective-permute-start.3 = (bf16[8,16,128,128]{3,2,1,0:T(8,128)(2,1)}, bf16[8,16,128,128]{3,2,1,0:T(8,128)(2,1)}, u32[]{:S(2)}, u32[]{:S(2)}) collective-permute-start(bf16[8,16,128,128]{3,2,1,0:T(8,128)(2,1)} %all-gather.3.cloned.1.call-done.left_ref), channel_id=1, source_target_pairs={{0,248},{4,252},{8,0},{12,4},{16,8},{20,12},{24,16},{28,20},{32,24... | collective-permute-start | bytes 12582920 | tf_op jit(solution)/shard_map/ppermute | solution.py:14
  155.4 94.9 %copy-start = (bf16[8,16,128,128]{3,2,1,0:T(8,128)(2,1)S(1)}, bf16[8,16,128,128]{3,2,1,0:T(8,128)(2,1)}, u32[]{:S(2)}) copy-start(bf16[8,16,128,128]{3,2,1,0:T(8,128)(2,1)} %all-gather.3.cloned.1.call-done.left_ref) | copy-start | bytes 12582916
Sparse Core Ops, SparseCore 0:
  9.2 53.0 all-gather.2
  148.3 67.1 all-gather.4

commit v2 on v1

v2 whole, which is shorter than its diff:
```python
import functools

import jax
import jax.numpy as jnp
from jax import lax
from jax.experimental import pallas as pl
from jax.experimental.pallas import tpu as pltpu
from jax.sharding import PartitionSpec as P


def shifted(value, axis, steps):
    count = lax.axis_size(axis)
    pairs = [(source, (source + steps) % count) for source in range(count)]
    return lax.ppermute(value, axis, pairs)


def block_table(block_cols, rows, targets, start_row, order_total, fill_count, miss):
    cols_of = block_cols[rows]
    matches = cols_of[:, None, :, :] == targets[:, :, None, None]
    has_match = jnp.any(matches, axis=3)
    slot_ids = jnp.arange(fill_count, dtype=jnp.int32)[None, None, None, :]
    position = jnp.sum(jnp.where(matches, slot_ids, 0), axis=3)
    local_rows = (rows - start_row) % order_total
    flat = local_rows[:, None, :] * fill_count + position
    flat = jnp.clip(flat, 0, miss)
    return jnp.where(has_match, flat, miss).astype(jnp.int32)


def product_kernel(n_out, n_inner, n_pieces, final, idx_ref, left_ref, *rest):
    pieces = rest[:n_pieces]
    rest = rest[n_pieces:]
    if final:
        own_ref, out_ref, halo, lcat, rcat, sems = rest
    else:
        out_ref, halo, lcat, rcat, sems = rest
    edge = left_ref.shape[-1]
    span = pieces[0].shape[0]
    copies = [
        pltpu.make_async_copy(piece, halo.at[pl.ds(k * span, span)], sems.at[k])
        for k, piece in enumerate(pieces)
    ]
    for copy in copies:
        copy.start()
    halo[n_pieces * span] = jnp.zeros((edge, edge), halo.dtype)
    for copy in copies:
        copy.wait()

    def row_body(row, carry):
        for inner in range(n_inner):
            lcat[:, inner * edge:(inner + 1) * edge] = left_ref[row, inner]

        def col_body(col, carry):
            item = row * n_out + col
            for inner in range(n_inner):
                pick = idx_ref[item * n_inner + inner]
                rcat[inner * edge:(inner + 1) * edge, :] = halo[pick]
            acc = jnp.dot(lcat[...], rcat[...], preferred_element_type=jnp.float32)
            if final:
                value = 3.0 * own_ref[row, col].astype(jnp.float32) - 2.0 * acc
            else:
                value = acc
            out_ref[row, col] = value.astype(out_ref.dtype)
            return carry

        return lax.fori_loop(0, n_out, col_body, carry)

    lax.fori_loop(0, left_ref.shape[0], row_body, 0)


def block_products(table, left, pieces, own=None):
    rows, n_inner, edge = left.shape[0], left.shape[1], left.shape[2]
    n_out = table.shape[1]
    final = own is not None
    flat_pieces = [piece.reshape(-1, edge, edge) for piece in pieces]
    span = flat_pieces[0].shape[0]
    operands = [table.reshape(-1), left] + flat_pieces + ([own] if final else [])
    vmem = pl.BlockSpec(memory_space=pltpu.VMEM)
    anywhere = pl.BlockSpec(memory_space=pl.ANY)
    in_specs = [pl.BlockSpec(memory_space=pltpu.SMEM), vmem] + [anywhere] * len(pieces)
    in_specs += [vmem] if final else []
    flops = 2 * rows * n_out * n_inner * edge ** 3
    moved = sum(int(x.size) * x.dtype.itemsize for x in operands) + rows * n_out * edge * edge * 2
    return pl.pallas_call(
        functools.partial(product_kernel, n_out, n_inner, len(pieces), final),
        out_shape=jax.ShapeDtypeStruct((rows, n_out, edge, edge), jnp.bfloat16),
        in_specs=in_specs,
        out_specs=vmem,
        scratch_shapes=[
            pltpu.VMEM((len(pieces) * span + 1, edge, edge), left.dtype),
            pltpu.VMEM((edge, n_inner * edge), left.dtype),
            pltpu.VMEM((n_inner * edge, edge), left.dtype),
            pltpu.SemaphoreType.DMA((len(pieces),)),
        ],
        compiler_params=pltpu.CompilerParams(vmem_limit_bytes=62 * 1024 * 1024),
        cost_estimate=pl.CostEstimate(flops=flops, transcendentals=0, bytes_accessed=moved),
    )(*operands)


def local(blocks, block_cols, product_cols):
    row_count = blocks.shape[0]
    block_edge = blocks.shape[2]
    fill_count = block_cols.shape[1]
    order_total = row_count * lax.axis_size(("row", "col"))
    row_place = lax.axis_index(("row", "col"))
    depth_index = lax.axis_index("depth")
    depth_count = lax.axis_size("depth")
    target_share = product_cols.shape[1] // depth_count

    full_rows = lax.all_gather(blocks, "depth", axis=1, tiled=True)
    near = {0: full_rows}
    near[1] = shifted(full_rows, ("row", "col"), 1)
    near[-1] = shifted(full_rows, ("row", "col"), -1)
    near[2] = shifted(near[1], ("row", "col"), 1)
    near[-2] = shifted(near[-1], ("row", "col"), -1)

    def halo_of(reach):
        return [near[offset] for offset in range(reach, -reach - 1, -1)]

    own_cols = lax.dynamic_slice_in_dim(block_cols, row_place * row_count, row_count, 0)
    own_targets = lax.dynamic_slice_in_dim(
        product_cols, depth_index * target_share, target_share, 1
    )

    halo_first = halo_of(1)
    table_first = block_table(
        block_cols, own_cols, own_targets, (row_place - 1) * row_count, order_total,
        fill_count, len(halo_first) * row_count * fill_count,
    )
    square = block_products(table_first, full_rows, halo_first)

    square_rows = lax.all_gather(square, "depth", axis=1, tiled=True)
    halo_second = halo_of(2)
    table_second = block_table(
        block_cols, product_cols, own_targets, (row_place - 2) * row_count, order_total,
        fill_count, len(halo_second) * row_count * fill_count,
    )
    return block_products(table_second, square_rows, halo_second, own=square)


def solution(mesh):
    placed = (P(("row", "col"), "depth", None, None), P(), P(("row", "col"), None))
    return jax.shard_map(
        local,
        mesh=mesh,
        in_specs=placed,
        out_specs=P(("row", "col"), "depth", None, None),
        check_vma=False,
    )
```

time: 303 us -> 245 us (0.81)
  local copies, waits for them, and re-layouts: 32.7 us -> 4.57 us
  waiting for transfers between devices: 186 us -> 162 us
  other arithmetic: 10 us -> 2.37 us
  Pallas kernels: 49.2 us -> 55.7 us
  starting transfers between devices: 10.5 us -> 5.5 us
    ppermute x4, waiting for transfers between devices: 130 us -> 95.7 us  [shifted(): return lax.ppermute(value, axis, pairs)]
    concatenate x3 -> x0, local copies, waits for them, and re-layouts: 19 us -> none  [the longest x2 15.9 us: halo_of(): return jnp.concatenate([flat, zero], axis=0)]
    all_gather x1, waiting for transfers between devices: 0.01 us -> 10.4 us  [local(): square_rows = lax.all_gather(square, 'depth', axis=1, tiled=True)]
    unnamed x7 -> x3, local copies, waits for them, and re-layouts: 10 us -> 0.88 us
    concatenate x1 -> x0, other arithmetic: 6.98 us -> none  [halo_of(): flat = jnp.concatenate(pieces, axis=0).reshape(-1, block_edge, block_edge)]
    pallas_call x2, Pallas kernels: 49.2 us -> 55.7 us  [block_products(): pl.pallas_call(functools.partial(product_kernel, n_out, n_inner, len(piec...]
    ppermute x4, starting transfers between devices: 10.5 us -> 5.46 us  [shifted(): return lax.ppermute(value, axis, pairs)]
  transfers between devices with their start and end apart: 6 -> 6, of which waited for: 3 -> 6; matrix products, arithmetic and copies ran while one was open for 10% -> 3% of each run, Pallas kernels for 0% -> 0%
where the time goes in v2:
time: 245 us; the launch traced here: 243 us
  waiting for transfers between devices  162 us (66%)
  Pallas kernels  55.7 us (23%)
  between operations  13.5 us (6%)
  starting transfers between devices  5.5 us (2%)
  local copies, waits for them, and re-layouts  4.57 us (2%)
    ppermute x4, waiting for transfers between devices, shifted(): return lax.ppermute(value, axis, pairs)  95.7 us
    pallas_call x2, Pallas kernels, block_products(): pl.pallas_call(functools.partial(product_kernel, n_out, n_inner, len(piec...  55.7 us
    all_gather x1, waiting for transfers between devices, local(): full_rows = lax.all_gather(blocks, 'depth', axis=1, tiled=True)  55 us
    all_gather x1, waiting for transfers between devices, local(): square_rows = lax.all_gather(square, 'depth', axis=1, tiled=True)  10.4 us
    ppermute x4, starting transfers between devices, shifted(): return lax.ppermute(value, axis, pairs)  5.46 us
  transfers between devices with their start and end apart: 6, of which 6 were waited for; matrix products, arithmetic and copies ran while one was open for 3% of the time, Pallas kernels for 0%

profile of v2, /device:TPU:8, one launch (start us, length us, event | category | flops | bytes accessed | tf_op | source)
XLA Modules:
  0.0 243.5 jit_solution(18433461428288567383)
XLA Ops:
  6.5 0.0 all-gather.3.cloned.1.call-start
  6.5 0.7 all-gather.3.cloned.1.call-update
  7.3 0.0 all-gather.5.cloned.1.call-start
  7.3 55.0 %all-gather.3.cloned.1.call-done.left_ref = bf16[8,16,128,128]{3,2,1,0:T(8,128)(2,1)} async-done(((bf16[8,4,128,128]{3,2,1,0:T(8,128)(2,1)}), bf16[8,16,128,128]{3,2,1,0:T(8,128)(2,1)}) %all-gather.3.cloned.1.call-update) | async-done | bytes 4194320 | tf_op jit(solution)/shard_map/all_gather | solution.py:109
  62.3 4.9 %collective-permute-start.1 = (bf16[8,16,128,128]{3,2,1,0:T(8,128)(2,1)}, bf16[8,16,128,128]{3,2,1,0:T(8,128)(2,1)}, u32[]{:S(2)}, u32[]{:S(2)}) collective-permute-start(bf16[8,16,128,128]{3,2,1,0:T(8,128)(2,1)} %all-gather.3.cloned.1.call-done.left_ref), channel_id=1, source_target_pairs={{0,252},{4,0},{8,4},{12,8},{16,12},{20,16},{24,20},{28,24},{32,28}... | collective-permute-start | bytes 12582920 | tf_op jit(solution)/shard_map/ppermute | solution.py:14
  67.2 0.0 collective-permute-start
  67.2 0.9 copy.17
  68.1 0.1 reshape.60
  68.2 0.6 gather_fusion.1
  68.8 0.8 constant_dynamic-slice_fusion
  69.6 1.0 compare_reduce_fusion
  70.5 1.0 fusion.1
  71.5 0.7 select_n.60.idx_ref
  72.2 41.3 %collective-permute-done.1 = bf16[8,16,128,128]{3,2,1,0:T(8,128)(2,1)} collective-permute-done((bf16[8,16,128,128]{3,2,1,0:T(8,128)(2,1)}, bf16[8,16,128,128]{3,2,1,0:T(8,128)(2,1)}, u32[]{:S(2)}, u32[]{:S(2)}) %collective-permute-start.1) | collective-permute-done | bytes 4194336 | tf_op jit(solution)/shard_map/ppermute | solution.py:14
  113.5 5.2 %collective-permute-done = bf16[8,16,128,128]{3,2,1,0:T(8,128)(2,1)} collective-permute-done((bf16[8,16,128,128]{3,2,1,0:T(8,128)(2,1)}, bf16[8,16,128,128]{3,2,1,0:T(8,128)(2,1)}, u32[]{:S(2)}, u32[]{:S(2)}) %collective-permute-start) | collective-permute-done | bytes 4194336 | tf_op jit(solution)/shard_map/ppermute | solution.py:14
  118.7 0.0 copy-start
  118.7 24.2 %shard_map.37.rest_5_ = bf16[8,6,128,128]{3,2,1,0:T(8,128)(2,1)} custom-call(s32[768]{0:T(1024)} %select_n.60.idx_ref, bf16[8,16,128,128]{3,2,1,0:T(8,128)(2,1)} %all-gather.3.cloned.1.call-done.left_ref, bf16[128,128,128]{2,1,0:T(8,128)(2,1)} %bitcast.2.rest_0_.rest_1_, bf16[128,128,128]{2,1,0:T(8,128)(2,1)} %bitcast.7, ...), custom_call_target="tpu_custom_call" | custom-call | flops 3221225472 | bytes 18353152 | tf_op jit(solution)/shard_map/pallas_call | solution.py:83
  142.9 0.0 all-gather.5.cloned.1.call-update
  142.9 0.1 collective-permute-start.3
  143.0 0.5 collective-permute-start.2
  143.5 0.0 copy-done
  143.5 0.1 reshape.52
  143.6 0.7 gather_fusion
  144.3 0.1 copy.18
  144.4 0.2 compare_reduce_fusion.1
  144.6 0.2 fusion
  144.8 0.7 select_n.54.idx_ref
  145.5 43.9 %collective-permute-done.3 = bf16[8,16,128,128]{3,2,1,0:T(8,128)(2,1)} collective-permute-done((bf16[8,16,128,128]{3,2,1,0:T(8,128)(2,1)}, bf16[8,16,128,128]{3,2,1,0:T(8,128)(2,1)}, u32[]{:S(2)}, u32[]{:S(2)}) %collective-permute-start.3) | collective-permute-done | bytes 4194336 | tf_op jit(solution)/shard_map/ppermute | solution.py:14
  189.4 5.3 %collective-permute-done.2 = bf16[8,16,128,128]{3,2,1,0:T(8,128)(2,1)} collective-permute-done((bf16[8,16,128,128]{3,2,1,0:T(8,128)(2,1)}, bf16[8,16,128,128]{3,2,1,0:T(8,128)(2,1)}, u32[]{:S(2)}, u32[]{:S(2)}) %collective-permute-start.2) | collective-permute-done | bytes 4194336 | tf_op jit(solution)/shard_map/ppermute | solution.py:14
  194.7 10.4 %all-gather.5.cloned.1.call-done.left_ref = bf16[8,24,128,128]{3,2,1,0:T(8,128)(2,1)} async-done(((bf16[8,6,128,128]{3,2,1,0:T(8,128)(2,1)}), bf16[8,24,128,128]{3,2,1,0:T(8,128)(2,1)}) %all-gather.5.cloned.1.call-update) | async-done | bytes 6291472 | tf_op jit(solution)/shard_map/all_gather | solution.py:131
  205.0 31.6 %shard_map.38 = bf16[8,6,128,128]{3,2,1,0:T(8,128)(2,1)} custom-call(s32[1152]{0:T(1024)} %select_n.54.idx_ref, bf16[8,24,128,128]{3,2,1,0:T(8,128)(2,1)} %all-gather.5.cloned.1.call-done.left_ref, bf16[128,128,128]{2,1,0:T(8,128)(2,1)} %bitcast.5.rest_0_, bf16[128,128,128]{2,1,0:T(8,128)(2,1)} %bitcast.2.rest_0_.rest_1_, bf16[128,128,128]{2,1,0:T(8,128)(2,1)} %bitcast.8, ...), custom_call_target="tpu_custom_call" | custom-call | flops 4831838208 | bytes 30413312 | tf_op jit(solution)/shard_map/pallas_call | solution.py:83
  (6 shorter events, 0.1 us)
Async XLA Ops:
  6.5 55.7 %all-gather.3.cloned.1.call-start = ((), (), s32[]{:S(2)}) async-start(), calls=%async_computation | async-start | bytes 5242880 | tf_op jit(solution)/shard_map/all_gather | solution.py:109
  7.3 197.8 %all-gather.5.cloned.1.call-start = ((), (), s32[]{:S(2)}) async-start(), calls=%async_computation.1 | async-start | bytes 7864320 | tf_op jit(solution)/shard_map/all_gather | solution.py:131
  62.3 51.2 %collective-permute-start.1 = (bf16[8,16,128,128]{3,2,1,0:T(8,128)(2,1)}, bf16[8,16,128,128]{3,2,1,0:T(8,128)(2,1)}, u32[]{:S(2)}, u32[]{:S(2)}) collective-permute-start(bf16[8,16,128,128]{3,2,1,0:T(8,128)(2,1)} %all-gather.3.cloned.1.call-done.left_ref), channel_id=1, source_target_pairs={{0,252},{4,0},{8,4},{12,8},{16,12},{20,16},{24,20},{28,24},{32,28}... | collective-permute-start | bytes 12582920 | tf_op jit(solution)/shard_map/ppermute | solution.py:14
  67.2 51.6 %collective-permute-start = (bf16[8,16,128,128]{3,2,1,0:T(8,128)(2,1)}, bf16[8,16,128,128]{3,2,1,0:T(8,128)(2,1)}, u32[]{:S(2)}, u32[]{:S(2)}) collective-permute-start(bf16[8,16,128,128]{3,2,1,0:T(8,128)(2,1)} %all-gather.3.cloned.1.call-done.left_ref), channel_id=1, source_target_pairs={{0,4},{4,8},{8,12},{12,16},{16,20},{20,24},{24,28},{28,32},{32,36}... | collective-permute-start | bytes 12582920 | tf_op jit(solution)/shard_map/ppermute | solution.py:14
  118.7 24.8 %copy-start = (s32[8,24]{1,0:T(8,128)S(1)}, s32[8,24]{1,0:T(8,128)}, u32[]{:S(2)}) copy-start(s32[8,24]{1,0:T(8,128)} %param.5) | copy-start | bytes 2308
  142.9 46.4 %collective-permute-start.3 = (bf16[8,16,128,128]{3,2,1,0:T(8,128)(2,1)}, bf16[8,16,128,128]{3,2,1,0:T(8,128)(2,1)}, u32[]{:S(2)}, u32[]{:S(2)}) collective-permute-start(bf16[8,16,128,128]{3,2,1,0:T(8,128)(2,1)} %collective-permute-done.1), channel_id=1, source_target_pairs={{0,252},{4,0},{8,4},{12,8},{16,12},{20,16},{24,20},{28,24},{32,28}... | collective-permute-start | bytes 12582920 | tf_op jit(solution)/shard_map/ppermute | solution.py:14
  143.0 51.6 %collective-permute-start.2 = (bf16[8,16,128,128]{3,2,1,0:T(8,128)(2,1)}, bf16[8,16,128,128]{3,2,1,0:T(8,128)(2,1)}, u32[]{:S(2)}, u32[]{:S(2)}) collective-permute-start(bf16[8,16,128,128]{3,2,1,0:T(8,128)(2,1)} %collective-permute-done), channel_id=1, source_target_pairs={{0,4},{4,8},{8,12},{12,16},{16,20},{20,24},{24,28},{28,32},{32,36}... | collective-permute-start | bytes 12582920 | tf_op jit(solution)/shard_map/ppermute | solution.py:14
Sparse Core Ops, SparseCore 0:
  9.2 53.0 all-gather.2
  143.0 61.9 all-gather.4

commit v3 on v2

--- a/solution.py
+++ b/solution.py
@@ -23,16 +23,22 @@
     local_rows = (rows - start_row) % order_total
     flat = local_rows[:, None, :] * fill_count + position
     flat = jnp.clip(flat, 0, miss)
-    return jnp.where(has_match, flat, miss).astype(jnp.int32)
+    flat = jnp.where(has_match, flat, miss).astype(jnp.int32)
+    inner = jnp.broadcast_to(jnp.arange(rows.shape[1], dtype=jnp.int32), flat.shape)
+    order = jnp.argsort(jnp.logical_not(has_match).astype(jnp.int32), axis=2, stable=True)
+    picks = jnp.take_along_axis(flat, order, axis=2)
+    inners = jnp.take_along_axis(inner, order, axis=2)
+    counts = jnp.sum(has_match.astype(jnp.int32), axis=2)
+    return picks, inners, counts
 
 
-def product_kernel(n_out, n_inner, n_pieces, final, idx_ref, left_ref, *rest):
+def product_kernel(n_out, n_inner, n_pieces, final, idx_ref, inner_ref, count_ref, left_ref, *rest):
     pieces = rest[:n_pieces]
     rest = rest[n_pieces:]
     if final:
-        own_ref, out_ref, halo, lcat, rcat, sems = rest
+        own_ref, out_ref, halo, sems = rest
     else:
-        out_ref, halo, lcat, rcat, sems = rest
+        out_ref, halo, sems = rest
     edge = left_ref.shape[-1]
     span = pieces[0].shape[0]
     copies = [
@@ -41,44 +47,49 @@
     ]
     for copy in copies:
         copy.start()
-    halo[n_pieces * span] = jnp.zeros((edge, edge), halo.dtype)
     for copy in copies:
         copy.wait()
 
-    def row_body(row, carry):
-        for inner in range(n_inner):
-            lcat[:, inner * edge:(inner + 1) * edge] = left_ref[row, inner]
+    def item_body(item, carry):
+        row = item // n_out
+        col = item % n_out
+        base = item * n_inner
 
-        def col_body(col, carry):
-            item = row * n_out + col
-            for inner in range(n_inner):
-                pick = idx_ref[item * n_inner + inner]
-                rcat[inner * edge:(inner + 1) * edge, :] = halo[pick]
-            acc = jnp.dot(lcat[...], rcat[...], preferred_element_type=jnp.float32)
-            if final:
-                value = 3.0 * own_ref[row, col].astype(jnp.float32) - 2.0 * acc
-            else:
-                value = acc
-            out_ref[row, col] = value.astype(out_ref.dtype)
-            return carry
+        def inner_body(k, acc):
+            pick = idx_ref[base + k]
+            slot = inner_ref[base + k]
+            return acc + jnp.dot(
+                left_ref[row, slot], halo[pick], preferred_element_type=jnp.float32
+            )
 
-        return lax.fori_loop(0, n_out, col_body, carry)
+        acc = lax.fori_loop(
+            0, count_ref[item], inner_body, jnp.zeros((edge, edge), jnp.float32)
+        )
+        if final:
+            value = 3.0 * own_ref[row, col].astype(jnp.float32) - 2.0 * acc
+        else:
+            value = acc
+        out_ref[row, col] = value.astype(out_ref.dtype)
+        return carry
 
-    lax.fori_loop(0, left_ref.shape[0], row_body, 0)
+    lax.fori_loop(0, left_ref.shape[0] * n_out, item_body, 0)
 
 
 def block_products(table, left, pieces, own=None):
+    picks, inners, counts = table
     rows, n_inner, edge = left.shape[0], left.shape[1], left.shape[2]
-    n_out = table.shape[1]
+    n_out = picks.shape[1]
     final = own is not None
     flat_pieces = [piece.reshape(-1, edge, edge) for piece in pieces]
     span = flat_pieces[0].shape[0]
-    operands = [table.reshape(-1), left] + flat_pieces + ([own] if final else [])
+    tables = [picks.reshape(-1), inners.reshape(-1), counts.reshape(-1)]
+    operands = tables + [left] + flat_pieces + ([own] if final else [])
     vmem = pl.BlockSpec(memory_space=pltpu.VMEM)
+    smem = pl.BlockSpec(memory_space=pltpu.SMEM)
     anywhere = pl.BlockSpec(memory_space=pl.ANY)
-    in_specs = [pl.BlockSpec(memory_space=pltpu.SMEM), vmem] + [anywhere] * len(pieces)
+    in_specs = [smem] * 3 + [vmem] + [anywhere] * len(pieces)
     in_specs += [vmem] if final else []
-    flops = 2 * rows * n_out * n_inner * edge ** 3
+    flops = rows * n_out * n_inner * edge ** 3
     moved = sum(int(x.size) * x.dtype.itemsize for x in operands) + rows * n_out * edge * edge * 2
     return pl.pallas_call(
         functools.partial(product_kernel, n_out, n_inner, len(pieces), final),
@@ -86,9 +97,7 @@
         in_specs=in_specs,
         out_specs=vmem,
         scratch_shapes=[
-            pltpu.VMEM((len(pieces) * span + 1, edge, edge), left.dtype),
-            pltpu.VMEM((edge, n_inner * edge), left.dtype),
-            pltpu.VMEM((n_inner * edge, edge), left.dtype),
+            pltpu.VMEM((len(pieces) * span, edge, edge), left.dtype),
             pltpu.SemaphoreType.DMA((len(pieces),)),
         ],
         compiler_params=pltpu.CompilerParams(vmem_limit_bytes=62 * 1024 * 1024),

time: 245 us -> 340 us (1.39); the launches traced: 243 us -> 335 us
  Pallas kernels: 55.7 us -> 139 us
  local copies, waits for them, and re-layouts: 4.57 us -> 32.8 us
  waiting for transfers between devices: 162 us -> 135 us
  other arithmetic: 2.37 us -> 9.22 us
    pallas_call x2, Pallas kernels: 55.7 us -> 139 us  [block_products(): pl.pallas_call(functools.partial(product_kernel, n_out, n_inner, len(piec...]
    ppermute x4, waiting for transfers between devices: 95.7 us -> 60.5 us  [shifted(): return lax.ppermute(value, axis, pairs)]
    gather x0 -> x14, local copies, waits for them, and re-layouts: none -> 25 us  [the longest x9 12.7 us: block_table(): picks = jnp.take_along_axis(flat, order, axis=2)]
    all_gather x1, waiting for transfers between devices: 10.4 us -> 18.5 us  [local(): square_rows = lax.all_gather(square, 'depth', axis=1, tiled=True)]
    sort x0 -> x2, other arithmetic: none -> 6.32 us  [block_table(): jnp.argsort(jnp.logical_not(has_match).astype(jnp.int32), axis=2, stable=...]
    reshape x0 -> x6, local copies, waits for them, and re-layouts: none -> 3.94 us  [block_products(): tables = [picks.reshape(-1), inners.reshape(-1), counts.reshape(-1)]]
  transfers between devices with their start and end apart: 6 -> 6, of which waited for: 6 -> 6; matrix products, arithmetic and copies ran while one was open for 3% -> 13% of each run, Pallas kernels for 0% -> 0%
where the time goes in v3:
time: 340 us; the launch traced here: 335 us
  Pallas kernels  139 us (41%)
  waiting for transfers between devices  135 us (40%)
  local copies, waits for them, and re-layouts  32.8 us (10%)
  between operations  13.6 us (4%)
  other arithmetic  9.22 us (3%)
  starting transfers between devices  5.5 us (2%)
    pallas_call x2, Pallas kernels, block_products(): pl.pallas_call(functools.partial(product_kernel, n_out, n_inner, len(piec...  139 us
    ppermute x4, waiting for transfers between devices, shifted(): return lax.ppermute(value, axis, pairs)  60.5 us
    all_gather x1, waiting for transfers between devices, local(): full_rows = lax.all_gather(blocks, 'depth', axis=1, tiled=True)  55 us
    all_gather x1, waiting for transfers between devices, local(): square_rows = lax.all_gather(square, 'depth', axis=1, tiled=True)  18.5 us
    gather x9, local copies, waits for them, and re-layouts, block_table(): picks = jnp.take_along_axis(flat, order, axis=2)  12.7 us
    gather x5, local copies, waits for them, and re-layouts, block_table(): inners = jnp.take_along_axis(inner, order, axis=2)  12.4 us
  transfers between devices with their start and end apart: 6, of which 6 were waited for; matrix products, arithmetic and copies ran while one was open for 13% of the time, Pallas kernels for 0%

profile of v3, /device:TPU:8, one launch (start us, length us, event | category | flops | bytes accessed | tf_op | source)
XLA Modules:
  0.0 334.9 jit_solution(436739943988944981)
XLA Ops:
  6.5 0.7 all-gather.3.cloned.1.call-update
  7.3 55.0 %all-gather.3.cloned.1.call-done.left_ref = bf16[8,16,128,128]{3,2,1,0:T(8,128)(2,1)} async-done(((bf16[8,4,128,128]{3,2,1,0:T(8,128)(2,1)}), bf16[8,16,128,128]{3,2,1,0:T(8,128)(2,1)}) %all-gather.3.cloned.1.call-update) | async-done | bytes 4194320 | tf_op jit(solution)/shard_map/all_gather | solution.py:118
  62.3 4.9 %collective-permute-start.1 = (bf16[8,16,128,128]{3,2,1,0:T(8,128)(2,1)}, bf16[8,16,128,128]{3,2,1,0:T(8,128)(2,1)}, u32[]{:S(2)}, u32[]{:S(2)}) collective-permute-start(bf16[8,16,128,128]{3,2,1,0:T(8,128)(2,1)} %all-gather.3.cloned.1.call-done.left_ref), channel_id=1, source_target_pairs={{0,252},{4,0},{8,4},{12,8},{16,12},{20,16},{24,20},{28,24},{32,28}... | collective-permute-start | bytes 12582920 | tf_op jit(solution)/shard_map/ppermute | solution.py:14
  67.2 0.9 copy.45
  68.1 0.1 reshape.106
  68.2 0.6 gather_fusion.1
  68.8 0.8 constant_dynamic-slice_fusion
  69.6 1.0 compare_reduce_fusion
  70.5 1.0 fusion.1
  71.5 0.2 convert_reduce_fusion
  71.7 0.6 reshape.64.count_ref
  72.3 0.1 copy.64
  72.5 2.9 sort.35
  75.4 0.1 copy.65
  75.5 0.1 reshape.147
  75.6 4.9 %gather_fusion.5 = s32[768]{0:T(1024)S(1)} fusion(s32[8,6,16]{2,1,0:T(8,128)S(1)} %iota.29, s32[768]{0:T(1024)S(1)} %reshape.147), kind=kCustom, calls=%fused_computation.3.clone | custom fusion | bytes 15360 | tf_op jit(solution)/shard_map/jit(take_along_axis)/gather | solution.py:30
  80.6 4.9 %gather_fusion.4 = s32[768]{0:T(1024)S(1)} fusion(s32[8,6,16]{2,1,0:T(8,128)S(1)} %get-tuple-element.18, s32[768]{0:T(1024)S(1)} %reshape.147), kind=kCustom, calls=%fused_computation.1.clone | custom fusion | bytes 15360 | tf_op jit(solution)/shard_map/jit(take_along_axis)/gather | solution.py:29
  85.6 0.1 copy.69
  85.8 0.1 copy.70
  85.9 0.7 reshape.63.inner_ref
  86.6 0.1 copy.66
  86.7 0.1 copy.67
  86.8 0.7 reshape.62.idx_ref
  87.5 26.0 %collective-permute-done.1 = bf16[8,16,128,128]{3,2,1,0:T(8,128)(2,1)} collective-permute-done((bf16[8,16,128,128]{3,2,1,0:T(8,128)(2,1)}, bf16[8,16,128,128]{3,2,1,0:T(8,128)(2,1)}, u32[]{:S(2)}, u32[]{:S(2)}) %collective-permute-start.1) | collective-permute-done | bytes 4194336 | tf_op jit(solution)/shard_map/ppermute | solution.py:14
  113.5 5.2 %collective-permute-done = bf16[8,16,128,128]{3,2,1,0:T(8,128)(2,1)} collective-permute-done((bf16[8,16,128,128]{3,2,1,0:T(8,128)(2,1)}, bf16[8,16,128,128]{3,2,1,0:T(8,128)(2,1)}, u32[]{:S(2)}, u32[]{:S(2)}) %collective-permute-start) | collective-permute-done | bytes 4194336 | tf_op jit(solution)/shard_map/ppermute | solution.py:14
  118.7 58.7 %shard_map.37.rest_5_ = bf16[8,6,128,128]{3,2,1,0:T(8,128)(2,1)} custom-call(s32[768]{0:T(1024)} %reshape.62.idx_ref, s32[768]{0:T(1024)} %reshape.63.inner_ref, s32[48]{0:T(128)} %reshape.64.count_ref, bf16[8,16,128,128]{3,2,1,0:T(8,128)(2,1)} %all-gather.3.cloned.1.call-done.left_ref, bf16[128,128,128]{2,1,0:T(8,128)(2,1)} %bitcast.4.rest_0_.rest_1_, ...), custom_call_target="tpu_custom_call" | custom-call | flops 1610612736 | bytes 18356416 | tf_op jit(solution)/shard_map/pallas_call | solution.py:94
  177.5 0.1 collective-permute-start.3
  177.6 0.5 collective-permute-start.2
  178.1 0.1 reshape.98
  178.2 0.7 gather_fusion
  179.0 0.2 compare_reduce_fusion.1
  179.1 0.2 fusion
  179.3 0.2 convert_reduce_fusion.1
  179.5 0.6 reshape.61.count_ref
  180.2 0.1 copy.48
  180.3 3.4 %sort.34 = (s32[8,6,24]{1,2,0:T(8,128)}, s32[8,6,24]{1,2,0:T(8,128)S(1)}) sort(s32[8,6,24]{1,2,0:T(8,128)S(1)} %copy.48, s32[8,6,24]{1,2,0:T(8,128)S(1)} %iota.26), dimensions={2}, to_apply=%region_2.3 | sort | flops 12672 | bytes 18432 | tf_op jit(solution)/shard_map/jit(argsort)/sort | solution.py:28
  183.7 0.1 copy.49
  183.9 0.1 reshape.137
  184.0 7.2 %gather_fusion.3 = s32[1152]{0:T(1024)S(1)} fusion(s32[8,6,24]{2,1,0:T(8,128)S(1)} %iota.27, s32[1152]{0:T(1024)S(1)} %reshape.137), kind=kCustom, calls=%fused_computation.2.clone | custom fusion | bytes 23040 | tf_op jit(solution)/shard_map/jit(take_along_axis)/gather | solution.py:30
  191.1 7.2 %gather_fusion.2 = s32[1152]{0:T(1024)S(1)} fusion(s32[8,6,24]{2,1,0:T(8,128)S(1)} %get-tuple-element.20, s32[1152]{0:T(1024)S(1)} %reshape.137), kind=kCustom, calls=%fused_computation.clone | custom fusion | bytes 23040 | tf_op jit(solution)/shard_map/jit(take_along_axis)/gather | solution.py:29
  198.3 0.1 reshape.140
  198.4 0.1 reshape.145
  198.5 0.7 reshape.60.inner_ref
  199.2 0.7 reshape.59.idx_ref
  199.9 24.0 %collective-permute-done.3 = bf16[8,16,128,128]{3,2,1,0:T(8,128)(2,1)} collective-permute-done((bf16[8,16,128,128]{3,2,1,0:T(8,128)(2,1)}, bf16[8,16,128,128]{3,2,1,0:T(8,128)(2,1)}, u32[]{:S(2)}, u32[]{:S(2)}) %collective-permute-start.3) | collective-permute-done | bytes 4194336 | tf_op jit(solution)/shard_map/ppermute | solution.py:14
  223.9 5.3 %collective-permute-done.2 = bf16[8,16,128,128]{3,2,1,0:T(8,128)(2,1)} collective-permute-done((bf16[8,16,128,128]{3,2,1,0:T(8,128)(2,1)}, bf16[8,16,128,128]{3,2,1,0:T(8,128)(2,1)}, u32[]{:S(2)}, u32[]{:S(2)}) %collective-permute-start.2) | collective-permute-done | bytes 4194336 | tf_op jit(solution)/shard_map/ppermute | solution.py:14
  229.2 18.5 %all-gather.5.cloned.1.call-done.left_ref = bf16[8,24,128,128]{3,2,1,0:T(8,128)(2,1)} async-done(((bf16[8,6,128,128]{3,2,1,0:T(8,128)(2,1)}), bf16[8,24,128,128]{3,2,1,0:T(8,128)(2,1)}) %all-gather.5.cloned.1.call-update) | async-done | bytes 6291472 | tf_op jit(solution)/shard_map/all_gather | solution.py:140
  247.7 80.4 %shard_map.38 = bf16[8,6,128,128]{3,2,1,0:T(8,128)(2,1)} custom-call(s32[1152]{0:T(1024)} %reshape.59.idx_ref, s32[1152]{0:T(1024)} %reshape.60.inner_ref, s32[48]{0:T(128)} %reshape.61.count_ref, bf16[8,24,128,128]{3,2,1,0:T(8,128)(2,1)} %all-gather.5.cloned.1.call-done.left_ref, bf16[128,128,128]{2,1,0:T(8,128)(2,1)} %bitcast.7.rest_0_, ...), custom_call_target="tpu_custom_call" | custom-call | flops 2415919104 | bytes 30418112 | tf_op jit(solution)/shard_map/pallas_call | solution.py:94
  (28 shorter events, 0.5 us)
Async XLA Ops:
  6.5 55.7 %all-gather.3.cloned.1.call-start = ((), (), s32[]{:S(2)}) async-start(), calls=%async_computation | async-start | bytes 5242880 | tf_op jit(solution)/shard_map/all_gather | solution.py:118
  7.3 240.4 %all-gather.5.cloned.1.call-start = ((), (), s32[]{:S(2)}) async-start(), calls=%async_computation.1 | async-start | bytes 7864320 | tf_op jit(solution)/shard_map/all_gather | solution.py:140
  62.3 51.2 %collective-permute-start.1 = (bf16[8,16,128,128]{3,2,1,0:T(8,128)(2,1)}, bf16[8,16,128,128]{3,2,1,0:T(8,128)(2,1)}, u32[]{:S(2)}, u32[]{:S(2)}) collective-permute-start(bf16[8,16,128,128]{3,2,1,0:T(8,128)(2,1)} %all-gather.3.cloned.1.call-done.left_ref), channel_id=1, source_target_pairs={{0,252},{4,0},{8,4},{12,8},{16,12},{20,16},{24,20},{28,24},{32,28}... | collective-permute-start | bytes 12582920 | tf_op jit(solution)/shard_map/ppermute | solution.py:14
  67.2 51.6 %collective-permute-start = (bf16[8,16,128,128]{3,2,1,0:T(8,128)(2,1)}, bf16[8,16,128,128]{3,2,1,0:T(8,128)(2,1)}, u32[]{:S(2)}, u32[]{:S(2)}) collective-permute-start(bf16[8,16,128,128]{3,2,1,0:T(8,128)(2,1)} %all-gather.3.cloned.1.call-done.left_ref), channel_id=1, source_target_pairs={{0,4},{4,8},{8,12},{12,16},{16,20},{20,24},{24,28},{28,32},{32,36}... | collective-permute-start | bytes 12582920 | tf_op jit(solution)/shard_map/ppermute | solution.py:14
  118.7 59.4 %copy-start = (s32[8,24]{1,0:T(8,128)S(1)}, s32[8,24]{1,0:T(8,128)}, u32[]{:S(2)}) copy-start(s32[8,24]{1,0:T(8,128)} %param.9) | copy-start | bytes 2308
  177.5 46.4 %collective-permute-start.3 = (bf16[8,16,128,128]{3,2,1,0:T(8,128)(2,1)}, bf16[8,16,128,128]{3,2,1,0:T(8,128)(2,1)}, u32[]{:S(2)}, u32[]{:S(2)}) collective-permute-start(bf16[8,16,128,128]{3,2,1,0:T(8,128)(2,1)} %collective-permute-done.1), channel_id=1, source_target_pairs={{0,252},{4,0},{8,4},{12,8},{16,12},{20,16},{24,20},{28,24},{32,28}... | collective-permute-start | bytes 12582920 | tf_op jit(solution)/shard_map/ppermute | solution.py:14
  177.6 51.6 %collective-permute-start.2 = (bf16[8,16,128,128]{3,2,1,0:T(8,128)(2,1)}, bf16[8,16,128,128]{3,2,1,0:T(8,128)(2,1)}, u32[]{:S(2)}, u32[]{:S(2)}) collective-permute-start(bf16[8,16,128,128]{3,2,1,0:T(8,128)(2,1)} %collective-permute-done), channel_id=1, source_target_pairs={{0,4},{4,8},{8,12},{12,16},{16,20},{20,24},{24,28},{28,32},{32,36}... | collective-permute-start | bytes 12582920 | tf_op jit(solution)/shard_map/ppermute | solution.py:14
Sparse Core Ops, SparseCore 0:
  9.2 53.0 all-gather.2
  177.6 70.0 all-gather.4

commit v4 on v2

--- a/solution.py
+++ b/solution.py
@@ -96,6 +96,109 @@
     )(*operands)
 
 
+MESH = pl.DeviceIdType.MESH
+
+
+def square_kernel(n_out, n_inner, n_pieces, idx_ref, left_ref, *rest):
+    pieces = rest[:n_pieces]
+    out_ref, spread_ref, halo, lcat, rcat, sems, send_sems, recv_sems = rest[n_pieces:]
+    edge = left_ref.shape[-1]
+    span = pieces[0].shape[0]
+    row_at = lax.axis_index("row")
+    col_at = lax.axis_index("col")
+    depth_at = lax.axis_index("depth")
+    depth_count = lax.axis_size("depth")
+    peers = [lax.rem(depth_at + k, depth_count) for k in range(depth_count)]
+
+    barrier = pltpu.get_barrier_semaphore()
+    for k in range(1, depth_count):
+        pl.semaphore_signal(
+            barrier, inc=1, device_id=(row_at, col_at, peers[k]), device_id_type=MESH
+        )
+    pl.semaphore_wait(barrier, depth_count - 1)
+
+    copies = [
+        pltpu.make_async_copy(piece, halo.at[pl.ds(k * span, span)], sems.at[k])
+        for k, piece in enumerate(pieces)
+    ]
+    for copy in copies:
+        copy.start()
+    halo[n_pieces * span] = jnp.zeros((edge, edge), halo.dtype)
+    for copy in copies:
+        copy.wait()
+
+    def spread(row, k):
+        target = spread_ref.at[row, pl.ds(depth_at * n_out, n_out)]
+        if k == 0:
+            return pltpu.make_async_copy(out_ref.at[row], target, send_sems.at[row, 0])
+        return pltpu.make_async_remote_copy(
+            src_ref=out_ref.at[row],
+            dst_ref=target,
+            send_sem=send_sems.at[row, k],
+            recv_sem=recv_sems.at[row, k],
+            device_id=(row_at, col_at, peers[k]),
+            device_id_type=MESH,
+        )
+
+    def row_body(row, carry):
+        for inner in range(n_inner):
+            lcat[:, inner * edge:(inner + 1) * edge] = left_ref[row, inner]
+
+        def col_body(col, carry):
+            item = row * n_out + col
+            for inner in range(n_inner):
+                pick = idx_ref[item * n_inner + inner]
+                rcat[inner * edge:(inner + 1) * edge, :] = halo[pick]
+            acc = jnp.dot(lcat[...], rcat[...], preferred_element_type=jnp.float32)
+            out_ref[row, col] = acc.astype(out_ref.dtype)
+            return carry
+
+        carry = lax.fori_loop(0, n_out, col_body, carry)
+        for k in range(depth_count):
+            spread(row, k).start()
+        return carry
+
+    lax.fori_loop(0, left_ref.shape[0], row_body, 0)
+    for row in range(left_ref.shape[0]):
+        spread(row, 0).wait()
+        for k in range(1, depth_count):
+            spread(row, k).wait()
+
+
+def square_products(table, left, pieces, depth_count):
+    rows, n_inner, edge = left.shape[0], left.shape[1], left.shape[2]
+    n_out = table.shape[1]
+    flat_pieces = [piece.reshape(-1, edge, edge) for piece in pieces]
+    span = flat_pieces[0].shape[0]
+    operands = [table.reshape(-1), left] + flat_pieces
+    vmem = pl.BlockSpec(memory_space=pltpu.VMEM)
+    anywhere = pl.BlockSpec(memory_space=pl.ANY)
+    in_specs = [pl.BlockSpec(memory_space=pltpu.SMEM), vmem] + [anywhere] * len(pieces)
+    flops = 2 * rows * n_out * n_inner * edge ** 3
+    moved = sum(int(x.size) * x.dtype.itemsize for x in operands) + rows * n_out * edge * edge * 8
+    return pl.pallas_call(
+        functools.partial(square_kernel, n_out, n_inner, len(pieces)),
+        out_shape=(
+            jax.ShapeDtypeStruct((rows, n_out, edge, edge), jnp.bfloat16),
+            jax.ShapeDtypeStruct((rows, depth_count * n_out, edge, edge), jnp.bfloat16),
+        ),
+        in_specs=in_specs,
+        out_specs=(vmem, anywhere),
+        scratch_shapes=[
+            pltpu.VMEM((len(pieces) * span + 1, edge, edge), left.dtype),
+            pltpu.VMEM((edge, n_inner * edge), left.dtype),
+            pltpu.VMEM((n_inner * edge, edge), left.dtype),
+            pltpu.SemaphoreType.DMA((len(pieces),)),
+            pltpu.SemaphoreType.DMA((rows, depth_count)),
+            pltpu.SemaphoreType.DMA((rows, depth_count)),
+        ],
+        compiler_params=pltpu.CompilerParams(
+            vmem_limit_bytes=62 * 1024 * 1024, collective_id=0, has_side_effects=True
+        ),
+        cost_estimate=pl.CostEstimate(flops=flops, transcendentals=0, bytes_accessed=moved),
+    )(*operands)
+
+
 def local(blocks, block_cols, product_cols):
     row_count = blocks.shape[0]
     block_edge = blocks.shape[2]
@@ -126,9 +229,7 @@
         block_cols, own_cols, own_targets, (row_place - 1) * row_count, order_total,
         fill_count, len(halo_first) * row_count * fill_count,
     )
-    square = block_products(table_first, full_rows, halo_first)
-
-    square_rows = lax.all_gather(square, "depth", axis=1, tiled=True)
+    square, square_rows = square_products(table_first, full_rows, halo_first, depth_count)
     halo_second = halo_of(2)
     table_second = block_table(
         block_cols, product_cols, own_targets, (row_place - 2) * row_count, order_total,

time: 245 us -> 243 us (level)
  waiting for transfers between devices: 162 us -> 102 us
  Pallas kernels: 55.7 us -> 108 us
  starting transfers between devices: 5.5 us -> 10.1 us
    pallas_call x0 -> x1, Pallas kernels: none -> 76.6 us  [square_products(): pl.pallas_call(functools.partial(square_kernel, n_out, n_inner, len(piece...]
    ppermute x4, waiting for transfers between devices: 95.7 us -> 46.3 us  [shifted(): return lax.ppermute(value, axis, pairs)]
    pallas_call x2 -> x1, Pallas kernels: 55.7 us -> 31.6 us  [block_products(): pl.pallas_call(functools.partial(product_kernel, n_out, n_inner, len(piec...]
    all_gather x1 -> x0, waiting for transfers between devices: 10.4 us -> none  [local(): square_rows = lax.all_gather(square, 'depth', axis=1, tiled=True)]
    ppermute x4, starting transfers between devices: 5.46 us -> 10.1 us  [shifted(): return lax.ppermute(value, axis, pairs)]
  transfers between devices with their start and end apart: 6 -> 5, of which waited for: 6 -> 2; matrix products, arithmetic and copies ran while one was open for 3% -> 3% of each run, Pallas kernels for 0% -> 32%
where the time goes in v4:
time: 243 us; the launch traced here: 242 us
  Pallas kernels  108 us (44%)
  waiting for transfers between devices  102 us (42%)
  between operations  13.5 us (6%)
  starting transfers between devices  10.1 us (4%)
  local copies, waits for them, and re-layouts  4.58 us (2%)
  other arithmetic  3.04 us (1%)
    pallas_call x1, Pallas kernels, square_products(): pl.pallas_call(functools.partial(square_kernel, n_out, n_inner, len(piece...  76.6 us
    all_gather x1, waiting for transfers between devices, local(): full_rows = lax.all_gather(blocks, 'depth', axis=1, tiled=True)  55 us
    ppermute x4, waiting for transfers between devices, shifted(): return lax.ppermute(value, axis, pairs)  46.3 us
    pallas_call x1, Pallas kernels, block_products(): pl.pallas_call(functools.partial(product_kernel, n_out, n_inner, len(piec...  31.6 us
    ppermute x4, starting transfers between devices, shifted(): return lax.ppermute(value, axis, pairs)  10.1 us
  transfers between devices with their start and end apart: 5, of which 2 were waited for; matrix products, arithmetic and copies ran while one was open for 3% of the time, Pallas kernels for 32%

profile of v4, /device:TPU:8, one launch (start us, length us, event | category | flops | bytes accessed | tf_op | source)
XLA Modules:
  0.0 241.5 jit_solution(6824682443087368192)
XLA Ops:
  6.5 0.0 all-gather.2.cloned.1.call-start
  6.5 0.7 all-gather.2.cloned.1.call-update
  7.3 55.0 %all-gather.2.cloned.1.call-done.left_ref = bf16[8,16,128,128]{3,2,1,0:T(8,128)(2,1)} async-done(((bf16[8,4,128,128]{3,2,1,0:T(8,128)(2,1)}), bf16[8,16,128,128]{3,2,1,0:T(8,128)(2,1)}) %all-gather.2.cloned.1.call-update) | async-done | bytes 4194320 | tf_op jit(solution)/shard_map/all_gather | solution.py:212
  62.3 4.9 %collective-permute-start.1 = (bf16[8,16,128,128]{3,2,1,0:T(8,128)(2,1)}, bf16[8,16,128,128]{3,2,1,0:T(8,128)(2,1)}, u32[]{:S(2)}, u32[]{:S(2)}) collective-permute-start(bf16[8,16,128,128]{3,2,1,0:T(8,128)(2,1)} %all-gather.2.cloned.1.call-done.left_ref), channel_id=1, source_target_pairs={{0,252},{4,0},{8,4},{12,8},{16,12},{20,16},{24,20},{28,24},{32,28}... | collective-permute-start | bytes 12582920 | tf_op jit(solution)/shard_map/ppermute | solution.py:14
  67.2 0.0 collective-permute-start
  67.2 46.3 %collective-permute-done.1 = bf16[8,16,128,128]{3,2,1,0:T(8,128)(2,1)} collective-permute-done((bf16[8,16,128,128]{3,2,1,0:T(8,128)(2,1)}, bf16[8,16,128,128]{3,2,1,0:T(8,128)(2,1)}, u32[]{:S(2)}, u32[]{:S(2)}) %collective-permute-start.1) | collective-permute-done | bytes 4194336 | tf_op jit(solution)/shard_map/ppermute | solution.py:14
  113.5 5.2 %collective-permute-start.3 = (bf16[8,16,128,128]{3,2,1,0:T(8,128)(2,1)}, bf16[8,16,128,128]{3,2,1,0:T(8,128)(2,1)}, u32[]{:S(2)}, u32[]{:S(2)}) collective-permute-start(bf16[8,16,128,128]{3,2,1,0:T(8,128)(2,1)} %collective-permute-done.1), channel_id=1, source_target_pairs={{0,252},{4,0},{8,4},{12,8},{16,12},{20,16},{24,20},{28,24},{32,28}... | collective-permute-start | bytes 12582920 | tf_op jit(solution)/shard_map/ppermute | solution.py:14
  118.7 0.0 collective-permute-done
  118.7 0.0 collective-permute-start.2
  118.7 0.7 fusion.3
  119.4 0.1 reshape.52
  119.5 0.9 copy.17
  120.4 0.1 reshape.60
  120.5 0.6 gather_fusion.1
  121.2 0.7 gather_fusion
  121.9 0.1 copy.18
  121.9 0.8 constant_dynamic-slice_fusion
  122.7 0.2 compare_reduce_fusion.1
  122.9 0.2 fusion
  123.1 0.7 select_n.54.idx_ref
  123.8 1.0 compare_reduce_fusion
  124.7 1.0 fusion.1
  125.7 0.7 select_n.60.idx_ref
  126.4 76.6 %shard_map.37 = (bf16[8,6,128,128]{3,2,1,0:T(8,128)(2,1)}, bf16[8,24,128,128]{3,2,1,0:T(8,128)(2,1)}) custom-call(s32[768]{0:T(1024)} %select_n.60.idx_ref, bf16[8,16,128,128]{3,2,1,0:T(8,128)(2,1)} %all-gather.2.cloned.1.call-done.left_ref, bf16[128,128,128]{2,1,0:T(8,128)(2,1)} %bitcast.2.rest_0_.rest_1_, bf16[128,128,128]{2,1,0:T(8,128)(2,1)} %bitcast.7, ...), custom_call_target="tpu_custom_call" | custom-call | flops 3221225472 | bytes 23071744 | tf_op jit(solution)/shard_map/pallas_call | solution.py:179
  203.0 0.0 collective-permute-done.3
  203.1 0.0 collective-permute-done.2
  203.1 31.6 %shard_map.38 = bf16[8,6,128,128]{3,2,1,0:T(8,128)(2,1)} custom-call(s32[1152]{0:T(1024)} %select_n.54.idx_ref, bf16[8,24,128,128]{3,2,1,0:T(8,128)(2,1)} %get-tuple-element.7.left_ref, bf16[128,128,128]{2,1,0:T(8,128)(2,1)} %bitcast.5.rest_0_, bf16[128,128,128]{2,1,0:T(8,128)(2,1)} %bitcast.2.rest_0_.rest_1_, bf16[128,128,128]{2,1,0:T(8,128)(2,1)} %bitcast.8, ...), custom_call_target="tpu_custom_call" | custom-call | flops 4831838208 | bytes 30413312 | tf_op jit(solution)/shard_map/pallas_call | solution.py:83
  (5 shorter events, 0.1 us)
Async XLA Ops:
  6.5 55.7 %all-gather.2.cloned.1.call-start = ((), (), s32[]{:S(2)}) async-start(), calls=%async_computation | async-start | bytes 5242880 | tf_op jit(solution)/shard_map/all_gather | solution.py:212
  62.3 51.2 %collective-permute-start.1 = (bf16[8,16,128,128]{3,2,1,0:T(8,128)(2,1)}, bf16[8,16,128,128]{3,2,1,0:T(8,128)(2,1)}, u32[]{:S(2)}, u32[]{:S(2)}) collective-permute-start(bf16[8,16,128,128]{3,2,1,0:T(8,128)(2,1)} %all-gather.2.cloned.1.call-done.left_ref), channel_id=1, source_target_pairs={{0,252},{4,0},{8,4},{12,8},{16,12},{20,16},{24,20},{28,24},{32,28}... | collective-permute-start | bytes 12582920 | tf_op jit(solution)/shard_map/ppermute | solution.py:14
  67.2 51.6 %collective-permute-start = (bf16[8,16,128,128]{3,2,1,0:T(8,128)(2,1)}, bf16[8,16,128,128]{3,2,1,0:T(8,128)(2,1)}, u32[]{:S(2)}, u32[]{:S(2)}) collective-permute-start(bf16[8,16,128,128]{3,2,1,0:T(8,128)(2,1)} %all-gather.2.cloned.1.call-done.left_ref), channel_id=1, source_target_pairs={{0,4},{4,8},{8,12},{12,16},{16,20},{20,24},{24,28},{28,32},{32,36}... | collective-permute-start | bytes 12582920 | tf_op jit(solution)/shard_map/ppermute | solution.py:14
  113.5 89.6 %collective-permute-start.3 = (bf16[8,16,128,128]{3,2,1,0:T(8,128)(2,1)}, bf16[8,16,128,128]{3,2,1,0:T(8,128)(2,1)}, u32[]{:S(2)}, u32[]{:S(2)}) collective-permute-start(bf16[8,16,128,128]{3,2,1,0:T(8,128)(2,1)} %collective-permute-done.1), channel_id=1, source_target_pairs={{0,252},{4,0},{8,4},{12,8},{16,12},{20,16},{24,20},{28,24},{32,28}... | collective-permute-start | bytes 12582920 | tf_op jit(solution)/shard_map/ppermute | solution.py:14
  118.7 84.3 %collective-permute-start.2 = (bf16[8,16,128,128]{3,2,1,0:T(8,128)(2,1)}, bf16[8,16,128,128]{3,2,1,0:T(8,128)(2,1)}, u32[]{:S(2)}, u32[]{:S(2)}) collective-permute-start(bf16[8,16,128,128]{3,2,1,0:T(8,128)(2,1)} %collective-permute-done), channel_id=1, source_target_pairs={{0,4},{4,8},{8,12},{12,16},{16,20},{20,24},{24,28},{28,32},{32,36}... | collective-permute-start | bytes 12582920 | tf_op jit(solution)/shard_map/ppermute | solution.py:14
Sparse Core Ops, SparseCore 0:
  9.2 53.0 all-gather.1

commit v5 on v4

--- a/solution.py
+++ b/solution.py
@@ -99,23 +99,28 @@
 MESH = pl.DeviceIdType.MESH
 
 
-def square_kernel(n_out, n_inner, n_pieces, idx_ref, left_ref, *rest):
+def square_kernel(n_own, n_inner, n_pieces, idx_ref, left_ref, *rest):
     pieces = rest[:n_pieces]
-    out_ref, spread_ref, halo, lcat, rcat, sems, send_sems, recv_sems = rest[n_pieces:]
+    out_ref, spread_ref, halo, lcat, rcat, sems, send_sems, recv_sems, keep_sems = rest[
+        n_pieces:
+    ]
     edge = left_ref.shape[-1]
     span = pieces[0].shape[0]
+    row_count = left_ref.shape[0]
     row_at = lax.axis_index("row")
     col_at = lax.axis_index("col")
     depth_at = lax.axis_index("depth")
     depth_count = lax.axis_size("depth")
-    peers = [lax.rem(depth_at + k, depth_count) for k in range(depth_count)]
+    ahead = lax.rem(depth_at + 1, depth_count)
+    behind = lax.rem(depth_at + depth_count - 1, depth_count)
+    across = lax.rem(depth_at + 2, depth_count)
 
     barrier = pltpu.get_barrier_semaphore()
-    for k in range(1, depth_count):
+    for peer in (ahead, behind):
         pl.semaphore_signal(
-            barrier, inc=1, device_id=(row_at, col_at, peers[k]), device_id_type=MESH
+            barrier, inc=1, device_id=(row_at, col_at, peer), device_id_type=MESH
         )
-    pl.semaphore_wait(barrier, depth_count - 1)
+    pl.semaphore_wait(barrier, 2)
 
     copies = [
         pltpu.make_async_copy(piece, halo.at[pl.ds(k * span, span)], sems.at[k])
@@ -128,24 +133,32 @@
         copy.wait()
 
     def spread(row, k):
-        target = spread_ref.at[row, pl.ds(depth_at * n_out, n_out)]
+        source = out_ref.at[row, pl.ds(0, n_own)]
+        target = spread_ref.at[row, pl.ds(depth_at * n_own, n_own)]
         if k == 0:
-            return pltpu.make_async_copy(out_ref.at[row], target, send_sems.at[row, 0])
+            return pltpu.make_async_copy(source, target, send_sems.at[row, 0])
         return pltpu.make_async_remote_copy(
-            src_ref=out_ref.at[row],
+            src_ref=source,
             dst_ref=target,
             send_sem=send_sems.at[row, k],
             recv_sem=recv_sems.at[row, k],
-            device_id=(row_at, col_at, peers[k]),
+            device_id=(row_at, col_at, ahead if k == 1 else behind),
             device_id_type=MESH,
         )
 
-    def row_body(row, carry):
+    def keep(row):
+        return pltpu.make_async_copy(
+            out_ref.at[row, pl.ds(n_own, n_own)],
+            spread_ref.at[row, pl.ds(across * n_own, n_own)],
+            keep_sems.at[row],
+        )
+
+    def products(row, first):
         for inner in range(n_inner):
             lcat[:, inner * edge:(inner + 1) * edge] = left_ref[row, inner]
 
         def col_body(col, carry):
-            item = row * n_out + col
+            item = row * 2 * n_own + col
             for inner in range(n_inner):
                 pick = idx_ref[item * n_inner + inner]
                 rcat[inner * edge:(inner + 1) * edge, :] = halo[pick]
@@ -153,34 +166,43 @@
             out_ref[row, col] = acc.astype(out_ref.dtype)
             return carry
 
-        carry = lax.fori_loop(0, n_out, col_body, carry)
-        for k in range(depth_count):
+        lax.fori_loop(first, first + n_own, col_body, 0)
+
+    def own_body(row, carry):
+        products(row, 0)
+        for k in range(3):
             spread(row, k).start()
         return carry
 
-    lax.fori_loop(0, left_ref.shape[0], row_body, 0)
-    for row in range(left_ref.shape[0]):
-        spread(row, 0).wait()
-        for k in range(1, depth_count):
+    def across_body(row, carry):
+        products(row, n_own)
+        keep(row).start()
+        return carry
+
+    lax.fori_loop(0, row_count, own_body, 0)
+    lax.fori_loop(0, row_count, across_body, 0)
+    for row in range(row_count):
+        for k in range(3):
             spread(row, k).wait()
+        keep(row).wait()
 
 
 def square_products(table, left, pieces, depth_count):
     rows, n_inner, edge = left.shape[0], left.shape[1], left.shape[2]
-    n_out = table.shape[1]
+    n_own = table.shape[1] // 2
     flat_pieces = [piece.reshape(-1, edge, edge) for piece in pieces]
     span = flat_pieces[0].shape[0]
     operands = [table.reshape(-1), left] + flat_pieces
     vmem = pl.BlockSpec(memory_space=pltpu.VMEM)
     anywhere = pl.BlockSpec(memory_space=pl.ANY)
     in_specs = [pl.BlockSpec(memory_space=pltpu.SMEM), vmem] + [anywhere] * len(pieces)
-    flops = 2 * rows * n_out * n_inner * edge ** 3
-    moved = sum(int(x.size) * x.dtype.itemsize for x in operands) + rows * n_out * edge * edge * 8
+    flops = 2 * rows * 2 * n_own * n_inner * edge ** 3
+    moved = sum(int(x.size) * x.dtype.itemsize for x in operands) + rows * n_own * edge * edge * 10
     return pl.pallas_call(
-        functools.partial(square_kernel, n_out, n_inner, len(pieces)),
+        functools.partial(square_kernel, n_own, n_inner, len(pieces)),
         out_shape=(
-            jax.ShapeDtypeStruct((rows, n_out, edge, edge), jnp.bfloat16),
-            jax.ShapeDtypeStruct((rows, depth_count * n_out, edge, edge), jnp.bfloat16),
+            jax.ShapeDtypeStruct((rows, 2 * n_own, edge, edge), jnp.bfloat16),
+            jax.ShapeDtypeStruct((rows, depth_count * n_own, edge, edge), jnp.bfloat16),
         ),
         in_specs=in_specs,
         out_specs=(vmem, anywhere),
@@ -189,8 +211,9 @@
             pltpu.VMEM((edge, n_inner * edge), left.dtype),
             pltpu.VMEM((n_inner * edge, edge), left.dtype),
             pltpu.SemaphoreType.DMA((len(pieces),)),
-            pltpu.SemaphoreType.DMA((rows, depth_count)),
-            pltpu.SemaphoreType.DMA((rows, depth_count)),
+            pltpu.SemaphoreType.DMA((rows, 3)),
+            pltpu.SemaphoreType.DMA((rows, 3)),
+            pltpu.SemaphoreType.DMA((rows,)),
         ],
         compiler_params=pltpu.CompilerParams(
             vmem_limit_bytes=62 * 1024 * 1024, collective_id=0, has_side_effects=True
@@ -224,9 +247,12 @@
         product_cols, depth_index * target_share, target_share, 1
     )
 
+    across_targets = lax.dynamic_slice_in_dim(
+        product_cols, ((depth_index + 2) % depth_count) * target_share, target_share, 1
+    )
     halo_first = halo_of(1)
     table_first = block_table(
-        block_cols, own_cols, own_targets, (row_place - 1) * row_count, order_total,
+        block_cols, own_cols, jnp.concatenate([own_targets, across_targets], axis=1), (row_place - 1) * row_count, order_total,
         fill_count, len(halo_first) * row_count * fill_count,
     )
     square, square_rows = square_products(table_first, full_rows, halo_first, depth_count)

time: 243 us -> 211 us (0.87)
  Pallas kernels: 108 us -> 75.5 us
    pallas_call x1, Pallas kernels: 76.6 us -> 43.4 us  [square_products(): pl.pallas_call(functools.partial(square_kernel, n_own, n_inner, len(piece...]
  transfers between devices with their start and end apart: 5 -> 5, of which waited for: 2 -> 2; matrix products, arithmetic and copies ran while one was open for 3% -> 5% of each run, Pallas kernels for 32% -> 21%
where the time goes in v5:
time: 211 us
  waiting for transfers between devices  102 us (48%)
  Pallas kernels  75.5 us (36%)
  between operations  13.5 us (6%)
  starting transfers between devices  10.1 us (5%)
  other arithmetic  4.85 us (2%)
  local copies, waits for them, and re-layouts  4.66 us (2%)
    all_gather x1, waiting for transfers between devices, local(): full_rows = lax.all_gather(blocks, 'depth', axis=1, tiled=True)  55 us
    ppermute x4, waiting for transfers between devices, shifted(): return lax.ppermute(value, axis, pairs)  46.3 us
    pallas_call x1, Pallas kernels, square_products(): pl.pallas_call(functools.partial(square_kernel, n_own, n_inner, len(piece...  43.4 us
    pallas_call x1, Pallas kernels, block_products(): pl.pallas_call(functools.partial(product_kernel, n_out, n_inner, len(piec...  32.1 us
    ppermute x4, starting transfers between devices, shifted(): return lax.ppermute(value, axis, pairs)  10.1 us
  transfers between devices with their start and end apart: 5, of which 2 were waited for; matrix products, arithmetic and copies ran while one was open for 5% of the time, Pallas kernels for 21%

profile of v5, /device:TPU:8, one launch (start us, length us, event | category | flops | bytes accessed | tf_op | source)
XLA Modules:
  0.0 210.6 jit_solution(3480827028829340515)
XLA Ops:
  6.5 0.0 all-gather.2.cloned.1.call-start
  6.5 0.7 all-gather.2.cloned.1.call-update
  7.3 55.0 %all-gather.2.cloned.1.call-done.left_ref = bf16[8,16,128,128]{3,2,1,0:T(8,128)(2,1)} async-done(((bf16[8,4,128,128]{3,2,1,0:T(8,128)(2,1)}), bf16[8,16,128,128]{3,2,1,0:T(8,128)(2,1)}) %all-gather.2.cloned.1.call-update) | async-done | bytes 4194320 | tf_op jit(solution)/shard_map/all_gather | solution.py:235
  62.3 4.9 %collective-permute-start.1 = (bf16[8,16,128,128]{3,2,1,0:T(8,128)(2,1)}, bf16[8,16,128,128]{3,2,1,0:T(8,128)(2,1)}, u32[]{:S(2)}, u32[]{:S(2)}) collective-permute-start(bf16[8,16,128,128]{3,2,1,0:T(8,128)(2,1)} %all-gather.2.cloned.1.call-done.left_ref), channel_id=1, source_target_pairs={{0,252},{4,0},{8,4},{12,8},{16,12},{20,16},{24,20},{28,24},{32,28}... | collective-permute-start | bytes 12582920 | tf_op jit(solution)/shard_map/ppermute | solution.py:14
  67.2 0.0 collective-permute-start
  67.2 46.3 %collective-permute-done.1 = bf16[8,16,128,128]{3,2,1,0:T(8,128)(2,1)} collective-permute-done((bf16[8,16,128,128]{3,2,1,0:T(8,128)(2,1)}, bf16[8,16,128,128]{3,2,1,0:T(8,128)(2,1)}, u32[]{:S(2)}, u32[]{:S(2)}) %collective-permute-start.1) | collective-permute-done | bytes 4194336 | tf_op jit(solution)/shard_map/ppermute | solution.py:14
  113.5 5.2 %collective-permute-start.3 = (bf16[8,16,128,128]{3,2,1,0:T(8,128)(2,1)}, bf16[8,16,128,128]{3,2,1,0:T(8,128)(2,1)}, u32[]{:S(2)}, u32[]{:S(2)}) collective-permute-start(bf16[8,16,128,128]{3,2,1,0:T(8,128)(2,1)} %collective-permute-done.1), channel_id=1, source_target_pairs={{0,252},{4,0},{8,4},{12,8},{16,12},{20,16},{24,20},{28,24},{32,28}... | collective-permute-start | bytes 12582920 | tf_op jit(solution)/shard_map/ppermute | solution.py:14
  118.7 0.0 collective-permute-done
  118.7 0.0 collective-permute-start.2
  118.7 0.7 fusion.3
  119.4 0.1 reshape.53
  119.5 0.9 copy.17
  120.4 0.1 reshape.61
  120.5 0.6 gather_fusion.1
  121.2 0.7 gather_fusion
  121.9 0.1 copy.18
  121.9 0.8 constant_dynamic-slice_fusion
  122.8 0.2 compare_reduce_fusion.1
  123.0 0.2 fusion.1
  123.1 0.7 select_n.63.idx_ref
  123.8 0.1 pad_add_fusion
  123.9 1.8 compare_reduce_fusion
  125.7 1.8 fusion
  127.6 0.7 select_n.71.idx_ref
  128.3 43.4 %shard_map.37 = (bf16[8,12,128,128]{3,2,1,0:T(8,128)(2,1)}, bf16[8,24,128,128]{3,2,1,0:T(8,128)(2,1)}) custom-call(s32[1536]{0:T(1024)} %select_n.71.idx_ref, bf16[8,16,128,128]{3,2,1,0:T(8,128)(2,1)} %all-gather.2.cloned.1.call-done.left_ref, bf16[128,128,128]{2,1,0:T(8,128)(2,1)} %bitcast.2.rest_0_.rest_1_, bf16[128,128,128]{2,1,0:T(8,128)(2,1)} %bitcast.7, ...), custom_call_target="tpu_custom_call" | custom-call | flops 6442450944 | bytes 24647680 | tf_op jit(solution)/shard_map/pallas_call | solution.py:201
  171.7 0.0 collective-permute-done.3
  171.7 0.0 collective-permute-done.2
  171.7 32.1 %shard_map.38 = bf16[8,6,128,128]{3,2,1,0:T(8,128)(2,1)} custom-call(s32[1152]{0:T(1024)} %select_n.63.idx_ref, bf16[8,24,128,128]{3,2,1,0:T(8,128)(2,1)} %get-tuple-element.7.left_ref, bf16[128,128,128]{2,1,0:T(8,128)(2,1)} %bitcast.5.rest_0_, bf16[128,128,128]{2,1,0:T(8,128)(2,1)} %bitcast.2.rest_0_.rest_1_, bf16[128,128,128]{2,1,0:T(8,128)(2,1)} %bitcast.8, ...), custom_call_target="tpu_custom_call" | custom-call | flops 4831838208 | bytes 31986176 | tf_op jit(solution)/shard_map/pallas_call | solution.py:83
  (5 shorter events, 0.1 us)
Async XLA Ops:
  6.5 55.7 %all-gather.2.cloned.1.call-start = ((), (), s32[]{:S(2)}) async-start(), calls=%async_computation | async-start | bytes 5242880 | tf_op jit(solution)/shard_map/all_gather | solution.py:235
  62.3 51.2 %collective-permute-start.1 = (bf16[8,16,128,128]{3,2,1,0:T(8,128)(2,1)}, bf16[8,16,128,128]{3,2,1,0:T(8,128)(2,1)}, u32[]{:S(2)}, u32[]{:S(2)}) collective-permute-start(bf16[8,16,128,128]{3,2,1,0:T(8,128)(2,1)} %all-gather.2.cloned.1.call-done.left_ref), channel_id=1, source_target_pairs={{0,252},{4,0},{8,4},{12,8},{16,12},{20,16},{24,20},{28,24},{32,28}... | collective-permute-start | bytes 12582920 | tf_op jit(solution)/shard_map/ppermute | solution.py:14
  67.2 51.6 %collective-permute-start = (bf16[8,16,128,128]{3,2,1,0:T(8,128)(2,1)}, bf16[8,16,128,128]{3,2,1,0:T(8,128)(2,1)}, u32[]{:S(2)}, u32[]{:S(2)}) collective-permute-start(bf16[8,16,128,128]{3,2,1,0:T(8,128)(2,1)} %all-gather.2.cloned.1.call-done.left_ref), channel_id=1, source_target_pairs={{0,4},{4,8},{8,12},{12,16},{16,20},{20,24},{24,28},{28,32},{32,36}... | collective-permute-start | bytes 12582920 | tf_op jit(solution)/shard_map/ppermute | solution.py:14
  113.5 58.2 %collective-permute-start.3 = (bf16[8,16,128,128]{3,2,1,0:T(8,128)(2,1)}, bf16[8,16,128,128]{3,2,1,0:T(8,128)(2,1)}, u32[]{:S(2)}, u32[]{:S(2)}) collective-permute-start(bf16[8,16,128,128]{3,2,1,0:T(8,128)(2,1)} %collective-permute-done.1), channel_id=1, source_target_pairs={{0,252},{4,0},{8,4},{12,8},{16,12},{20,16},{24,20},{28,24},{32,28}... | collective-permute-start | bytes 12582920 | tf_op jit(solution)/shard_map/ppermute | solution.py:14
  118.7 53.0 %collective-permute-start.2 = (bf16[8,16,128,128]{3,2,1,0:T(8,128)(2,1)}, bf16[8,16,128,128]{3,2,1,0:T(8,128)(2,1)}, u32[]{:S(2)}, u32[]{:S(2)}) collective-permute-start(bf16[8,16,128,128]{3,2,1,0:T(8,128)(2,1)} %collective-permute-done), channel_id=1, source_target_pairs={{0,4},{4,8},{8,12},{12,16},{16,20},{20,24},{24,28},{28,32},{32,36}... | collective-permute-start | bytes 12582920 | tf_op jit(solution)/shard_map/ppermute | solution.py:14
Sparse Core Ops, SparseCore 0:
  9.2 53.0 all-gather.1

commit v6 on v5

--- a/solution.py
+++ b/solution.py
@@ -222,6 +222,93 @@
     )(*operands)
 
 
+def halo_kernel(blocks_ref, full_ref, left_ref, right_ref, send_sems, recv_sems, side_send, side_recv):
+    quarter = blocks_ref.shape[1]
+    row_at = lax.axis_index("row")
+    col_at = lax.axis_index("col")
+    depth_at = lax.axis_index("depth")
+    col_count = lax.axis_size("col")
+    depth_count = lax.axis_size("depth")
+    ring = lax.axis_size("row") * col_count
+    place = row_at * col_count + col_at
+    after = lax.rem(place + 1, ring)
+    before = lax.rem(place + ring - 1, ring)
+    after_id = (after // col_count, after % col_count, depth_at)
+    before_id = (before // col_count, before % col_count, depth_at)
+    peer_ids = [
+        (row_at, col_at, lax.rem(depth_at + k, depth_count)) for k in range(1, depth_count)
+    ]
+
+    barrier = pltpu.get_barrier_semaphore()
+    for device in peer_ids + [after_id, before_id]:
+        pl.semaphore_signal(barrier, inc=1, device_id=device, device_id_type=MESH)
+    pl.semaphore_wait(barrier, depth_count + 1)
+
+    own = pl.ds(depth_at * quarter, quarter)
+    local = pltpu.make_async_copy(blocks_ref, full_ref.at[:, own], send_sems.at[0])
+    local.start()
+
+    def to_peer(k):
+        return pltpu.make_async_remote_copy(
+            src_ref=blocks_ref,
+            dst_ref=full_ref.at[:, own],
+            send_sem=send_sems.at[k],
+            recv_sem=recv_sems.at[k],
+            device_id=peer_ids[k - 1],
+            device_id_type=MESH,
+        )
+
+    def to_side(k, source, way):
+        origin = lax.rem(depth_at + depth_count - k, depth_count)
+        slot = pl.ds(origin * quarter, quarter)
+        return pltpu.make_async_remote_copy(
+            src_ref=source,
+            dst_ref=(left_ref if way == 0 else right_ref).at[:, slot],
+            send_sem=side_send.at[way, k],
+            recv_sem=side_recv.at[way, k],
+            device_id=after_id if way == 0 else before_id,
+            device_id_type=MESH,
+        )
+
+    for way in range(2):
+        to_side(0, blocks_ref, way).start()
+    for k in range(1, depth_count):
+        to_peer(k).start()
+    for k in range(1, depth_count):
+        to_peer(k).wait_recv()
+        origin = lax.rem(depth_at + depth_count - k, depth_count)
+        arrived = full_ref.at[:, pl.ds(origin * quarter, quarter)]
+        for way in range(2):
+            to_side(k, arrived, way).start()
+    local.wait()
+    for k in range(1, depth_count):
+        to_peer(k).wait_send()
+    for k in range(depth_count):
+        for way in range(2):
+            to_side(k, blocks_ref, way).wait()
+
+
+def halo_exchange(blocks, depth_count):
+    rows, quarter, edge = blocks.shape[0], blocks.shape[1], blocks.shape[2]
+    whole = jax.ShapeDtypeStruct((rows, depth_count * quarter, edge, edge), blocks.dtype)
+    anywhere = pl.BlockSpec(memory_space=pl.ANY)
+    moved = int(blocks.size) * blocks.dtype.itemsize * (3 * depth_count + 3)
+    return pl.pallas_call(
+        halo_kernel,
+        out_shape=(whole, whole, whole),
+        in_specs=[anywhere],
+        out_specs=(anywhere, anywhere, anywhere),
+        scratch_shapes=[
+            pltpu.SemaphoreType.DMA((depth_count,)),
+            pltpu.SemaphoreType.DMA((depth_count,)),
+            pltpu.SemaphoreType.DMA((2, depth_count)),
+            pltpu.SemaphoreType.DMA((2, depth_count)),
+        ],
+        compiler_params=pltpu.CompilerParams(collective_id=1, has_side_effects=True),
+        cost_estimate=pl.CostEstimate(flops=0, transcendentals=0, bytes_accessed=moved),
+    )(blocks)
+
+
 def local(blocks, block_cols, product_cols):
     row_count = blocks.shape[0]
     block_edge = blocks.shape[2]
@@ -232,10 +319,8 @@
     depth_count = lax.axis_size("depth")
     target_share = product_cols.shape[1] // depth_count
 
-    full_rows = lax.all_gather(blocks, "depth", axis=1, tiled=True)
-    near = {0: full_rows}
-    near[1] = shifted(full_rows, ("row", "col"), 1)
-    near[-1] = shifted(full_rows, ("row", "col"), -1)
+    full_rows, from_before, from_after = halo_exchange(blocks, depth_count)
+    near = {0: full_rows, 1: from_before, -1: from_after}
     near[2] = shifted(near[1], ("row", "col"), 1)
     near[-2] = shifted(near[-1], ("row", "col"), -1)
 

time: 211 us -> 171 us (0.81)
  waiting for transfers between devices: 102 us -> 0.01 us
  Pallas kernels: 75.5 us -> 156 us
  between operations: 13.5 us -> 0.09 us
  starting transfers between devices: 10.1 us -> 5.14 us
    pallas_call x0 -> x1, Pallas kernels: none -> 69 us  [halo_exchange(): pl.pallas_call(halo_kernel, out_shape=(whole, whole, whole), in_specs=[an...]
    all_gather x1 -> x0, waiting for transfers between devices: 55 us -> none  [local(): full_rows = lax.all_gather(blocks, 'depth', axis=1, tiled=True)]
    ppermute x4 -> x2, waiting for transfers between devices: 46.3 us -> 0.01 us  [shifted(): return lax.ppermute(value, axis, pairs)]
    pallas_call x1, Pallas kernels: 43.4 us -> 54.9 us  [square_products(): pl.pallas_call(functools.partial(square_kernel, n_own, n_inner, len(piece...]
    ppermute x4 -> x2, starting transfers between devices: 10.1 us -> 5.14 us  [shifted(): return lax.ppermute(value, axis, pairs)]
  transfers between devices with their start and end apart: 5 -> 2, of which waited for: 2 -> 0; matrix products, arithmetic and copies ran while one was open for 5% -> 6% of each run, Pallas kernels for 21% -> 32%
where the time goes in v6:
time: 171 us
  Pallas kernels  156 us (91%)
  starting transfers between devices  5.14 us (3%)
  other arithmetic  4.84 us (3%)
  local copies, waits for them, and re-layouts  4.66 us (3%)
    pallas_call x1, Pallas kernels, halo_exchange(): pl.pallas_call(halo_kernel, out_shape=(whole, whole, whole), in_specs=[an...  69 us
    pallas_call x1, Pallas kernels, square_products(): pl.pallas_call(functools.partial(square_kernel, n_own, n_inner, len(piece...  54.9 us
    pallas_call x1, Pallas kernels, block_products(): pl.pallas_call(functools.partial(product_kernel, n_out, n_inner, len(piec...  32.1 us
    ppermute x2, starting transfers between devices, shifted(): return lax.ppermute(value, axis, pairs)  5.14 us
  transfers between devices with their start and end apart: 2, of which 0 were waited for; matrix products, arithmetic and copies ran while one was open for 6% of the time, Pallas kernels for 32%

profile of v6, /device:TPU:8, one launch (start us, length us, event | category | flops | bytes accessed | tf_op | source)
XLA Modules:
  0.0 170.7 jit_solution(1965675674020174081)
XLA Ops:
  0.0 69.0 %shard_map.37 = (bf16[8,16,128,128]{3,2,1,0:T(8,128)(2,1)}, bf16[8,16,128,128]{3,2,1,0:T(8,128)(2,1)}, bf16[8,16,128,128]{3,2,1,0:T(8,128)(2,1)}) custom-call(bf16[8,4,128,128]{3,2,1,0:T(8,128)(2,1)} %blocks_ref.1), custom_call_target="tpu_custom_call" | custom-call | bytes 15728640 | tf_op jit(solution)/shard_map/pallas_call | solution.py:296
  69.0 0.1 collective-permute-start
  69.1 5.1 %collective-permute-start.1 = (bf16[8,16,128,128]{3,2,1,0:T(8,128)(2,1)}, bf16[8,16,128,128]{3,2,1,0:T(8,128)(2,1)}, u32[]{:S(2)}, u32[]{:S(2)}) collective-permute-start(bf16[8,16,128,128]{3,2,1,0:T(8,128)(2,1)} %get-tuple-element.12), channel_id=1, source_target_pairs={{0,252},{4,0},{8,4},{12,8},{16,12},{20,16},{24,20},{28,24},{32,28}... | collective-permute-start | bytes 12582920 | tf_op jit(solution)/shard_map/ppermute | solution.py:14
  74.1 0.7 fusion.3
  74.8 0.1 reshape.53
  74.9 0.9 copy.17
  75.8 0.1 reshape.61
  75.9 0.6 gather_fusion.1
  76.6 0.7 gather_fusion
  77.2 0.1 copy.18
  77.3 0.8 constant_dynamic-slice_fusion
  78.2 0.2 compare_reduce_fusion.1
  78.4 0.2 fusion.1
  78.5 0.7 select_n.63.idx_ref
  79.2 0.1 pad_add_fusion
  79.3 1.8 %compare_reduce_fusion = pred[8,12,16]{2,1,0:T(8,128)(4,1)S(1)} fusion(s32[8,12]{1,0:T(8,128)S(1)} %pad_add_fusion, s32[8,16,16]{2,1,0:T(8,128)S(1)} %bitcast.13), kind=kLoop, calls=%fused_computation.3 | loop fusion | flops 47616 | bytes 10112 | tf_op jit(solution)/shard_map/reduce_or | solution.py:20
  81.1 1.8 %fusion = s32[8,12,16]{2,1,0:T(8,128)S(1)} fusion(s32[8,12]{1,0:T(8,128)S(1)} %pad_add_fusion, s32[8,16,16]{2,1,0:T(8,128)S(1)} %bitcast.14), kind=kLoop, calls=%fused_computation.4 | loop fusion | flops 72192 | bytes 14720 | tf_op jit(solution)/shard_map/reduce_sum | solution.py:22
  83.0 0.7 select_n.71.idx_ref
  83.7 54.9 %shard_map.38 = (bf16[8,12,128,128]{3,2,1,0:T(8,128)(2,1)}, bf16[8,24,128,128]{3,2,1,0:T(8,128)(2,1)}) custom-call(s32[1536]{0:T(1024)} %select_n.71.idx_ref, bf16[8,16,128,128]{3,2,1,0:T(8,128)(2,1)} %get-tuple-element.10.left_ref, bf16[128,128,128]{2,1,0:T(8,128)(2,1)} %bitcast.9, bf16[128,128,128]{2,1,0:T(8,128)(2,1)} %bitcast.7, ...), custom_call_target="tpu_custom_call" | custom-call | flops 6442450944 | bytes 24647680 | tf_op jit(solution)/shard_map/pallas_call | solution.py:201
  138.6 0.0 collective-permute-done
  138.6 0.0 collective-permute-done.1
  138.6 32.1 %shard_map.39 = bf16[8,6,128,128]{3,2,1,0:T(8,128)(2,1)} custom-call(s32[1152]{0:T(1024)} %select_n.63.idx_ref, bf16[8,24,128,128]{3,2,1,0:T(8,128)(2,1)} %get-tuple-element.13.left_ref, bf16[128,128,128]{2,1,0:T(8,128)(2,1)} %bitcast.5.rest_0_, bf16[128,128,128]{2,1,0:T(8,128)(2,1)} %bitcast.10, bf16[128,128,128]{2,1,0:T(8,128)(2,1)} %bitcast.8, ...), custom_call_target="tpu_custom_call" | custom-call | flops 4831838208 | bytes 31986176 | tf_op jit(solution)/shard_map/pallas_call | solution.py:83
  (5 shorter events, 0.1 us)
Async XLA Ops:
  69.0 69.6 %collective-permute-start = (bf16[8,16,128,128]{3,2,1,0:T(8,128)(2,1)}, bf16[8,16,128,128]{3,2,1,0:T(8,128)(2,1)}, u32[]{:S(2)}, u32[]{:S(2)}) collective-permute-start(bf16[8,16,128,128]{3,2,1,0:T(8,128)(2,1)} %get-tuple-element.11), channel_id=1, source_target_pairs={{0,4},{4,8},{8,12},{12,16},{16,20},{20,24},{24,28},{28,32},{32,36}... | collective-permute-start | bytes 12582920 | tf_op jit(solution)/shard_map/ppermute | solution.py:14
  69.1 69.5 %collective-permute-start.1 = (bf16[8,16,128,128]{3,2,1,0:T(8,128)(2,1)}, bf16[8,16,128,128]{3,2,1,0:T(8,128)(2,1)}, u32[]{:S(2)}, u32[]{:S(2)}) collective-permute-start(bf16[8,16,128,128]{3,2,1,0:T(8,128)(2,1)} %get-tuple-element.12), channel_id=1, source_target_pairs={{0,252},{4,0},{8,4},{12,8},{16,12},{20,16},{24,20},{28,24},{32,28}... | collective-permute-start | bytes 12582920 | tf_op jit(solution)/shard_map/ppermute | solution.py:14

commit v7 on v6

--- a/solution.py
+++ b/solution.py
@@ -49,20 +49,24 @@
         for inner in range(n_inner):
             lcat[:, inner * edge:(inner + 1) * edge] = left_ref[row, inner]
 
-        def col_body(col, carry):
-            item = row * n_out + col
-            for inner in range(n_inner):
-                pick = idx_ref[item * n_inner + inner]
-                rcat[inner * edge:(inner + 1) * edge, :] = halo[pick]
+        def col_body(pair, carry):
+            col = 2 * pair
+            for half in range(2):
+                item = row * n_out + col + half
+                for inner in range(n_inner):
+                    pick = idx_ref[item * n_inner + inner]
+                    rcat[inner * edge:(inner + 1) * edge, half * edge:(half + 1) * edge] = halo[pick]
             acc = jnp.dot(lcat[...], rcat[...], preferred_element_type=jnp.float32)
-            if final:
-                value = 3.0 * own_ref[row, col].astype(jnp.float32) - 2.0 * acc
-            else:
-                value = acc
-            out_ref[row, col] = value.astype(out_ref.dtype)
+            for half in range(2):
+                part = acc[:, half * edge:(half + 1) * edge]
+                if final:
+                    value = 3.0 * own_ref[row, col + half].astype(jnp.float32) - 2.0 * part
+                else:
+                    value = part
+                out_ref[row, col + half] = value.astype(out_ref.dtype)
             return carry
 
-        return lax.fori_loop(0, n_out, col_body, carry)
+        return lax.fori_loop(0, n_out // 2, col_body, carry)
 
     lax.fori_loop(0, left_ref.shape[0], row_body, 0)
 
@@ -88,7 +92,7 @@
         scratch_shapes=[
             pltpu.VMEM((len(pieces) * span + 1, edge, edge), left.dtype),
             pltpu.VMEM((edge, n_inner * edge), left.dtype),
-            pltpu.VMEM((n_inner * edge, edge), left.dtype),
+            pltpu.VMEM((n_inner * edge, 2 * edge), left.dtype),
             pltpu.SemaphoreType.DMA((len(pieces),)),
         ],
         compiler_params=pltpu.CompilerParams(vmem_limit_bytes=62 * 1024 * 1024),
@@ -157,16 +161,19 @@
         for inner in range(n_inner):
             lcat[:, inner * edge:(inner + 1) * edge] = left_ref[row, inner]
 
-        def col_body(col, carry):
-            item = row * 2 * n_own + col
-            for inner in range(n_inner):
-                pick = idx_ref[item * n_inner + inner]
-                rcat[inner * edge:(inner + 1) * edge, :] = halo[pick]
+        def col_body(pair, carry):
+            col = first + 2 * pair
+            for half in range(2):
+                item = row * 2 * n_own + col + half
+                for inner in range(n_inner):
+                    pick = idx_ref[item * n_inner + inner]
+                    rcat[inner * edge:(inner + 1) * edge, half * edge:(half + 1) * edge] = halo[pick]
             acc = jnp.dot(lcat[...], rcat[...], preferred_element_type=jnp.float32)
-            out_ref[row, col] = acc.astype(out_ref.dtype)
+            for half in range(2):
+                out_ref[row, col + half] = acc[:, half * edge:(half + 1) * edge].astype(out_ref.dtype)
             return carry
 
-        lax.fori_loop(first, first + n_own, col_body, 0)
+        lax.fori_loop(0, n_own // 2, col_body, 0)
 
     def own_body(row, carry):
         products(row, 0)
@@ -209,7 +216,7 @@
         scratch_shapes=[
             pltpu.VMEM((len(pieces) * span + 1, edge, edge), left.dtype),
             pltpu.VMEM((edge, n_inner * edge), left.dtype),
-            pltpu.VMEM((n_inner * edge, edge), left.dtype),
+            pltpu.VMEM((n_inner * edge, 2 * edge), left.dtype),
             pltpu.SemaphoreType.DMA((len(pieces),)),
             pltpu.SemaphoreType.DMA((rows, 3)),
             pltpu.SemaphoreType.DMA((rows, 3)),

time: 171 us -> 167 us (0.977)
  Pallas kernels: 156 us -> 151 us
    pallas_call x1, Pallas kernels: 32.1 us -> 28.5 us  [block_products(): pl.pallas_call(functools.partial(product_kernel, n_out, n_inner, len(piec...]
where the time goes in v7:
time: 167 us; the launch traced here: 166 us
  Pallas kernels  151 us (90%)
  starting transfers between devices  5.14 us (3%)
  other arithmetic  4.84 us (3%)
  local copies, waits for them, and re-layouts  4.66 us (3%)
    pallas_call x1, Pallas kernels, halo_exchange(): pl.pallas_call(halo_kernel, out_shape=(whole, whole, whole), in_specs=[an...  69 us
    pallas_call x1, Pallas kernels, square_products(): pl.pallas_call(functools.partial(square_kernel, n_own, n_inner, len(piece...  53.6 us
    pallas_call x1, Pallas kernels, block_products(): pl.pallas_call(functools.partial(product_kernel, n_out, n_inner, len(piec...  28.5 us
    ppermute x2, starting transfers between devices, shifted(): return lax.ppermute(value, axis, pairs)  5.14 us
  transfers between devices with their start and end apart: 2, of which 0 were waited for; matrix products, arithmetic and copies ran while one was open for 6% of the time, Pallas kernels for 32%

profile of v7, /device:TPU:8, one launch (start us, length us, event | category | flops | bytes accessed | tf_op | source)
XLA Modules:
  0.0 165.8 jit_solution(210066652208583663)
XLA Ops:
  0.0 69.0 %shard_map.37 = (bf16[8,16,128,128]{3,2,1,0:T(8,128)(2,1)}, bf16[8,16,128,128]{3,2,1,0:T(8,128)(2,1)}, bf16[8,16,128,128]{3,2,1,0:T(8,128)(2,1)}) custom-call(bf16[8,4,128,128]{3,2,1,0:T(8,128)(2,1)} %blocks_ref.1), custom_call_target="tpu_custom_call" | custom-call | bytes 15728640 | tf_op jit(solution)/shard_map/pallas_call | solution.py:303
  69.0 0.1 collective-permute-start
  69.1 5.1 %collective-permute-start.1 = (bf16[8,16,128,128]{3,2,1,0:T(8,128)(2,1)}, bf16[8,16,128,128]{3,2,1,0:T(8,128)(2,1)}, u32[]{:S(2)}, u32[]{:S(2)}) collective-permute-start(bf16[8,16,128,128]{3,2,1,0:T(8,128)(2,1)} %get-tuple-element.12), channel_id=1, source_target_pairs={{0,252},{4,0},{8,4},{12,8},{16,12},{20,16},{24,20},{28,24},{32,28}... | collective-permute-start | bytes 12582920 | tf_op jit(solution)/shard_map/ppermute | solution.py:14
  74.1 0.7 fusion.3
  74.8 0.1 reshape.53
  74.9 0.9 copy.17
  75.8 0.1 reshape.61
  75.9 0.6 gather_fusion.1
  76.6 0.7 gather_fusion
  77.2 0.1 copy.18
  77.3 0.8 constant_dynamic-slice_fusion
  78.2 0.2 compare_reduce_fusion.1
  78.4 0.2 fusion.1
  78.5 0.7 select_n.63.idx_ref
  79.2 0.1 pad_add_fusion
  79.3 1.8 %compare_reduce_fusion = pred[8,12,16]{2,1,0:T(8,128)(4,1)S(1)} fusion(s32[8,12]{1,0:T(8,128)S(1)} %pad_add_fusion, s32[8,16,16]{2,1,0:T(8,128)S(1)} %bitcast.13), kind=kLoop, calls=%fused_computation.3 | loop fusion | flops 47616 | bytes 10112 | tf_op jit(solution)/shard_map/reduce_or | solution.py:20
  81.1 1.8 %fusion = s32[8,12,16]{2,1,0:T(8,128)S(1)} fusion(s32[8,12]{1,0:T(8,128)S(1)} %pad_add_fusion, s32[8,16,16]{2,1,0:T(8,128)S(1)} %bitcast.14), kind=kLoop, calls=%fused_computation.4 | loop fusion | flops 72192 | bytes 14720 | tf_op jit(solution)/shard_map/reduce_sum | solution.py:22
  83.0 0.7 select_n.71.idx_ref
  83.7 53.6 %shard_map.38 = (bf16[8,12,128,128]{3,2,1,0:T(8,128)(2,1)}, bf16[8,24,128,128]{3,2,1,0:T(8,128)(2,1)}) custom-call(s32[1536]{0:T(1024)} %select_n.71.idx_ref, bf16[8,16,128,128]{3,2,1,0:T(8,128)(2,1)} %get-tuple-element.10.left_ref, bf16[128,128,128]{2,1,0:T(8,128)(2,1)} %bitcast.9, bf16[128,128,128]{2,1,0:T(8,128)(2,1)} %bitcast.7, ...), custom_call_target="tpu_custom_call" | custom-call | flops 6442450944 | bytes 24647680 | tf_op jit(solution)/shard_map/pallas_call | solution.py:208
  137.3 0.0 collective-permute-done
  137.3 0.0 collective-permute-done.1
  137.3 28.5 %shard_map.39 = bf16[8,6,128,128]{3,2,1,0:T(8,128)(2,1)} custom-call(s32[1152]{0:T(1024)} %select_n.63.idx_ref, bf16[8,24,128,128]{3,2,1,0:T(8,128)(2,1)} %get-tuple-element.13.left_ref, bf16[128,128,128]{2,1,0:T(8,128)(2,1)} %bitcast.5.rest_0_, bf16[128,128,128]{2,1,0:T(8,128)(2,1)} %bitcast.10, bf16[128,128,128]{2,1,0:T(8,128)(2,1)} %bitcast.8, ...), custom_call_target="tpu_custom_call" | custom-call | flops 4831838208 | bytes 31986176 | tf_op jit(solution)/shard_map/pallas_call | solution.py:87
  (5 shorter events, 0.1 us)
Async XLA Ops:
  69.0 68.3 %collective-permute-start = (bf16[8,16,128,128]{3,2,1,0:T(8,128)(2,1)}, bf16[8,16,128,128]{3,2,1,0:T(8,128)(2,1)}, u32[]{:S(2)}, u32[]{:S(2)}) collective-permute-start(bf16[8,16,128,128]{3,2,1,0:T(8,128)(2,1)} %get-tuple-element.11), channel_id=1, source_target_pairs={{0,4},{4,8},{8,12},{12,16},{16,20},{20,24},{24,28},{28,32},{32,36}... | collective-permute-start | bytes 12582920 | tf_op jit(solution)/shard_map/ppermute | solution.py:14
  69.1 68.2 %collective-permute-start.1 = (bf16[8,16,128,128]{3,2,1,0:T(8,128)(2,1)}, bf16[8,16,128,128]{3,2,1,0:T(8,128)(2,1)}, u32[]{:S(2)}, u32[]{:S(2)}) collective-permute-start(bf16[8,16,128,128]{3,2,1,0:T(8,128)(2,1)} %get-tuple-element.12), channel_id=1, source_target_pairs={{0,252},{4,0},{8,4},{12,8},{16,12},{20,16},{24,20},{28,24},{32,28}... | collective-permute-start | bytes 12582920 | tf_op jit(solution)/shard_map/ppermute | solution.py:14

commit v8 on v7

--- a/solution.py
+++ b/solution.py
@@ -105,9 +105,8 @@
 
 def square_kernel(n_own, n_inner, n_pieces, idx_ref, left_ref, *rest):
     pieces = rest[:n_pieces]
-    out_ref, spread_ref, halo, lcat, rcat, sems, send_sems, recv_sems, keep_sems = rest[
-        n_pieces:
-    ]
+    (out_ref, spread_ref, far_before, far_after, halo, lcat, rcat, sems, send_sems,
+     recv_sems, keep_sems, side_send, side_recv) = rest[n_pieces:]
     edge = left_ref.shape[-1]
     span = pieces[0].shape[0]
     row_count = left_ref.shape[0]
@@ -119,12 +118,31 @@
     behind = lax.rem(depth_at + depth_count - 1, depth_count)
     across = lax.rem(depth_at + 2, depth_count)
 
+    col_count = lax.axis_size("col")
+    ring = lax.axis_size("row") * col_count
+    place = row_at * col_count + col_at
+    after = lax.rem(place + 1, ring)
+    before = lax.rem(place + ring - 1, ring)
+    after_id = (after // col_count, after % col_count, depth_at)
+    before_id = (before // col_count, before % col_count, depth_at)
+
     barrier = pltpu.get_barrier_semaphore()
-    for peer in (ahead, behind):
-        pl.semaphore_signal(
-            barrier, inc=1, device_id=(row_at, col_at, peer), device_id_type=MESH
-        )
-    pl.semaphore_wait(barrier, 2)
+    for device in [(row_at, col_at, ahead), (row_at, col_at, behind), after_id, before_id]:
+        pl.semaphore_signal(barrier, inc=1, device_id=device, device_id_type=MESH)
+    pl.semaphore_wait(barrier, 4)
+
+    sides = [
+        pltpu.make_async_remote_copy(
+            src_ref=pieces[0], dst_ref=far_before, send_sem=side_send.at[0],
+            recv_sem=side_recv.at[0], device_id=after_id, device_id_type=MESH,
+        ),
+        pltpu.make_async_remote_copy(
+            src_ref=pieces[n_pieces - 1], dst_ref=far_after, send_sem=side_send.at[1],
+            recv_sem=side_recv.at[1], device_id=before_id, device_id_type=MESH,
+        ),
+    ]
+    for side in sides:
+        side.start()
 
     copies = [
         pltpu.make_async_copy(piece, halo.at[pl.ds(k * span, span)], sems.at[k])
@@ -192,6 +210,8 @@
         for k in range(3):
             spread(row, k).wait()
         keep(row).wait()
+    for side in sides:
+        side.wait()
 
 
 def square_products(table, left, pieces, depth_count):
@@ -210,9 +230,11 @@
         out_shape=(
             jax.ShapeDtypeStruct((rows, 2 * n_own, edge, edge), jnp.bfloat16),
             jax.ShapeDtypeStruct((rows, depth_count * n_own, edge, edge), jnp.bfloat16),
+            jax.ShapeDtypeStruct(flat_pieces[0].shape, left.dtype),
+            jax.ShapeDtypeStruct(flat_pieces[0].shape, left.dtype),
         ),
         in_specs=in_specs,
-        out_specs=(vmem, anywhere),
+        out_specs=(vmem, anywhere, anywhere, anywhere),
         scratch_shapes=[
             pltpu.VMEM((len(pieces) * span + 1, edge, edge), left.dtype),
             pltpu.VMEM((edge, n_inner * edge), left.dtype),
@@ -221,6 +243,8 @@
             pltpu.SemaphoreType.DMA((rows, 3)),
             pltpu.SemaphoreType.DMA((rows, 3)),
             pltpu.SemaphoreType.DMA((rows,)),
+            pltpu.SemaphoreType.DMA((2,)),
+            pltpu.SemaphoreType.DMA((2,)),
         ],
         compiler_params=pltpu.CompilerParams(
             vmem_limit_bytes=62 * 1024 * 1024, collective_id=0, has_side_effects=True
@@ -281,7 +305,7 @@
         to_side(0, blocks_ref, way).start()
     for k in range(1, depth_count):
         to_peer(k).start()
-    for k in range(1, depth_count):
+    for k in sorted(range(1, depth_count), key=lambda k: min(k, depth_count - k)):
         to_peer(k).wait_recv()
         origin = lax.rem(depth_at + depth_count - k, depth_count)
         arrived = full_ref.at[:, pl.ds(origin * quarter, quarter)]
@@ -328,8 +352,6 @@
 
     full_rows, from_before, from_after = halo_exchange(blocks, depth_count)
     near = {0: full_rows, 1: from_before, -1: from_after}
-    near[2] = shifted(near[1], ("row", "col"), 1)
-    near[-2] = shifted(near[-1], ("row", "col"), -1)
 
     def halo_of(reach):
         return [near[offset] for offset in range(reach, -reach - 1, -1)]
@@ -347,7 +369,9 @@
         block_cols, own_cols, jnp.concatenate([own_targets, across_targets], axis=1), (row_place - 1) * row_count, order_total,
         fill_count, len(halo_first) * row_count * fill_count,
     )
-    square, square_rows = square_products(table_first, full_rows, halo_first, depth_count)
+    square, square_rows, near[2], near[-2] = square_products(
+        table_first, full_rows, halo_first, depth_count
+    )
     halo_second = halo_of(2)
     table_second = block_table(
         block_cols, product_cols, own_targets, (row_place - 2) * row_count, order_total,

time: 167 us -> 176 us (1.054)
  Pallas kernels: 151 us -> 165 us
  starting transfers between devices: 5.14 us -> 0 us
    pallas_call x1, Pallas kernels: 69 us -> 79.9 us  [halo_exchange(): pl.pallas_call(halo_kernel, out_shape=(whole, whole, whole), in_specs=[an...]
    ppermute x2 -> x0, starting transfers between devices: 5.14 us -> none  [shifted(): return lax.ppermute(value, axis, pairs)]
    pallas_call x1, Pallas kernels: 53.6 us -> 56.3 us  [square_products(): pl.pallas_call(functools.partial(square_kernel, n_own, n_inner, len(piece...]
  transfers between devices with their start and end apart: 2 -> 0, of which waited for: 0 -> 0; matrix products, arithmetic and copies ran while one was open for 6% -> 0% of each run, Pallas kernels for 32% -> 0%
where the time goes in v8:
time: 176 us; the launch traced here: 174 us
  Pallas kernels  165 us (94%)
  other arithmetic  4.86 us (3%)
  local copies, waits for them, and re-layouts  4.64 us (3%)
    pallas_call x1, Pallas kernels, halo_exchange(): pl.pallas_call(halo_kernel, out_shape=(whole, whole, whole), in_specs=[an...  79.9 us
    pallas_call x1, Pallas kernels, square_products(): pl.pallas_call(functools.partial(square_kernel, n_own, n_inner, len(piece...  56.3 us
    pallas_call x1, Pallas kernels, block_products(): pl.pallas_call(functools.partial(product_kernel, n_out, n_inner, len(piec...  28.5 us

profile of v8, /device:TPU:8, one launch (start us, length us, event | category | flops | bytes accessed | tf_op | source)
XLA Modules:
  0.0 174.2 jit_solution(10737702510960155957)
XLA Ops:
  0.0 0.8 constant_dynamic-slice_fusion
  0.8 0.1 pad_add_fusion
  0.9 0.7 fusion.3
  1.6 0.1 reshape.45
  1.7 0.9 copy.17
  2.6 0.1 reshape.53
  2.7 0.6 gather_fusion.1
  3.3 0.7 gather_fusion
  4.0 0.1 copy.18
  4.1 0.2 compare_reduce_fusion.1
  4.3 0.2 fusion.1
  4.5 0.7 select_n.63.idx_ref
  5.2 1.8 %compare_reduce_fusion = pred[8,12,16]{2,1,0:T(8,128)(4,1)S(1)} fusion(s32[8,12]{1,0:T(8,128)S(1)} %pad_add_fusion, s32[8,16,16]{2,1,0:T(8,128)S(1)} %bitcast.11), kind=kLoop, calls=%fused_computation.3 | loop fusion | flops 47616 | bytes 10112 | tf_op jit(solution)/shard_map/reduce_or | solution.py:20
  7.0 1.8 %fusion = s32[8,12,16]{2,1,0:T(8,128)S(1)} fusion(s32[8,12]{1,0:T(8,128)S(1)} %pad_add_fusion, s32[8,16,16]{2,1,0:T(8,128)S(1)} %bitcast.12), kind=kLoop, calls=%fused_computation.4 | loop fusion | flops 72192 | bytes 14720 | tf_op jit(solution)/shard_map/reduce_sum | solution.py:22
  8.9 0.7 select_n.71.idx_ref
  9.5 79.9 %shard_map.37 = (bf16[8,16,128,128]{3,2,1,0:T(8,128)(2,1)}, bf16[8,16,128,128]{3,2,1,0:T(8,128)(2,1)}, bf16[8,16,128,128]{3,2,1,0:T(8,128)(2,1)}) custom-call(bf16[8,4,128,128]{3,2,1,0:T(8,128)(2,1)} %blocks_ref.1), custom_call_target="tpu_custom_call" | custom-call | bytes 15728640 | tf_op jit(solution)/shard_map/pallas_call | solution.py:327
  89.5 56.3 %shard_map.38 = (bf16[8,12,128,128]{3,2,1,0:T(8,128)(2,1)}, bf16[8,24,128,128]{3,2,1,0:T(8,128)(2,1)}, bf16[128,128,128]{2,1,0:T(8,128)(2,1)}, bf16[128,128,128]{2,1,0:T(8,128)(2,1)}) custom-call(s32[1536]{0:T(1024)} %select_n.71.idx_ref, bf16[8,16,128,128]{3,2,1,0:T(8,128)(2,1)} %get-tuple-element.12.left_ref, bf16[128,128,128]{2,1,0:T(8,128)(2,1)} %bitcast.7, ...), custom_call_target="tpu_custom_call" | custom-call | flops 6442450944 | bytes 24647680 | tf_op jit(solution)/shard_map/pallas_call | solution.py:228
  145.7 28.5 %shard_map.39 = bf16[8,6,128,128]{3,2,1,0:T(8,128)(2,1)} custom-call(s32[1152]{0:T(1024)} %select_n.63.idx_ref, bf16[8,24,128,128]{3,2,1,0:T(8,128)(2,1)} %get-tuple-element.15.left_ref, bf16[128,128,128]{2,1,0:T(8,128)(2,1)} %get-tuple-element.16.rest_0_, bf16[128,128,128]{2,1,0:T(8,128)(2,1)} %bitcast.8, bf16[128,128,128]{2,1,0:T(8,128)(2,1)} %bitcast.6, ...), custom_call_target="tpu_custom_call" | custom-call | flops 4831838208 | bytes 31986176 | tf_op jit(solution)/shard_map/pallas_call | solution.py:87
  (5 shorter events, 0.1 us)

commit v9 on v7

--- a/solution.py
+++ b/solution.py
@@ -252,47 +252,52 @@
     pl.semaphore_wait(barrier, depth_count + 1)
 
     own = pl.ds(depth_at * quarter, quarter)
-    local = pltpu.make_async_copy(blocks_ref, full_ref.at[:, own], send_sems.at[0])
+    rows = blocks_ref.shape[0]
+    local = pltpu.make_async_copy(blocks_ref, full_ref.at[:, own], side_send.at[2, 0, 0])
     local.start()
 
-    def to_peer(k):
+    def to_peer(k, row):
         return pltpu.make_async_remote_copy(
-            src_ref=blocks_ref,
-            dst_ref=full_ref.at[:, own],
-            send_sem=send_sems.at[k],
-            recv_sem=recv_sems.at[k],
+            src_ref=blocks_ref.at[row],
+            dst_ref=full_ref.at[row, own],
+            send_sem=send_sems.at[k, row],
+            recv_sem=recv_sems.at[k, row],
             device_id=peer_ids[k - 1],
             device_id_type=MESH,
         )
 
-    def to_side(k, source, way):
+    def to_side(k, row, way):
         origin = lax.rem(depth_at + depth_count - k, depth_count)
         slot = pl.ds(origin * quarter, quarter)
+        source = blocks_ref.at[row] if k == 0 else full_ref.at[row, slot]
         return pltpu.make_async_remote_copy(
             src_ref=source,
-            dst_ref=(left_ref if way == 0 else right_ref).at[:, slot],
-            send_sem=side_send.at[way, k],
-            recv_sem=side_recv.at[way, k],
+            dst_ref=(left_ref if way == 0 else right_ref).at[row, slot],
+            send_sem=side_send.at[way, k, row],
+            recv_sem=side_recv.at[way, k, row],
             device_id=after_id if way == 0 else before_id,
             device_id_type=MESH,
         )
 
-    for way in range(2):
-        to_side(0, blocks_ref, way).start()
     for k in range(1, depth_count):
-        to_peer(k).start()
-    for k in range(1, depth_count):
-        to_peer(k).wait_recv()
-        origin = lax.rem(depth_at + depth_count - k, depth_count)
-        arrived = full_ref.at[:, pl.ds(origin * quarter, quarter)]
+        for row in range(rows):
+            to_peer(k, row).start()
+    for row in range(rows):
         for way in range(2):
-            to_side(k, arrived, way).start()
+            to_side(0, row, way).start()
+    for k in sorted(range(1, depth_count), key=lambda k: min(k, depth_count - k)):
+        for row in range(rows):
+            to_peer(k, row).wait_recv()
+            for way in range(2):
+                to_side(k, row, way).start()
     local.wait()
     for k in range(1, depth_count):
-        to_peer(k).wait_send()
+        for row in range(rows):
+            to_peer(k, row).wait_send()
     for k in range(depth_count):
-        for way in range(2):
-            to_side(k, blocks_ref, way).wait()
+        for row in range(rows):
+            for way in range(2):
+                to_side(k, row, way).wait()
 
 
 def halo_exchange(blocks, depth_count):
@@ -306,10 +311,10 @@
         in_specs=[anywhere],
         out_specs=(anywhere, anywhere, anywhere),
         scratch_shapes=[
-            pltpu.SemaphoreType.DMA((depth_count,)),
-            pltpu.SemaphoreType.DMA((depth_count,)),
-            pltpu.SemaphoreType.DMA((2, depth_count)),
-            pltpu.SemaphoreType.DMA((2, depth_count)),
+            pltpu.SemaphoreType.DMA((depth_count, rows)),
+            pltpu.SemaphoreType.DMA((depth_count, rows)),
+            pltpu.SemaphoreType.DMA((3, depth_count, rows)),
+            pltpu.SemaphoreType.DMA((2, depth_count, rows)),
         ],
         compiler_params=pltpu.CompilerParams(collective_id=1, has_side_effects=True),
         cost_estimate=pl.CostEstimate(flops=0, transcendentals=0, bytes_accessed=moved),

time: 167 us -> 161 us (0.964)
  Pallas kernels: 151 us -> 146 us
    pallas_call x1, Pallas kernels: 53.6 us -> 45.2 us  [square_products(): pl.pallas_call(functools.partial(square_kernel, n_own, n_inner, len(piece...]
    pallas_call x1, Pallas kernels: 69 us -> 71.9 us  [halo_exchange(): pl.pallas_call(halo_kernel, out_shape=(whole, whole, whole), in_specs=[an...]
  transfers between devices with their start and end apart: 2 -> 2, of which waited for: 0 -> 0; matrix products, arithmetic and copies ran while one was open for 6% -> 6% of each run, Pallas kernels for 32% -> 28%
where the time goes in v9:
time: 161 us; the launch traced here: 160 us
  Pallas kernels  146 us (91%)
  starting transfers between devices  5.14 us (3%)
  other arithmetic  4.84 us (3%)
  local copies, waits for them, and re-layouts  4.66 us (3%)
    pallas_call x1, Pallas kernels, halo_exchange(): pl.pallas_call(halo_kernel, out_shape=(whole, whole, whole), in_specs=[an...  71.9 us
    pallas_call x1, Pallas kernels, square_products(): pl.pallas_call(functools.partial(square_kernel, n_own, n_inner, len(piece...  45.2 us
    pallas_call x1, Pallas kernels, block_products(): pl.pallas_call(functools.partial(product_kernel, n_out, n_inner, len(piec...  28.5 us
    ppermute x2, starting transfers between devices, shifted(): return lax.ppermute(value, axis, pairs)  5.14 us
  transfers between devices with their start and end apart: 2, of which 0 were waited for; matrix products, arithmetic and copies ran while one was open for 6% of the time, Pallas kernels for 28%

profile of v9, /device:TPU:8, one launch (start us, length us, event | category | flops | bytes accessed | tf_op | source)
XLA Modules:
  0.0 160.3 jit_solution(6310255262678358043)
XLA Ops:
  0.0 71.9 %shard_map.37 = (bf16[8,16,128,128]{3,2,1,0:T(8,128)(2,1)}, bf16[8,16,128,128]{3,2,1,0:T(8,128)(2,1)}, bf16[8,16,128,128]{3,2,1,0:T(8,128)(2,1)}) custom-call(bf16[8,4,128,128]{3,2,1,0:T(8,128)(2,1)} %blocks_ref.1), custom_call_target="tpu_custom_call" | custom-call | bytes 15728640 | tf_op jit(solution)/shard_map/pallas_call | solution.py:308
  71.9 0.1 collective-permute-start
  72.0 5.1 %collective-permute-start.1 = (bf16[8,16,128,128]{3,2,1,0:T(8,128)(2,1)}, bf16[8,16,128,128]{3,2,1,0:T(8,128)(2,1)}, u32[]{:S(2)}, u32[]{:S(2)}) collective-permute-start(bf16[8,16,128,128]{3,2,1,0:T(8,128)(2,1)} %get-tuple-element.12), channel_id=1, source_target_pairs={{0,252},{4,0},{8,4},{12,8},{16,12},{20,16},{24,20},{28,24},{32,28}... | collective-permute-start | bytes 12582920 | tf_op jit(solution)/shard_map/ppermute | solution.py:14
  77.0 0.7 fusion.3
  77.7 0.1 reshape.53
  77.8 0.9 copy.17
  78.7 0.1 reshape.61
  78.8 0.6 gather_fusion.1
  79.5 0.7 gather_fusion
  80.2 0.1 copy.18
  80.2 0.8 constant_dynamic-slice_fusion
  81.1 0.2 compare_reduce_fusion.1
  81.3 0.2 fusion.1
  81.4 0.7 select_n.63.idx_ref
  82.1 0.1 pad_add_fusion
  82.2 1.8 %compare_reduce_fusion = pred[8,12,16]{2,1,0:T(8,128)(4,1)S(1)} fusion(s32[8,12]{1,0:T(8,128)S(1)} %pad_add_fusion, s32[8,16,16]{2,1,0:T(8,128)S(1)} %bitcast.13), kind=kLoop, calls=%fused_computation.3 | loop fusion | flops 47616 | bytes 10112 | tf_op jit(solution)/shard_map/reduce_or | solution.py:20
  84.0 1.8 %fusion = s32[8,12,16]{2,1,0:T(8,128)S(1)} fusion(s32[8,12]{1,0:T(8,128)S(1)} %pad_add_fusion, s32[8,16,16]{2,1,0:T(8,128)S(1)} %bitcast.14), kind=kLoop, calls=%fused_computation.4 | loop fusion | flops 72192 | bytes 14720 | tf_op jit(solution)/shard_map/reduce_sum | solution.py:22
  85.9 0.7 select_n.71.idx_ref
  86.6 45.2 %shard_map.38 = (bf16[8,12,128,128]{3,2,1,0:T(8,128)(2,1)}, bf16[8,24,128,128]{3,2,1,0:T(8,128)(2,1)}) custom-call(s32[1536]{0:T(1024)} %select_n.71.idx_ref, bf16[8,16,128,128]{3,2,1,0:T(8,128)(2,1)} %get-tuple-element.10.left_ref, bf16[128,128,128]{2,1,0:T(8,128)(2,1)} %bitcast.9, bf16[128,128,128]{2,1,0:T(8,128)(2,1)} %bitcast.7, ...), custom_call_target="tpu_custom_call" | custom-call | flops 6442450944 | bytes 24647680 | tf_op jit(solution)/shard_map/pallas_call | solution.py:208
  131.8 0.0 collective-permute-done
  131.8 0.0 collective-permute-done.1
  131.8 28.5 %shard_map.39 = bf16[8,6,128,128]{3,2,1,0:T(8,128)(2,1)} custom-call(s32[1152]{0:T(1024)} %select_n.63.idx_ref, bf16[8,24,128,128]{3,2,1,0:T(8,128)(2,1)} %get-tuple-element.13.left_ref, bf16[128,128,128]{2,1,0:T(8,128)(2,1)} %bitcast.5.rest_0_, bf16[128,128,128]{2,1,0:T(8,128)(2,1)} %bitcast.10, bf16[128,128,128]{2,1,0:T(8,128)(2,1)} %bitcast.8, ...), custom_call_target="tpu_custom_call" | custom-call | flops 4831838208 | bytes 31986176 | tf_op jit(solution)/shard_map/pallas_call | solution.py:87
  (5 shorter events, 0.1 us)
Async XLA Ops:
  71.9 59.9 %collective-permute-start = (bf16[8,16,128,128]{3,2,1,0:T(8,128)(2,1)}, bf16[8,16,128,128]{3,2,1,0:T(8,128)(2,1)}, u32[]{:S(2)}, u32[]{:S(2)}) collective-permute-start(bf16[8,16,128,128]{3,2,1,0:T(8,128)(2,1)} %get-tuple-element.11), channel_id=1, source_target_pairs={{0,4},{4,8},{8,12},{12,16},{16,20},{20,24},{24,28},{28,32},{32,36}... | collective-permute-start | bytes 12582920 | tf_op jit(solution)/shard_map/ppermute | solution.py:14
  72.0 59.8 %collective-permute-start.1 = (bf16[8,16,128,128]{3,2,1,0:T(8,128)(2,1)}, bf16[8,16,128,128]{3,2,1,0:T(8,128)(2,1)}, u32[]{:S(2)}, u32[]{:S(2)}) collective-permute-start(bf16[8,16,128,128]{3,2,1,0:T(8,128)(2,1)} %get-tuple-element.12), channel_id=1, source_target_pairs={{0,252},{4,0},{8,4},{12,8},{16,12},{20,16},{24,20},{28,24},{32,28}... | collective-permute-start | bytes 12582920 | tf_op jit(solution)/shard_map/ppermute | solution.py:14

commit v10 on v9

--- a/solution.py
+++ b/solution.py
@@ -16,17 +16,23 @@
 
 def block_table(block_cols, rows, targets, start_row, order_total, fill_count, miss):
     cols_of = block_cols[rows]
-    matches = cols_of[:, None, :, :] == targets[:, :, None, None]
+    matches = cols_of[:, :, None, :] == targets[:, None, :, None]
     has_match = jnp.any(matches, axis=3)
     slot_ids = jnp.arange(fill_count, dtype=jnp.int32)[None, None, None, :]
     position = jnp.sum(jnp.where(matches, slot_ids, 0), axis=3)
     local_rows = (rows - start_row) % order_total
-    flat = local_rows[:, None, :] * fill_count + position
+    flat = local_rows[:, :, None] * fill_count + position
     flat = jnp.clip(flat, 0, miss)
     return jnp.where(has_match, flat, miss).astype(jnp.int32)
 
 
-def product_kernel(n_out, n_inner, n_pieces, final, idx_ref, left_ref, *rest):
+def table_pick(idx_ref, view, row, inner, col):
+    row_stride, first, inner_stride, shift, cap = view
+    entry = idx_ref[row * row_stride + (first + inner) * inner_stride + col]
+    return jnp.minimum(jnp.maximum(entry - shift, 0), cap)
+
+
+def product_kernel(n_out, n_inner, n_pieces, final, view, idx_ref, left_ref, *rest):
     pieces = rest[:n_pieces]
     rest = rest[n_pieces:]
     if final:
@@ -52,9 +58,8 @@
         def col_body(pair, carry):
             col = 2 * pair
             for half in range(2):
-                item = row * n_out + col + half
                 for inner in range(n_inner):
-                    pick = idx_ref[item * n_inner + inner]
+                    pick = table_pick(idx_ref, view, row, inner, col + half)
                     rcat[inner * edge:(inner + 1) * edge, half * edge:(half + 1) * edge] = halo[pick]
             acc = jnp.dot(lcat[...], rcat[...], preferred_element_type=jnp.float32)
             for half in range(2):
@@ -71,9 +76,8 @@
     lax.fori_loop(0, left_ref.shape[0], row_body, 0)
 
 
-def block_products(table, left, pieces, own=None):
+def block_products(table, left, pieces, n_out, view, own=None):
     rows, n_inner, edge = left.shape[0], left.shape[1], left.shape[2]
-    n_out = table.shape[1]
     final = own is not None
     flat_pieces = [piece.reshape(-1, edge, edge) for piece in pieces]
     span = flat_pieces[0].shape[0]
@@ -85,7 +89,7 @@
     flops = 2 * rows * n_out * n_inner * edge ** 3
     moved = sum(int(x.size) * x.dtype.itemsize for x in operands) + rows * n_out * edge * edge * 2
     return pl.pallas_call(
-        functools.partial(product_kernel, n_out, n_inner, len(pieces), final),
+        functools.partial(product_kernel, n_out, n_inner, len(pieces), final, view),
         out_shape=jax.ShapeDtypeStruct((rows, n_out, edge, edge), jnp.bfloat16),
         in_specs=in_specs,
         out_specs=vmem,
@@ -103,7 +107,7 @@
 MESH = pl.DeviceIdType.MESH
 
 
-def square_kernel(n_own, n_inner, n_pieces, idx_ref, left_ref, *rest):
+def square_kernel(n_own, n_inner, n_pieces, view, idx_ref, left_ref, *rest):
     pieces = rest[:n_pieces]
     out_ref, spread_ref, halo, lcat, rcat, sems, send_sems, recv_sems, keep_sems = rest[
         n_pieces:
@@ -164,9 +168,8 @@
         def col_body(pair, carry):
             col = first + 2 * pair
             for half in range(2):
-                item = row * 2 * n_own + col + half
                 for inner in range(n_inner):
-                    pick = idx_ref[item * n_inner + inner]
+                    pick = table_pick(idx_ref, view, row, inner, col + half)
                     rcat[inner * edge:(inner + 1) * edge, half * edge:(half + 1) * edge] = halo[pick]
             acc = jnp.dot(lcat[...], rcat[...], preferred_element_type=jnp.float32)
             for half in range(2):
@@ -194,9 +197,8 @@
         keep(row).wait()
 
 
-def square_products(table, left, pieces, depth_count):
+def square_products(table, left, pieces, depth_count, n_own, view):
     rows, n_inner, edge = left.shape[0], left.shape[1], left.shape[2]
-    n_own = table.shape[1] // 2
     flat_pieces = [piece.reshape(-1, edge, edge) for piece in pieces]
     span = flat_pieces[0].shape[0]
     operands = [table.reshape(-1), left] + flat_pieces
@@ -206,7 +208,7 @@
     flops = 2 * rows * 2 * n_own * n_inner * edge ** 3
     moved = sum(int(x.size) * x.dtype.itemsize for x in operands) + rows * n_own * edge * edge * 10
     return pl.pallas_call(
-        functools.partial(square_kernel, n_own, n_inner, len(pieces)),
+        functools.partial(square_kernel, n_own, n_inner, len(pieces), view),
         out_shape=(
             jax.ShapeDtypeStruct((rows, 2 * n_own, edge, edge), jnp.bfloat16),
             jax.ShapeDtypeStruct((rows, depth_count * n_own, edge, edge), jnp.bfloat16),
@@ -348,17 +350,23 @@
         product_cols, ((depth_index + 2) % depth_count) * target_share, target_share, 1
     )
     halo_first = halo_of(1)
-    table_first = block_table(
-        block_cols, own_cols, jnp.concatenate([own_targets, across_targets], axis=1), (row_place - 1) * row_count, order_total,
-        fill_count, len(halo_first) * row_count * fill_count,
-    )
-    square, square_rows = square_products(table_first, full_rows, halo_first, depth_count)
     halo_second = halo_of(2)
-    table_second = block_table(
-        block_cols, product_cols, own_targets, (row_place - 2) * row_count, order_total,
-        fill_count, len(halo_second) * row_count * fill_count,
-    )
-    return block_products(table_second, square_rows, halo_second, own=square)
+    piece_blocks = row_count * fill_count
+    inner_rows = jnp.concatenate([own_cols, product_cols], axis=1)
+    targets = jnp.concatenate([own_targets, across_targets], axis=1)
+    table = block_table(
+        block_cols, inner_rows, targets, (row_place - 2) * row_count, order_total,
+        fill_count, len(halo_second) * piece_blocks,
+    )
+    row_stride = inner_rows.shape[1] * targets.shape[1]
+    first_view = (row_stride, 0, targets.shape[1], piece_blocks, len(halo_first) * piece_blocks)
+    second_view = (row_stride, fill_count, targets.shape[1], 0, len(halo_second) * piece_blocks)
+    square, square_rows = square_products(
+        table, full_rows, halo_first, depth_count, target_share, first_view
+    )
+    return block_products(
+        table, square_rows, halo_second, target_share, second_view, own=square
+    )
 
 
 def solution(mesh):

time: 161 us -> 157 us (0.975)
  other arithmetic: 4.84 us -> 2.16 us
    reduce_or x2 -> x1, other arithmetic: 2.02 us -> 0.26 us  [block_table(): has_match = jnp.any(matches, axis=3)]
    reduce_sum x2 -> x1, other arithmetic: 1.98 us -> 0.26 us  [block_table(): position = jnp.sum(jnp.where(matches, slot_ids, 0), axis=3)]
  transfers between devices with their start and end apart: 2 -> 2, of which waited for: 0 -> 0; matrix products, arithmetic and copies ran while one was open for 6% -> 4% of each run, Pallas kernels for 28% -> 29%
where the time goes in v10:
time: 157 us
  Pallas kernels  146 us (93%)
  starting transfers between devices  5.14 us (3%)
  local copies, waits for them, and re-layouts  3.85 us (2%)
  other arithmetic  2.16 us (1%)
    pallas_call x1, Pallas kernels, halo_exchange(): pl.pallas_call(halo_kernel, out_shape=(whole, whole, whole), in_specs=[an...  71.9 us
    pallas_call x1, Pallas kernels, square_products(): pl.pallas_call(functools.partial(square_kernel, n_own, n_inner, len(piece...  45.2 us
    pallas_call x1, Pallas kernels, block_products(): pl.pallas_call(functools.partial(product_kernel, n_out, n_inner, len(piec...  28.7 us
    ppermute x2, starting transfers between devices, shifted(): return lax.ppermute(value, axis, pairs)  5.14 us
  transfers between devices with their start and end apart: 2, of which 0 were waited for; matrix products, arithmetic and copies ran while one was open for 4% of the time, Pallas kernels for 29%

profile of v10, /device:TPU:8, one launch (start us, length us, event | category | flops | bytes accessed | tf_op | source)
XLA Modules:
  0.0 157.0 jit_solution(11607449887416449683)
XLA Ops:
  0.0 71.9 %shard_map.37 = (bf16[8,16,128,128]{3,2,1,0:T(8,128)(2,1)}, bf16[8,16,128,128]{3,2,1,0:T(8,128)(2,1)}, bf16[8,16,128,128]{3,2,1,0:T(8,128)(2,1)}) custom-call(bf16[8,4,128,128]{3,2,1,0:T(8,128)(2,1)} %blocks_ref.1), custom_call_target="tpu_custom_call" | custom-call | bytes 15728640 | tf_op jit(solution)/shard_map/pallas_call | solution.py:310
  71.9 0.1 collective-permute-start
  72.0 5.1 %collective-permute-start.1 = (bf16[8,16,128,128]{3,2,1,0:T(8,128)(2,1)}, bf16[8,16,128,128]{3,2,1,0:T(8,128)(2,1)}, u32[]{:S(2)}, u32[]{:S(2)}) collective-permute-start(bf16[8,16,128,128]{3,2,1,0:T(8,128)(2,1)} %get-tuple-element.12), channel_id=1, source_target_pairs={{0,252},{4,0},{8,4},{12,8},{16,12},{20,16},{24,20},{28,24},{32,28}... | collective-permute-start | bytes 12582920 | tf_op jit(solution)/shard_map/ppermute | solution.py:14
  77.0 0.9 copy.9
  77.9 0.8 compare_select_fusion.1
  78.7 0.1 reshape.149
  78.8 1.1 gather_fusion
  79.9 0.1 copy.10
  79.9 0.9 constant_dynamic-slice_fusion.1
  80.8 0.1 pad_add_fusion
  80.9 0.8 fusion.2
  81.7 0.3 compare_reduce_fusion
  81.9 0.3 fusion
  82.2 0.1 copy.11
  82.3 0.7 select_n.56.idx_ref
  83.1 45.2 %shard_map.38 = (bf16[8,12,128,128]{3,2,1,0:T(8,128)(2,1)}, bf16[8,24,128,128]{3,2,1,0:T(8,128)(2,1)}) custom-call(s32[3840]{0:T(1024)} %select_n.56.idx_ref, bf16[8,16,128,128]{3,2,1,0:T(8,128)(2,1)} %get-tuple-element.10.left_ref, bf16[128,128,128]{2,1,0:T(8,128)(2,1)} %bitcast.13, bf16[128,128,128]{2,1,0:T(8,128)(2,1)} %bitcast.11, ...), custom_call_target="tpu_custom_call" | custom-call | flops 6442450944 | bytes 24656896 | tf_op jit(solution)/shard_map/pallas_call | solution.py:210
  128.3 0.0 collective-permute-done
  128.3 0.0 collective-permute-done.1
  128.3 28.7 %shard_map.39 = bf16[8,6,128,128]{3,2,1,0:T(8,128)(2,1)} custom-call(s32[3840]{0:T(1024)} %select_n.56.idx_ref, bf16[8,24,128,128]{3,2,1,0:T(8,128)(2,1)} %get-tuple-element.13.left_ref, bf16[128,128,128]{2,1,0:T(8,128)(2,1)} %bitcast.6.rest_0_, bf16[128,128,128]{2,1,0:T(8,128)(2,1)} %bitcast.14, bf16[128,128,128]{2,1,0:T(8,128)(2,1)} %bitcast.12, ...), custom_call_target="tpu_custom_call" | custom-call | flops 4831838208 | bytes 31996928 | tf_op jit(solution)/shard_map/pallas_call | solution.py:91
  (4 shorter events, 0.0 us)
Async XLA Ops:
  71.9 56.5 %collective-permute-start = (bf16[8,16,128,128]{3,2,1,0:T(8,128)(2,1)}, bf16[8,16,128,128]{3,2,1,0:T(8,128)(2,1)}, u32[]{:S(2)}, u32[]{:S(2)}) collective-permute-start(bf16[8,16,128,128]{3,2,1,0:T(8,128)(2,1)} %get-tuple-element.11), channel_id=1, source_target_pairs={{0,4},{4,8},{8,12},{12,16},{16,20},{20,24},{24,28},{28,32},{32,36}... | collective-permute-start | bytes 12582920 | tf_op jit(solution)/shard_map/ppermute | solution.py:14
  72.0 56.4 %collective-permute-start.1 = (bf16[8,16,128,128]{3,2,1,0:T(8,128)(2,1)}, bf16[8,16,128,128]{3,2,1,0:T(8,128)(2,1)}, u32[]{:S(2)}, u32[]{:S(2)}) collective-permute-start(bf16[8,16,128,128]{3,2,1,0:T(8,128)(2,1)} %get-tuple-element.12), channel_id=1, source_target_pairs={{0,252},{4,0},{8,4},{12,8},{16,12},{20,16},{24,20},{28,24},{32,28}... | collective-permute-start | bytes 12582920 | tf_op jit(solution)/shard_map/ppermute | solution.py:14

commit v11 on v10

--- a/solution.py
+++ b/solution.py
@@ -55,23 +55,19 @@
         for inner in range(n_inner):
             lcat[:, inner * edge:(inner + 1) * edge] = left_ref[row, inner]
 
-        def col_body(pair, carry):
-            col = 2 * pair
-            for half in range(2):
-                for inner in range(n_inner):
-                    pick = table_pick(idx_ref, view, row, inner, col + half)
-                    rcat[inner * edge:(inner + 1) * edge, half * edge:(half + 1) * edge] = halo[pick]
-            acc = jnp.dot(lcat[...], rcat[...], preferred_element_type=jnp.float32)
-            for half in range(2):
-                part = acc[:, half * edge:(half + 1) * edge]
-                if final:
-                    value = 3.0 * own_ref[row, col + half].astype(jnp.float32) - 2.0 * part
-                else:
-                    value = part
-                out_ref[row, col + half] = value.astype(out_ref.dtype)
-            return carry
-
-        return lax.fori_loop(0, n_out // 2, col_body, carry)
+        for col in range(n_out):
+            for inner in range(n_inner):
+                pick = table_pick(idx_ref, view, row, inner, col)
+                rcat[inner * edge:(inner + 1) * edge, col * edge:(col + 1) * edge] = halo[pick]
+        acc = jnp.dot(lcat[...], rcat[...], preferred_element_type=jnp.float32)
+        for col in range(n_out):
+            part = acc[:, col * edge:(col + 1) * edge]
+            if final:
+                value = 3.0 * own_ref[row, col].astype(jnp.float32) - 2.0 * part
+            else:
+                value = part
+            out_ref[row, col] = value.astype(out_ref.dtype)
+        return carry
 
     lax.fori_loop(0, left_ref.shape[0], row_body, 0)
 
@@ -96,7 +92,7 @@
         scratch_shapes=[
             pltpu.VMEM((len(pieces) * span + 1, edge, edge), left.dtype),
             pltpu.VMEM((edge, n_inner * edge), left.dtype),
-            pltpu.VMEM((n_inner * edge, 2 * edge), left.dtype),
+            pltpu.VMEM((n_inner * edge, n_out * edge), left.dtype),
             pltpu.SemaphoreType.DMA((len(pieces),)),
         ],
         compiler_params=pltpu.CompilerParams(vmem_limit_bytes=62 * 1024 * 1024),
@@ -165,18 +161,13 @@
         for inner in range(n_inner):
             lcat[:, inner * edge:(inner + 1) * edge] = left_ref[row, inner]
 
-        def col_body(pair, carry):
-            col = first + 2 * pair
-            for half in range(2):
-                for inner in range(n_inner):
-                    pick = table_pick(idx_ref, view, row, inner, col + half)
-                    rcat[inner * edge:(inner + 1) * edge, half * edge:(half + 1) * edge] = halo[pick]
-            acc = jnp.dot(lcat[...], rcat[...], preferred_element_type=jnp.float32)
-            for half in range(2):
-                out_ref[row, col + half] = acc[:, half * edge:(half + 1) * edge].astype(out_ref.dtype)
-            return carry
-
-        lax.fori_loop(0, n_own // 2, col_body, 0)
+        for part in range(n_own):
+            for inner in range(n_inner):
+                pick = table_pick(idx_ref, view, row, inner, first + part)
+                rcat[inner * edge:(inner + 1) * edge, part * edge:(part + 1) * edge] = halo[pick]
+        acc = jnp.dot(lcat[...], rcat[...], preferred_element_type=jnp.float32)
+        for part in range(n_own):
+            out_ref[row, first + part] = acc[:, part * edge:(part + 1) * edge].astype(out_ref.dtype)
 
     def own_body(row, carry):
         products(row, 0)
@@ -218,7 +209,7 @@
         scratch_shapes=[
             pltpu.VMEM((len(pieces) * span + 1, edge, edge), left.dtype),
             pltpu.VMEM((edge, n_inner * edge), left.dtype),
-            pltpu.VMEM((n_inner * edge, 2 * edge), left.dtype),
+            pltpu.VMEM((n_inner * edge, n_own * edge), left.dtype),
             pltpu.SemaphoreType.DMA((len(pieces),)),
             pltpu.SemaphoreType.DMA((rows, 3)),
             pltpu.SemaphoreType.DMA((rows, 3)),

time: 157 us -> 155 us (0.987)
  Pallas kernels: 146 us -> 143 us
    pallas_call x1, Pallas kernels: 28.7 us -> 26.2 us  [block_products(): pl.pallas_call(functools.partial(product_kernel, n_out, n_inner, len(piec...]
where the time goes in v11:
time: 155 us; the launch traced here: 154 us
  Pallas kernels  143 us (92%)
  starting transfers between devices  5.14 us (3%)
  local copies, waits for them, and re-layouts  3.85 us (2%)
  other arithmetic  2.16 us (1%)
    pallas_call x1, Pallas kernels, halo_exchange(): pl.pallas_call(halo_kernel, out_shape=(whole, whole, whole), in_specs=[an...  71.9 us
    pallas_call x1, Pallas kernels, square_products(): pl.pallas_call(functools.partial(square_kernel, n_own, n_inner, len(piece...  44.9 us
    pallas_call x1, Pallas kernels, block_products(): pl.pallas_call(functools.partial(product_kernel, n_out, n_inner, len(piec...  26.2 us
    ppermute x2, starting transfers between devices, shifted(): return lax.ppermute(value, axis, pairs)  5.14 us
  transfers between devices with their start and end apart: 2, of which 0 were waited for; matrix products, arithmetic and copies ran while one was open for 4% of the time, Pallas kernels for 29%

profile of v11, /device:TPU:8, one launch (start us, length us, event | category | flops | bytes accessed | tf_op | source)
XLA Modules:
  0.0 154.2 jit_solution(17810308760085708928)
XLA Ops:
  0.0 71.9 %shard_map.37 = (bf16[8,16,128,128]{3,2,1,0:T(8,128)(2,1)}, bf16[8,16,128,128]{3,2,1,0:T(8,128)(2,1)}, bf16[8,16,128,128]{3,2,1,0:T(8,128)(2,1)}) custom-call(bf16[8,4,128,128]{3,2,1,0:T(8,128)(2,1)} %blocks_ref.1), custom_call_target="tpu_custom_call" | custom-call | bytes 15728640 | tf_op jit(solution)/shard_map/pallas_call | solution.py:301
  71.9 0.1 collective-permute-start
  72.0 5.1 %collective-permute-start.1 = (bf16[8,16,128,128]{3,2,1,0:T(8,128)(2,1)}, bf16[8,16,128,128]{3,2,1,0:T(8,128)(2,1)}, u32[]{:S(2)}, u32[]{:S(2)}) collective-permute-start(bf16[8,16,128,128]{3,2,1,0:T(8,128)(2,1)} %get-tuple-element.12), channel_id=1, source_target_pairs={{0,252},{4,0},{8,4},{12,8},{16,12},{20,16},{24,20},{28,24},{32,28}... | collective-permute-start | bytes 12582920 | tf_op jit(solution)/shard_map/ppermute | solution.py:14
  77.0 0.9 copy.9
  77.9 0.8 compare_select_fusion.1
  78.7 0.1 reshape.149
  78.8 1.1 gather_fusion
  79.9 0.1 copy.10
  79.9 0.9 constant_dynamic-slice_fusion.1
  80.8 0.1 pad_add_fusion
  80.9 0.8 fusion.2
  81.7 0.3 compare_reduce_fusion
  81.9 0.3 fusion
  82.2 0.1 copy.11
  82.3 0.7 select_n.56.idx_ref
  83.1 44.9 %shard_map.38 = (bf16[8,12,128,128]{3,2,1,0:T(8,128)(2,1)}, bf16[8,24,128,128]{3,2,1,0:T(8,128)(2,1)}) custom-call(s32[3840]{0:T(1024)} %select_n.56.idx_ref, bf16[8,16,128,128]{3,2,1,0:T(8,128)(2,1)} %get-tuple-element.10.left_ref, bf16[128,128,128]{2,1,0:T(8,128)(2,1)} %bitcast.13, bf16[128,128,128]{2,1,0:T(8,128)(2,1)} %bitcast.11, ...), custom_call_target="tpu_custom_call" | custom-call | flops 6442450944 | bytes 24656896 | tf_op jit(solution)/shard_map/pallas_call | solution.py:201
  128.0 0.0 collective-permute-done
  128.0 0.0 collective-permute-done.1
  128.0 26.2 %shard_map.39 = bf16[8,6,128,128]{3,2,1,0:T(8,128)(2,1)} custom-call(s32[3840]{0:T(1024)} %select_n.56.idx_ref, bf16[8,24,128,128]{3,2,1,0:T(8,128)(2,1)} %get-tuple-element.13.left_ref, bf16[128,128,128]{2,1,0:T(8,128)(2,1)} %bitcast.6.rest_0_, bf16[128,128,128]{2,1,0:T(8,128)(2,1)} %bitcast.14, bf16[128,128,128]{2,1,0:T(8,128)(2,1)} %bitcast.12, ...), custom_call_target="tpu_custom_call" | custom-call | flops 4831838208 | bytes 31996928 | tf_op jit(solution)/shard_map/pallas_call | solution.py:87
  (4 shorter events, 0.0 us)
Async XLA Ops:
  71.9 56.1 %collective-permute-start = (bf16[8,16,128,128]{3,2,1,0:T(8,128)(2,1)}, bf16[8,16,128,128]{3,2,1,0:T(8,128)(2,1)}, u32[]{:S(2)}, u32[]{:S(2)}) collective-permute-start(bf16[8,16,128,128]{3,2,1,0:T(8,128)(2,1)} %get-tuple-element.11), channel_id=1, source_target_pairs={{0,4},{4,8},{8,12},{12,16},{16,20},{20,24},{24,28},{28,32},{32,36}... | collective-permute-start | bytes 12582920 | tf_op jit(solution)/shard_map/ppermute | solution.py:14
  72.0 56.0 %collective-permute-start.1 = (bf16[8,16,128,128]{3,2,1,0:T(8,128)(2,1)}, bf16[8,16,128,128]{3,2,1,0:T(8,128)(2,1)}, u32[]{:S(2)}, u32[]{:S(2)}) collective-permute-start(bf16[8,16,128,128]{3,2,1,0:T(8,128)(2,1)} %get-tuple-element.12), channel_id=1, source_target_pairs={{0,252},{4,0},{8,4},{12,8},{16,12},{20,16},{24,20},{28,24},{32,28}... | collective-permute-start | bytes 12582920 | tf_op jit(solution)/shard_map/ppermute | solution.py:14

commit v12 on v11

--- a/solution.py
+++ b/solution.py
@@ -222,7 +222,10 @@
     )(*operands)
 
 
-def halo_kernel(blocks_ref, full_ref, left_ref, right_ref, send_sems, recv_sems, side_send, side_recv):
+def halo_kernel(
+    blocks_ref, full_ref, left_ref, right_ref, send_sems, recv_sems, side_send, side_recv,
+    relay_sems,
+):
     quarter = blocks_ref.shape[1]
     row_at = lax.axis_index("row")
     col_at = lax.axis_index("col")
@@ -272,21 +275,42 @@
             device_id_type=MESH,
         )
 
-    for k in range(1, depth_count):
+    def slot_of(k):
+        return pl.ds(lax.rem(depth_at + depth_count - k, depth_count) * quarter, quarter)
+
+    def relay(row):
+        k, target = (1, peer_ids[0]) if row < rows // 2 else (3, peer_ids[2])
+        return pltpu.make_async_remote_copy(
+            src_ref=full_ref.at[row, slot_of(k)],
+            dst_ref=full_ref.at[row, slot_of(k)],
+            send_sem=relay_sems.at[0, row],
+            recv_sem=relay_sems.at[1, row],
+            device_id=target,
+            device_id_type=MESH,
+        )
+
+    for k in (1, 3):
         for row in range(rows):
             to_peer(k, row).start()
     for row in range(rows):
         for way in range(2):
             to_side(0, row, way).start()
-    for k in sorted(range(1, depth_count), key=lambda k: min(k, depth_count - k)):
-        for row in range(rows):
+    for row in range(rows):
+        for k in (1, 3):
             to_peer(k, row).wait_recv()
             for way in range(2):
                 to_side(k, row, way).start()
+            if (k == 1) == (row < rows // 2):
+                relay(row).start()
+    for row in range(rows):
+        relay(row).wait_recv()
+        for way in range(2):
+            to_side(2, row, way).start()
     local.wait()
-    for k in range(1, depth_count):
-        for row in range(rows):
+    for row in range(rows):
+        for k in (1, 3):
             to_peer(k, row).wait_send()
+        relay(row).wait_send()
     for k in range(depth_count):
         for row in range(rows):
             for way in range(2):
@@ -308,6 +332,7 @@
             pltpu.SemaphoreType.DMA((depth_count, rows)),
             pltpu.SemaphoreType.DMA((3, depth_count, rows)),
             pltpu.SemaphoreType.DMA((2, depth_count, rows)),
+            pltpu.SemaphoreType.DMA((2, rows)),
         ],
         compiler_params=pltpu.CompilerParams(collective_id=1, has_side_effects=True),
         cost_estimate=pl.CostEstimate(flops=0, transcendentals=0, bytes_accessed=moved),

time: 155 us -> 139 us (0.90)
  Pallas kernels: 143 us -> 127 us
    pallas_call x1, Pallas kernels: 71.9 us -> 58.3 us  [halo_exchange(): pl.pallas_call(halo_kernel, out_shape=(whole, whole, whole), in_specs=[an...]
    pallas_call x1, Pallas kernels: 44.9 us -> 42.7 us  [square_products(): pl.pallas_call(functools.partial(square_kernel, n_own, n_inner, len(piece...]
  transfers between devices with their start and end apart: 2 -> 2, of which waited for: 0 -> 0; matrix products, arithmetic and copies ran while one was open for 4% -> 4% of each run, Pallas kernels for 29% -> 31%
where the time goes in v12:
time: 139 us; the launch traced here: 138 us
  Pallas kernels  127 us (91%)
  starting transfers between devices  5.14 us (4%)
  local copies, waits for them, and re-layouts  3.85 us (3%)
  other arithmetic  2.16 us (2%)
    pallas_call x1, Pallas kernels, halo_exchange(): pl.pallas_call(halo_kernel, out_shape=(whole, whole, whole), in_specs=[an...  58.3 us
    pallas_call x1, Pallas kernels, square_products(): pl.pallas_call(functools.partial(square_kernel, n_own, n_inner, len(piece...  42.7 us
    pallas_call x1, Pallas kernels, block_products(): pl.pallas_call(functools.partial(product_kernel, n_out, n_inner, len(piec...  26.2 us
    ppermute x2, starting transfers between devices, shifted(): return lax.ppermute(value, axis, pairs)  5.14 us
  transfers between devices with their start and end apart: 2, of which 0 were waited for; matrix products, arithmetic and copies ran while one was open for 4% of the time, Pallas kernels for 31%

profile of v12, /device:TPU:8, one launch (start us, length us, event | category | flops | bytes accessed | tf_op | source)
XLA Modules:
  0.0 138.5 jit_solution(14126313607032158316)
XLA Ops:
  0.0 58.3 %shard_map.37 = (bf16[8,16,128,128]{3,2,1,0:T(8,128)(2,1)}, bf16[8,16,128,128]{3,2,1,0:T(8,128)(2,1)}, bf16[8,16,128,128]{3,2,1,0:T(8,128)(2,1)}) custom-call(bf16[8,4,128,128]{3,2,1,0:T(8,128)(2,1)} %blocks_ref.1), custom_call_target="tpu_custom_call" | custom-call | bytes 15728640 | tf_op jit(solution)/shard_map/pallas_call | solution.py:325
  58.3 0.1 collective-permute-start
  58.4 5.1 %collective-permute-start.1 = (bf16[8,16,128,128]{3,2,1,0:T(8,128)(2,1)}, bf16[8,16,128,128]{3,2,1,0:T(8,128)(2,1)}, u32[]{:S(2)}, u32[]{:S(2)}) collective-permute-start(bf16[8,16,128,128]{3,2,1,0:T(8,128)(2,1)} %get-tuple-element.12), channel_id=1, source_target_pairs={{0,252},{4,0},{8,4},{12,8},{16,12},{20,16},{24,20},{28,24},{32,28}... | collective-permute-start | bytes 12582920 | tf_op jit(solution)/shard_map/ppermute | solution.py:14
  63.4 0.9 copy.9
  64.3 0.8 compare_select_fusion.1
  65.1 0.1 reshape.149
  65.2 1.1 gather_fusion
  66.3 0.1 copy.10
  66.4 0.9 constant_dynamic-slice_fusion.1
  67.2 0.1 pad_add_fusion
  67.3 0.8 fusion.2
  68.1 0.3 compare_reduce_fusion
  68.3 0.3 fusion
  68.6 0.1 copy.11
  68.8 0.7 select_n.56.idx_ref
  69.5 42.7 %shard_map.38 = (bf16[8,12,128,128]{3,2,1,0:T(8,128)(2,1)}, bf16[8,24,128,128]{3,2,1,0:T(8,128)(2,1)}) custom-call(s32[3840]{0:T(1024)} %select_n.56.idx_ref, bf16[8,16,128,128]{3,2,1,0:T(8,128)(2,1)} %get-tuple-element.10.left_ref, bf16[128,128,128]{2,1,0:T(8,128)(2,1)} %bitcast.13, bf16[128,128,128]{2,1,0:T(8,128)(2,1)} %bitcast.11, ...), custom_call_target="tpu_custom_call" | custom-call | flops 6442450944 | bytes 24656896 | tf_op jit(solution)/shard_map/pallas_call | solution.py:201
  112.2 0.0 collective-permute-done
  112.2 0.0 collective-permute-done.1
  112.3 26.2 %shard_map.39 = bf16[8,6,128,128]{3,2,1,0:T(8,128)(2,1)} custom-call(s32[3840]{0:T(1024)} %select_n.56.idx_ref, bf16[8,24,128,128]{3,2,1,0:T(8,128)(2,1)} %get-tuple-element.13.left_ref, bf16[128,128,128]{2,1,0:T(8,128)(2,1)} %bitcast.6.rest_0_, bf16[128,128,128]{2,1,0:T(8,128)(2,1)} %bitcast.14, bf16[128,128,128]{2,1,0:T(8,128)(2,1)} %bitcast.12, ...), custom_call_target="tpu_custom_call" | custom-call | flops 4831838208 | bytes 31996928 | tf_op jit(solution)/shard_map/pallas_call | solution.py:87
  (4 shorter events, 0.0 us)
Async XLA Ops:
  58.3 53.9 %collective-permute-start = (bf16[8,16,128,128]{3,2,1,0:T(8,128)(2,1)}, bf16[8,16,128,128]{3,2,1,0:T(8,128)(2,1)}, u32[]{:S(2)}, u32[]{:S(2)}) collective-permute-start(bf16[8,16,128,128]{3,2,1,0:T(8,128)(2,1)} %get-tuple-element.11), channel_id=1, source_target_pairs={{0,4},{4,8},{8,12},{12,16},{16,20},{20,24},{24,28},{28,32},{32,36}... | collective-permute-start | bytes 12582920 | tf_op jit(solution)/shard_map/ppermute | solution.py:14
  58.4 53.9 %collective-permute-start.1 = (bf16[8,16,128,128]{3,2,1,0:T(8,128)(2,1)}, bf16[8,16,128,128]{3,2,1,0:T(8,128)(2,1)}, u32[]{:S(2)}, u32[]{:S(2)}) collective-permute-start(bf16[8,16,128,128]{3,2,1,0:T(8,128)(2,1)} %get-tuple-element.12), channel_id=1, source_target_pairs={{0,252},{4,0},{8,4},{12,8},{16,12},{20,16},{24,20},{28,24},{32,28}... | collective-permute-start | bytes 12582920 | tf_op jit(solution)/shard_map/ppermute | solution.py:14

commit v13 on v12

--- a/solution.py
+++ b/solution.py
@@ -351,8 +351,6 @@
 
     full_rows, from_before, from_after = halo_exchange(blocks, depth_count)
     near = {0: full_rows, 1: from_before, -1: from_after}
-    near[2] = shifted(near[1], ("row", "col"), 1)
-    near[-2] = shifted(near[-1], ("row", "col"), -1)
 
     def halo_of(reach):
         return [near[offset] for offset in range(reach, -reach - 1, -1)]
@@ -365,15 +363,21 @@
     across_targets = lax.dynamic_slice_in_dim(
         product_cols, ((depth_index + 2) % depth_count) * target_share, target_share, 1
     )
-    halo_first = halo_of(1)
-    halo_second = halo_of(2)
     piece_blocks = row_count * fill_count
+    block_cols, product_cols, near[1] = lax.optimization_barrier(
+        (block_cols, product_cols, near[1])
+    )
     inner_rows = jnp.concatenate([own_cols, product_cols], axis=1)
     targets = jnp.concatenate([own_targets, across_targets], axis=1)
     table = block_table(
         block_cols, inner_rows, targets, (row_place - 2) * row_count, order_total,
-        fill_count, len(halo_second) * piece_blocks,
-    )
+        fill_count, 5 * piece_blocks,
+    )
+    table, near[1], near[-1] = lax.optimization_barrier((table, near[1], near[-1]))
+    near[2] = shifted(near[1], ("row", "col"), 1)
+    near[-2] = shifted(near[-1], ("row", "col"), -1)
+    halo_first = halo_of(1)
+    halo_second = halo_of(2)
     row_stride = inner_rows.shape[1] * targets.shape[1]
     first_view = (row_stride, 0, targets.shape[1], piece_blocks, len(halo_first) * piece_blocks)
     second_view = (row_stride, fill_count, targets.shape[1], 0, len(halo_second) * piece_blocks)

time: 139 us -> 143 us (1.029)
  waiting for transfers between devices: 0.01 us -> 2.89 us
    ppermute x2, waiting for transfers between devices: 0.01 us -> 2.89 us  [shifted(): return lax.ppermute(value, axis, pairs)]
  transfers between devices with their start and end apart: 2 -> 2, of which waited for: 0 -> 1; matrix products, arithmetic and copies ran while one was open for 4% -> 1% of each run, Pallas kernels for 31% -> 30%
where the time goes in v13:
time: 143 us; the launch traced here: 142 us
  Pallas kernels  127 us (89%)
  starting transfers between devices  5.14 us (4%)
  local copies, waits for them, and re-layouts  4.69 us (3%)
  waiting for transfers between devices  2.89 us (2%)
  other arithmetic  2.17 us (2%)
    pallas_call x1, Pallas kernels, halo_exchange(): pl.pallas_call(halo_kernel, out_shape=(whole, whole, whole), in_specs=[an...  58.3 us
    pallas_call x1, Pallas kernels, square_products(): pl.pallas_call(functools.partial(square_kernel, n_own, n_inner, len(piece...  42.7 us
    pallas_call x1, Pallas kernels, block_products(): pl.pallas_call(functools.partial(product_kernel, n_out, n_inner, len(piec...  26.2 us
    ppermute x2, starting transfers between devices, shifted(): return lax.ppermute(value, axis, pairs)  5.14 us
    ppermute x2, waiting for transfers between devices, shifted(): return lax.ppermute(value, axis, pairs)  2.89 us
  transfers between devices with their start and end apart: 2, of which 1 were waited for; matrix products, arithmetic and copies ran while one was open for 1% of the time, Pallas kernels for 30%

profile of v13, /device:TPU:8, one launch (start us, length us, event | category | flops | bytes accessed | tf_op | source)
XLA Modules:
  0.0 142.2 jit_solution(10573851269611556460)
XLA Ops:
  0.0 0.8 constant_dynamic-slice_fusion.2
  0.8 0.1 copy.12
  0.8 58.3 %shard_map.37 = (bf16[8,16,128,128]{3,2,1,0:T(8,128)(2,1)}, bf16[8,16,128,128]{3,2,1,0:T(8,128)(2,1)}, bf16[8,16,128,128]{3,2,1,0:T(8,128)(2,1)}) custom-call(bf16[8,4,128,128]{3,2,1,0:T(8,128)(2,1)} %blocks_ref.1), custom_call_target="tpu_custom_call" | custom-call | bytes 15728640 | tf_op jit(solution)/shard_map/pallas_call | solution.py:325
  59.2 0.8 compare_select_fusion.1
  59.9 0.1 reshape.143
  60.0 0.9 copy.9
  60.9 1.1 gather_fusion
  62.0 0.1 copy.10
  62.1 0.9 constant_dynamic-slice_fusion.1
  62.9 0.1 pad_add_fusion
  63.0 0.3 compare_reduce_fusion
  63.3 0.3 fusion
  63.6 0.8 fusion.2
  64.4 0.1 collective-permute-start
  64.5 5.1 %collective-permute-start.1 = (bf16[8,16,128,128]{3,2,1,0:T(8,128)(2,1)}, bf16[8,16,128,128]{3,2,1,0:T(8,128)(2,1)}, u32[]{:S(2)}, u32[]{:S(2)}) collective-permute-start(bf16[8,16,128,128]{3,2,1,0:T(8,128)(2,1)} %get-tuple-element.24), channel_id=1, source_target_pairs={{0,252},{4,0},{8,4},{12,8},{16,12},{20,16},{24,20},{28,24},{32,28}... | collective-permute-start | bytes 12582920 | tf_op jit(solution)/shard_map/ppermute | solution.py:14
  69.5 0.1 copy.11
  69.6 0.7 reshape.135.idx_ref
  70.4 42.7 %shard_map.38 = (bf16[8,12,128,128]{3,2,1,0:T(8,128)(2,1)}, bf16[8,24,128,128]{3,2,1,0:T(8,128)(2,1)}) custom-call(s32[3840]{0:T(1024)} %reshape.135.idx_ref, bf16[8,16,128,128]{3,2,1,0:T(8,128)(2,1)} %get-tuple-element.22.left_ref, bf16[128,128,128]{2,1,0:T(8,128)(2,1)} %bitcast.12, bf16[128,128,128]{2,1,0:T(8,128)(2,1)} %bitcast.10, ...), custom_call_target="tpu_custom_call" | custom-call | flops 6442450944 | bytes 24656896 | tf_op jit(solution)/shard_map/pallas_call | solution.py:201
  113.1 2.9 %collective-permute-done = bf16[8,16,128,128]{3,2,1,0:T(8,128)(2,1)} collective-permute-done((bf16[8,16,128,128]{3,2,1,0:T(8,128)(2,1)}, bf16[8,16,128,128]{3,2,1,0:T(8,128)(2,1)}, u32[]{:S(2)}, u32[]{:S(2)}) %collective-permute-start) | collective-permute-done | bytes 4194336 | tf_op jit(solution)/shard_map/ppermute | solution.py:14
  116.0 0.0 collective-permute-done.1
  116.0 26.2 %shard_map.39 = bf16[8,6,128,128]{3,2,1,0:T(8,128)(2,1)} custom-call(s32[3840]{0:T(1024)} %reshape.135.idx_ref, bf16[8,24,128,128]{3,2,1,0:T(8,128)(2,1)} %get-tuple-element.25.left_ref, bf16[128,128,128]{2,1,0:T(8,128)(2,1)} %bitcast.6.rest_0_, bf16[128,128,128]{2,1,0:T(8,128)(2,1)} %bitcast.13, bf16[128,128,128]{2,1,0:T(8,128)(2,1)} %bitcast.11, ...), custom_call_target="tpu_custom_call" | custom-call | flops 4831838208 | bytes 31996928 | tf_op jit(solution)/shard_map/pallas_call | solution.py:87
  (2 shorter events, 0.0 us)
Async XLA Ops:
  64.4 51.6 %collective-permute-start = (bf16[8,16,128,128]{3,2,1,0:T(8,128)(2,1)}, bf16[8,16,128,128]{3,2,1,0:T(8,128)(2,1)}, u32[]{:S(2)}, u32[]{:S(2)}) collective-permute-start(bf16[8,16,128,128]{3,2,1,0:T(8,128)(2,1)} %get-tuple-element.23), channel_id=1, source_target_pairs={{0,4},{4,8},{8,12},{12,16},{16,20},{20,24},{24,28},{28,32},{32,36}... | collective-permute-start | bytes 12582920 | tf_op jit(solution)/shard_map/ppermute | solution.py:14
  64.5 51.6 %collective-permute-start.1 = (bf16[8,16,128,128]{3,2,1,0:T(8,128)(2,1)}, bf16[8,16,128,128]{3,2,1,0:T(8,128)(2,1)}, u32[]{:S(2)}, u32[]{:S(2)}) collective-permute-start(bf16[8,16,128,128]{3,2,1,0:T(8,128)(2,1)} %get-tuple-element.24), channel_id=1, source_target_pairs={{0,252},{4,0},{8,4},{12,8},{16,12},{20,16},{24,20},{28,24},{32,28}... | collective-permute-start | bytes 12582920 | tf_op jit(solution)/shard_map/ppermute | solution.py:14

commit v14 on v12

--- a/solution.py
+++ b/solution.py
@@ -289,23 +289,26 @@
             device_id_type=MESH,
         )
 
-    for k in (1, 3):
-        for row in range(rows):
-            to_peer(k, row).start()
+    order = {1: list(range(rows)), 3: list(range(rows - 1, -1, -1))}
+    for step in range(rows):
+        for k in (1, 3):
+            to_peer(k, order[k][step]).start()
     for row in range(rows):
         for way in range(2):
             to_side(0, row, way).start()
-    for row in range(rows):
+    for step in range(rows):
         for k in (1, 3):
+            row = order[k][step]
             to_peer(k, row).wait_recv()
+            if (k == 1) == (row < rows // 2):
+                relay(row).start()
             for way in range(2):
                 to_side(k, row, way).start()
-            if (k == 1) == (row < rows // 2):
-                relay(row).start()
-    for row in range(rows):
-        relay(row).wait_recv()
-        for way in range(2):
-            to_side(2, row, way).start()
+    for step in range(rows // 2):
+        for row in (step, rows - 1 - step):
+            relay(row).wait_recv()
+            for way in range(2):
+                to_side(2, row, way).start()
     local.wait()
     for row in range(rows):
         for k in (1, 3):

time: 139 us -> 139 us (level)
  no operation moved by 1% of the time
where the time goes in v14:
time: 139 us; the launch traced here: 138 us
  Pallas kernels  127 us (91%)
  starting transfers between devices  5.14 us (4%)
  local copies, waits for them, and re-layouts  3.85 us (3%)
  other arithmetic  2.16 us (2%)
    pallas_call x1, Pallas kernels, halo_exchange(): pl.pallas_call(halo_kernel, out_shape=(whole, whole, whole), in_specs=[an...  58.3 us
    pallas_call x1, Pallas kernels, square_products(): pl.pallas_call(functools.partial(square_kernel, n_own, n_inner, len(piece...  42.7 us
    pallas_call x1, Pallas kernels, block_products(): pl.pallas_call(functools.partial(product_kernel, n_out, n_inner, len(piec...  26.2 us
    ppermute x2, starting transfers between devices, shifted(): return lax.ppermute(value, axis, pairs)  5.14 us
  transfers between devices with their start and end apart: 2, of which 0 were waited for; matrix products, arithmetic and copies ran while one was open for 4% of the time, Pallas kernels for 31%

profile of v14, /device:TPU:8, one launch (start us, length us, event | category | flops | bytes accessed | tf_op | source)
XLA Modules:
  0.0 138.5 jit_solution(9231410796003863919)
XLA Ops:
  0.0 58.3 %shard_map.37 = (bf16[8,16,128,128]{3,2,1,0:T(8,128)(2,1)}, bf16[8,16,128,128]{3,2,1,0:T(8,128)(2,1)}, bf16[8,16,128,128]{3,2,1,0:T(8,128)(2,1)}) custom-call(bf16[8,4,128,128]{3,2,1,0:T(8,128)(2,1)} %blocks_ref.1), custom_call_target="tpu_custom_call" | custom-call | bytes 15728640 | tf_op jit(solution)/shard_map/pallas_call | solution.py:328
  58.3 0.1 collective-permute-start
  58.4 5.1 %collective-permute-start.1 = (bf16[8,16,128,128]{3,2,1,0:T(8,128)(2,1)}, bf16[8,16,128,128]{3,2,1,0:T(8,128)(2,1)}, u32[]{:S(2)}, u32[]{:S(2)}) collective-permute-start(bf16[8,16,128,128]{3,2,1,0:T(8,128)(2,1)} %get-tuple-element.12), channel_id=1, source_target_pairs={{0,252},{4,0},{8,4},{12,8},{16,12},{20,16},{24,20},{28,24},{32,28}... | collective-permute-start | bytes 12582920 | tf_op jit(solution)/shard_map/ppermute | solution.py:14
  63.4 0.9 copy.9
  64.4 0.8 compare_select_fusion.1
  65.1 0.1 reshape.149
  65.2 1.1 gather_fusion
  66.3 0.1 copy.10
  66.4 0.9 constant_dynamic-slice_fusion.1
  67.2 0.1 pad_add_fusion
  67.3 0.8 fusion.2
  68.1 0.3 compare_reduce_fusion
  68.3 0.3 fusion
  68.6 0.1 copy.11
  68.8 0.7 select_n.56.idx_ref
  69.5 42.7 %shard_map.38 = (bf16[8,12,128,128]{3,2,1,0:T(8,128)(2,1)}, bf16[8,24,128,128]{3,2,1,0:T(8,128)(2,1)}) custom-call(s32[3840]{0:T(1024)} %select_n.56.idx_ref, bf16[8,16,128,128]{3,2,1,0:T(8,128)(2,1)} %get-tuple-element.10.left_ref, bf16[128,128,128]{2,1,0:T(8,128)(2,1)} %bitcast.13, bf16[128,128,128]{2,1,0:T(8,128)(2,1)} %bitcast.11, ...), custom_call_target="tpu_custom_call" | custom-call | flops 6442450944 | bytes 24656896 | tf_op jit(solution)/shard_map/pallas_call | solution.py:201
  112.2 0.0 collective-permute-done
  112.3 0.0 collective-permute-done.1
  112.3 26.2 %shard_map.39 = bf16[8,6,128,128]{3,2,1,0:T(8,128)(2,1)} custom-call(s32[3840]{0:T(1024)} %select_n.56.idx_ref, bf16[8,24,128,128]{3,2,1,0:T(8,128)(2,1)} %get-tuple-element.13.left_ref, bf16[128,128,128]{2,1,0:T(8,128)(2,1)} %bitcast.6.rest_0_, bf16[128,128,128]{2,1,0:T(8,128)(2,1)} %bitcast.14, bf16[128,128,128]{2,1,0:T(8,128)(2,1)} %bitcast.12, ...), custom_call_target="tpu_custom_call" | custom-call | flops 4831838208 | bytes 31996928 | tf_op jit(solution)/shard_map/pallas_call | solution.py:87
  (4 shorter events, 0.0 us)
Async XLA Ops:
  58.3 53.9 %collective-permute-start = (bf16[8,16,128,128]{3,2,1,0:T(8,128)(2,1)}, bf16[8,16,128,128]{3,2,1,0:T(8,128)(2,1)}, u32[]{:S(2)}, u32[]{:S(2)}) collective-permute-start(bf16[8,16,128,128]{3,2,1,0:T(8,128)(2,1)} %get-tuple-element.11), channel_id=1, source_target_pairs={{0,4},{4,8},{8,12},{12,16},{16,20},{20,24},{24,28},{28,32},{32,36}... | collective-permute-start | bytes 12582920 | tf_op jit(solution)/shard_map/ppermute | solution.py:14
  58.4 53.9 %collective-permute-start.1 = (bf16[8,16,128,128]{3,2,1,0:T(8,128)(2,1)}, bf16[8,16,128,128]{3,2,1,0:T(8,128)(2,1)}, u32[]{:S(2)}, u32[]{:S(2)}) collective-permute-start(bf16[8,16,128,128]{3,2,1,0:T(8,128)(2,1)} %get-tuple-element.12), channel_id=1, source_target_pairs={{0,252},{4,0},{8,4},{12,8},{16,12},{20,16},{24,20},{28,24},{32,28}... | collective-permute-start | bytes 12582920 | tf_op jit(solution)/shard_map/ppermute | solution.py:14

commit v15 on v14

--- a/solution.py
+++ b/solution.py
@@ -32,16 +32,16 @@
     return jnp.minimum(jnp.maximum(entry - shift, 0), cap)
 
 
-def product_kernel(n_out, n_inner, n_pieces, final, view, idx_ref, left_ref, *rest):
+def product_kernel(n_out, n_inner, n_pieces, final, view, idx_ref, left_hbm, *rest):
     pieces = rest[:n_pieces]
     rest = rest[n_pieces:]
     if final:
-        own_ref, out_ref, halo, lcat, rcat, sems = rest
+        own_ref, out_ref, halo, lcat, rcat, left_ref, sems = rest
     else:
-        out_ref, halo, lcat, rcat, sems = rest
+        out_ref, halo, lcat, rcat, left_ref, sems = rest
     edge = left_ref.shape[-1]
     span = pieces[0].shape[0]
-    copies = [
+    copies = [pltpu.make_async_copy(left_hbm, left_ref, sems.at[n_pieces])] + [
         pltpu.make_async_copy(piece, halo.at[pl.ds(k * span, span)], sems.at[k])
         for k, piece in enumerate(pieces)
     ]
@@ -80,7 +80,7 @@
     operands = [table.reshape(-1), left] + flat_pieces + ([own] if final else [])
     vmem = pl.BlockSpec(memory_space=pltpu.VMEM)
     anywhere = pl.BlockSpec(memory_space=pl.ANY)
-    in_specs = [pl.BlockSpec(memory_space=pltpu.SMEM), vmem] + [anywhere] * len(pieces)
+    in_specs = [pl.BlockSpec(memory_space=pltpu.SMEM), anywhere] + [anywhere] * len(pieces)
     in_specs += [vmem] if final else []
     flops = 2 * rows * n_out * n_inner * edge ** 3
     moved = sum(int(x.size) * x.dtype.itemsize for x in operands) + rows * n_out * edge * edge * 2
@@ -93,7 +93,8 @@
             pltpu.VMEM((len(pieces) * span + 1, edge, edge), left.dtype),
             pltpu.VMEM((edge, n_inner * edge), left.dtype),
             pltpu.VMEM((n_inner * edge, n_out * edge), left.dtype),
-            pltpu.SemaphoreType.DMA((len(pieces),)),
+            pltpu.VMEM(left.shape, left.dtype),
+            pltpu.SemaphoreType.DMA((len(pieces) + 1,)),
         ],
         compiler_params=pltpu.CompilerParams(vmem_limit_bytes=62 * 1024 * 1024),
         cost_estimate=pl.CostEstimate(flops=flops, transcendentals=0, bytes_accessed=moved),

time: 139 us -> 139 us (level)
  no operation moved by 1% of the time
where the time goes in v15:
time: 139 us; the launch traced here: 138 us
  Pallas kernels  127 us (91%)
  starting transfers between devices  5.14 us (4%)
  local copies, waits for them, and re-layouts  3.85 us (3%)
  other arithmetic  2.16 us (2%)
    pallas_call x1, Pallas kernels, halo_exchange(): pl.pallas_call(halo_kernel, out_shape=(whole, whole, whole), in_specs=[an...  58.3 us
    pallas_call x1, Pallas kernels, square_products(): pl.pallas_call(functools.partial(square_kernel, n_own, n_inner, len(piece...  42.7 us
    pallas_call x1, Pallas kernels, block_products(): pl.pallas_call(functools.partial(product_kernel, n_out, n_inner, len(piec...  26.1 us
    ppermute x2, starting transfers between devices, shifted(): return lax.ppermute(value, axis, pairs)  5.14 us
  transfers between devices with their start and end apart: 2, of which 0 were waited for; matrix products, arithmetic and copies ran while one was open for 4% of the time, Pallas kernels for 31%

profile of v15, /device:TPU:8, one launch (start us, length us, event | category | flops | bytes accessed | tf_op | source)
XLA Modules:
  0.0 138.4 jit_solution(15350484505332824853)
XLA Ops:
  0.0 58.3 %shard_map.37 = (bf16[8,16,128,128]{3,2,1,0:T(8,128)(2,1)}, bf16[8,16,128,128]{3,2,1,0:T(8,128)(2,1)}, bf16[8,16,128,128]{3,2,1,0:T(8,128)(2,1)}) custom-call(bf16[8,4,128,128]{3,2,1,0:T(8,128)(2,1)} %blocks_ref.1), custom_call_target="tpu_custom_call" | custom-call | bytes 15728640 | tf_op jit(solution)/shard_map/pallas_call | solution.py:329
  58.3 0.1 collective-permute-start
  58.4 5.1 %collective-permute-start.1 = (bf16[8,16,128,128]{3,2,1,0:T(8,128)(2,1)}, bf16[8,16,128,128]{3,2,1,0:T(8,128)(2,1)}, u32[]{:S(2)}, u32[]{:S(2)}) collective-permute-start(bf16[8,16,128,128]{3,2,1,0:T(8,128)(2,1)} %get-tuple-element.12), channel_id=1, source_target_pairs={{0,252},{4,0},{8,4},{12,8},{16,12},{20,16},{24,20},{28,24},{32,28}... | collective-permute-start | bytes 12582920 | tf_op jit(solution)/shard_map/ppermute | solution.py:14
  63.4 0.9 copy.9
  64.4 0.8 compare_select_fusion.1
  65.1 0.1 reshape.149
  65.2 1.1 gather_fusion
  66.3 0.1 copy.10
  66.4 0.9 constant_dynamic-slice_fusion.1
  67.2 0.1 pad_add_fusion
  67.3 0.8 fusion.2
  68.1 0.3 compare_reduce_fusion
  68.3 0.3 fusion
  68.6 0.1 copy.11
  68.8 0.7 select_n.56.idx_ref
  69.5 42.7 %shard_map.38 = (bf16[8,12,128,128]{3,2,1,0:T(8,128)(2,1)}, bf16[8,24,128,128]{3,2,1,0:T(8,128)(2,1)}) custom-call(s32[3840]{0:T(1024)} %select_n.56.idx_ref, bf16[8,16,128,128]{3,2,1,0:T(8,128)(2,1)} %get-tuple-element.10.left_ref, bf16[128,128,128]{2,1,0:T(8,128)(2,1)} %bitcast.13, bf16[128,128,128]{2,1,0:T(8,128)(2,1)} %bitcast.11, ...), custom_call_target="tpu_custom_call" | custom-call | flops 6442450944 | bytes 24656896 | tf_op jit(solution)/shard_map/pallas_call | solution.py:202
  112.2 0.0 collective-permute-done
  112.3 0.0 collective-permute-done.1
  112.3 26.1 %shard_map.39 = bf16[8,6,128,128]{3,2,1,0:T(8,128)(2,1)} custom-call(s32[3840]{0:T(1024)} %select_n.56.idx_ref, bf16[8,24,128,128]{3,2,1,0:T(8,128)(2,1)} %get-tuple-element.13.left_hbm, bf16[128,128,128]{2,1,0:T(8,128)(2,1)} %bitcast.6.rest_0_, bf16[128,128,128]{2,1,0:T(8,128)(2,1)} %bitcast.14, bf16[128,128,128]{2,1,0:T(8,128)(2,1)} %bitcast.12, ...), custom_call_target="tpu_custom_call" | custom-call | flops 4831838208 | bytes 31996928 | tf_op jit(solution)/shard_map/pallas_call | solution.py:87
  (4 shorter events, 0.0 us)
Async XLA Ops:
  58.3 53.9 %collective-permute-start = (bf16[8,16,128,128]{3,2,1,0:T(8,128)(2,1)}, bf16[8,16,128,128]{3,2,1,0:T(8,128)(2,1)}, u32[]{:S(2)}, u32[]{:S(2)}) collective-permute-start(bf16[8,16,128,128]{3,2,1,0:T(8,128)(2,1)} %get-tuple-element.11), channel_id=1, source_target_pairs={{0,4},{4,8},{8,12},{12,16},{16,20},{20,24},{24,28},{28,32},{32,36}... | collective-permute-start | bytes 12582920 | tf_op jit(solution)/shard_map/ppermute | solution.py:14
  58.4 53.9 %collective-permute-start.1 = (bf16[8,16,128,128]{3,2,1,0:T(8,128)(2,1)}, bf16[8,16,128,128]{3,2,1,0:T(8,128)(2,1)}, u32[]{:S(2)}, u32[]{:S(2)}) collective-permute-start(bf16[8,16,128,128]{3,2,1,0:T(8,128)(2,1)} %get-tuple-element.12), channel_id=1, source_target_pairs={{0,252},{4,0},{8,4},{12,8},{16,12},{20,16},{24,20},{28,24},{32,28}... | collective-permute-start | bytes 12582920 | tf_op jit(solution)/shard_map/ppermute | solution.py:14

commit v16 on v15

--- a/solution.py
+++ b/solution.py
@@ -138,8 +138,9 @@
         copy.wait()
 
     def spread(row, k):
-        source = out_ref.at[row, pl.ds(0, n_own)]
-        target = spread_ref.at[row, pl.ds(depth_at * n_own, n_own)]
+        width = n_own if k == 0 else n_own - 1
+        source = out_ref.at[row, pl.ds(0, width)]
+        target = spread_ref.at[row, pl.ds(depth_at * n_own, width)]
         if k == 0:
             return pltpu.make_async_copy(source, target, send_sems.at[row, 0])
         return pltpu.make_async_remote_copy(
@@ -151,34 +152,43 @@
             device_id_type=MESH,
         )
 
-    def keep(row):
+    def keep(row, j):
+        last = n_own - 1
+        start, width, slot = [
+            (n_own, n_own, across * n_own),
+            (2 * n_own, 1, ahead * n_own + last),
+            (2 * n_own + 1, 1, behind * n_own + last),
+        ][j]
         return pltpu.make_async_copy(
-            out_ref.at[row, pl.ds(n_own, n_own)],
-            spread_ref.at[row, pl.ds(across * n_own, n_own)],
-            keep_sems.at[row],
-        )
-
-    def products(row, first):
+            out_ref.at[row, pl.ds(start, width)],
+            spread_ref.at[row, pl.ds(slot, width)],
+            keep_sems.at[row, j],
+        )
+
+    def products(row, first, count):
         for inner in range(n_inner):
             lcat[:, inner * edge:(inner + 1) * edge] = left_ref[row, inner]
 
-        for part in range(n_own):
+        for part in range(count):
             for inner in range(n_inner):
                 pick = table_pick(idx_ref, view, row, inner, first + part)
                 rcat[inner * edge:(inner + 1) * edge, part * edge:(part + 1) * edge] = halo[pick]
-        acc = jnp.dot(lcat[...], rcat[...], preferred_element_type=jnp.float32)
-        for part in range(n_own):
+        acc = jnp.dot(
+            lcat[...], rcat[:, : count * edge], preferred_element_type=jnp.float32
+        )
+        for part in range(count):
             out_ref[row, first + part] = acc[:, part * edge:(part + 1) * edge].astype(out_ref.dtype)
 
     def own_body(row, carry):
-        products(row, 0)
+        products(row, 0, n_own)
         for k in range(3):
             spread(row, k).start()
         return carry
 
     def across_body(row, carry):
-        products(row, n_own)
-        keep(row).start()
+        products(row, n_own, n_own + 2)
+        for j in range(3):
+            keep(row, j).start()
         return carry
 
     lax.fori_loop(0, row_count, own_body, 0)
@@ -186,7 +196,8 @@
     for row in range(row_count):
         for k in range(3):
             spread(row, k).wait()
-        keep(row).wait()
+        for j in range(3):
+            keep(row, j).wait()
 
 
 def square_products(table, left, pieces, depth_count, n_own, view):
@@ -197,12 +208,12 @@
     vmem = pl.BlockSpec(memory_space=pltpu.VMEM)
     anywhere = pl.BlockSpec(memory_space=pl.ANY)
     in_specs = [pl.BlockSpec(memory_space=pltpu.SMEM), vmem] + [anywhere] * len(pieces)
-    flops = 2 * rows * 2 * n_own * n_inner * edge ** 3
+    flops = 2 * rows * (2 * n_own + 2) * n_inner * edge ** 3
     moved = sum(int(x.size) * x.dtype.itemsize for x in operands) + rows * n_own * edge * edge * 10
     return pl.pallas_call(
         functools.partial(square_kernel, n_own, n_inner, len(pieces), view),
         out_shape=(
-            jax.ShapeDtypeStruct((rows, 2 * n_own, edge, edge), jnp.bfloat16),
+            jax.ShapeDtypeStruct((rows, 2 * n_own + 2, edge, edge), jnp.bfloat16),
             jax.ShapeDtypeStruct((rows, depth_count * n_own, edge, edge), jnp.bfloat16),
         ),
         in_specs=in_specs,
@@ -210,11 +221,11 @@
         scratch_shapes=[
             pltpu.VMEM((len(pieces) * span + 1, edge, edge), left.dtype),
             pltpu.VMEM((edge, n_inner * edge), left.dtype),
-            pltpu.VMEM((n_inner * edge, n_own * edge), left.dtype),
+            pltpu.VMEM((n_inner * edge, (n_own + 2) * edge), left.dtype),
             pltpu.SemaphoreType.DMA((len(pieces),)),
             pltpu.SemaphoreType.DMA((rows, 3)),
             pltpu.SemaphoreType.DMA((rows, 3)),
-            pltpu.SemaphoreType.DMA((rows,)),
+            pltpu.SemaphoreType.DMA((rows, 3)),
         ],
         compiler_params=pltpu.CompilerParams(
             vmem_limit_bytes=62 * 1024 * 1024, collective_id=0, has_side_effects=True
@@ -373,7 +384,14 @@
     halo_second = halo_of(2)
     piece_blocks = row_count * fill_count
     inner_rows = jnp.concatenate([own_cols, product_cols], axis=1)
-    targets = jnp.concatenate([own_targets, across_targets], axis=1)
+    ahead_last = lax.dynamic_slice_in_dim(
+        product_cols, ((depth_index + 1) % depth_count) * target_share + target_share - 1, 1, 1
+    )
+    behind_last = lax.dynamic_slice_in_dim(
+        product_cols,
+        ((depth_index + depth_count - 1) % depth_count) * target_share + target_share - 1, 1, 1,
+    )
+    targets = jnp.concatenate([own_targets, across_targets, ahead_last, behind_last], axis=1)
     table = block_table(
         block_cols, inner_rows, targets, (row_place - 2) * row_count, order_total,
         fill_count, len(halo_second) * piece_blocks,

time: 139 us -> 137 us (0.986)
  Pallas kernels: 127 us -> 122 us
  waiting for transfers between devices: 0.01 us -> 2.23 us
    pallas_call x1, Pallas kernels: 42.7 us -> 37.3 us  [square_products(): pl.pallas_call(functools.partial(square_kernel, n_own, n_inner, len(piece...]
    ppermute x2, waiting for transfers between devices: 0.01 us -> 2.23 us  [shifted(): return lax.ppermute(value, axis, pairs)]
  transfers between devices with their start and end apart: 2 -> 2, of which waited for: 0 -> 1; matrix products, arithmetic and copies ran while one was open for 4% -> 5% of each run, Pallas kernels for 31% -> 27%
where the time goes in v16:
time: 137 us; the launch traced here: 136 us
  Pallas kernels  122 us (89%)
  starting transfers between devices  5.14 us (4%)
  local copies, waits for them, and re-layouts  4.67 us (3%)
  other arithmetic  2.24 us (2%)
  waiting for transfers between devices  2.23 us (2%)
    pallas_call x1, Pallas kernels, halo_exchange(): pl.pallas_call(halo_kernel, out_shape=(whole, whole, whole), in_specs=[an...  58.3 us
    pallas_call x1, Pallas kernels, square_products(): pl.pallas_call(functools.partial(square_kernel, n_own, n_inner, len(piece...  37.3 us
    pallas_call x1, Pallas kernels, block_products(): pl.pallas_call(functools.partial(product_kernel, n_out, n_inner, len(piec...  26.3 us
    ppermute x2, starting transfers between devices, shifted(): return lax.ppermute(value, axis, pairs)  5.14 us
  transfers between devices with their start and end apart: 2, of which 1 were waited for; matrix products, arithmetic and copies ran while one was open for 5% of the time, Pallas kernels for 27%

profile of v16, /device:TPU:8, one launch (start us, length us, event | category | flops | bytes accessed | tf_op | source)
XLA Modules:
  0.0 136.2 jit_solution(10554371558152711257)
XLA Ops:
  0.0 58.3 %shard_map.37 = (bf16[8,16,128,128]{3,2,1,0:T(8,128)(2,1)}, bf16[8,16,128,128]{3,2,1,0:T(8,128)(2,1)}, bf16[8,16,128,128]{3,2,1,0:T(8,128)(2,1)}) custom-call(bf16[8,4,128,128]{3,2,1,0:T(8,128)(2,1)} %blocks_ref.1), custom_call_target="tpu_custom_call" | custom-call | bytes 15728640 | tf_op jit(solution)/shard_map/pallas_call | solution.py:340
  58.3 0.1 collective-permute-start
  58.4 5.1 %collective-permute-start.1 = (bf16[8,16,128,128]{3,2,1,0:T(8,128)(2,1)}, bf16[8,16,128,128]{3,2,1,0:T(8,128)(2,1)}, u32[]{:S(2)}, u32[]{:S(2)}) collective-permute-start(bf16[8,16,128,128]{3,2,1,0:T(8,128)(2,1)} %get-tuple-element.12), channel_id=1, source_target_pairs={{0,252},{4,0},{8,4},{12,8},{16,12},{20,16},{24,20},{28,24},{32,28}... | collective-permute-start | bytes 12582920 | tf_op jit(solution)/shard_map/ppermute | solution.py:14
  63.4 0.9 copy.9
  64.4 0.8 compare_select_fusion.1
  65.1 0.1 reshape.149
  65.2 1.1 gather_fusion
  66.3 0.1 copy.10
  66.4 0.8 fusion.2
  67.2 0.8 constant_dynamic-slice_fusion.3
  68.0 0.8 constant_dynamic-slice_fusion.1
  68.8 0.1 pad_add_fusion
  68.9 0.3 compare_reduce_fusion
  69.2 0.3 fusion
  69.5 0.1 copy.11
  69.7 0.7 select_n.74.idx_ref
  70.4 37.3 %shard_map.38 = (bf16[8,14,128,128]{3,2,1,0:T(8,128)(2,1)}, bf16[8,24,128,128]{3,2,1,0:T(8,128)(2,1)}) custom-call(s32[4480]{0:T(1024)} %select_n.74.idx_ref, bf16[8,16,128,128]{3,2,1,0:T(8,128)(2,1)} %get-tuple-element.10.left_ref, bf16[128,128,128]{2,1,0:T(8,128)(2,1)} %bitcast.13, bf16[128,128,128]{2,1,0:T(8,128)(2,1)} %bitcast.11, ...), custom_call_target="tpu_custom_call" | custom-call | flops 7516192768 | bytes 24659456 | tf_op jit(solution)/shard_map/pallas_call | solution.py:213
  107.7 2.2 %collective-permute-done = bf16[8,16,128,128]{3,2,1,0:T(8,128)(2,1)} collective-permute-done((bf16[8,16,128,128]{3,2,1,0:T(8,128)(2,1)}, bf16[8,16,128,128]{3,2,1,0:T(8,128)(2,1)}, u32[]{:S(2)}, u32[]{:S(2)}) %collective-permute-start) | collective-permute-done | bytes 4194336 | tf_op jit(solution)/shard_map/ppermute | solution.py:14
  109.9 0.0 collective-permute-done.1
  110.0 26.3 %shard_map.39 = bf16[8,6,128,128]{3,2,1,0:T(8,128)(2,1)} custom-call(s32[4480]{0:T(1024)} %select_n.74.idx_ref, bf16[8,24,128,128]{3,2,1,0:T(8,128)(2,1)} %get-tuple-element.13.left_hbm, bf16[128,128,128]{2,1,0:T(8,128)(2,1)} %bitcast.6.rest_0_, bf16[128,128,128]{2,1,0:T(8,128)(2,1)} %bitcast.14, bf16[128,128,128]{2,1,0:T(8,128)(2,1)} %bitcast.12, ...), custom_call_target="tpu_custom_call" | custom-call | flops 4831838208 | bytes 32523776 | tf_op jit(solution)/shard_map/pallas_call | solution.py:87
  (4 shorter events, 0.0 us)
Async XLA Ops:
  58.3 51.6 %collective-permute-start = (bf16[8,16,128,128]{3,2,1,0:T(8,128)(2,1)}, bf16[8,16,128,128]{3,2,1,0:T(8,128)(2,1)}, u32[]{:S(2)}, u32[]{:S(2)}) collective-permute-start(bf16[8,16,128,128]{3,2,1,0:T(8,128)(2,1)} %get-tuple-element.11), channel_id=1, source_target_pairs={{0,4},{4,8},{8,12},{12,16},{16,20},{20,24},{24,28},{28,32},{32,36}... | collective-permute-start | bytes 12582920 | tf_op jit(solution)/shard_map/ppermute | solution.py:14
  58.4 51.6 %collective-permute-start.1 = (bf16[8,16,128,128]{3,2,1,0:T(8,128)(2,1)}, bf16[8,16,128,128]{3,2,1,0:T(8,128)(2,1)}, u32[]{:S(2)}, u32[]{:S(2)}) collective-permute-start(bf16[8,16,128,128]{3,2,1,0:T(8,128)(2,1)} %get-tuple-element.12), channel_id=1, source_target_pairs={{0,252},{4,0},{8,4},{12,8},{16,12},{20,16},{24,20},{28,24},{32,28}... | collective-permute-start | bytes 12582920 | tf_op jit(solution)/shard_map/ppermute | solution.py:14

commit v17 on v16

--- a/solution.py
+++ b/solution.py
@@ -51,15 +51,16 @@
     for copy in copies:
         copy.wait()
 
-    def row_body(row, carry):
+    for row in range(left_ref.shape[0]):
+        lbuf, rbuf = lcat.at[row % 2], rcat.at[row % 2]
         for inner in range(n_inner):
-            lcat[:, inner * edge:(inner + 1) * edge] = left_ref[row, inner]
+            lbuf[:, inner * edge:(inner + 1) * edge] = left_ref[row, inner]
 
         for col in range(n_out):
             for inner in range(n_inner):
                 pick = table_pick(idx_ref, view, row, inner, col)
-                rcat[inner * edge:(inner + 1) * edge, col * edge:(col + 1) * edge] = halo[pick]
-        acc = jnp.dot(lcat[...], rcat[...], preferred_element_type=jnp.float32)
+                rbuf[inner * edge:(inner + 1) * edge, col * edge:(col + 1) * edge] = halo[pick]
+        acc = jnp.dot(lbuf[...], rbuf[...], preferred_element_type=jnp.float32)
         for col in range(n_out):
             part = acc[:, col * edge:(col + 1) * edge]
             if final:
@@ -67,9 +68,6 @@
             else:
                 value = part
             out_ref[row, col] = value.astype(out_ref.dtype)
-        return carry
-
-    lax.fori_loop(0, left_ref.shape[0], row_body, 0)
 
 
 def block_products(table, left, pieces, n_out, view, own=None):
@@ -91,8 +89,8 @@
         out_specs=vmem,
         scratch_shapes=[
             pltpu.VMEM((len(pieces) * span + 1, edge, edge), left.dtype),
-            pltpu.VMEM((edge, n_inner * edge), left.dtype),
-            pltpu.VMEM((n_inner * edge, n_out * edge), left.dtype),
+            pltpu.VMEM((2, edge, n_inner * edge), left.dtype),
+            pltpu.VMEM((2, n_inner * edge, n_out * edge), left.dtype),
             pltpu.VMEM(left.shape, left.dtype),
             pltpu.SemaphoreType.DMA((len(pieces) + 1,)),
         ],

time: 137 us -> 135 us (0.985)
  Pallas kernels: 122 us -> 120 us
    pallas_call x1, Pallas kernels: 26.3 us -> 24.8 us  [block_products(): pl.pallas_call(functools.partial(product_kernel, n_out, n_inner, len(piec...]
  transfers between devices with their start and end apart: 2 -> 2, of which waited for: 1 -> 1; matrix products, arithmetic and copies ran while one was open for 5% -> 5% of each run, Pallas kernels for 27% -> 28%
where the time goes in v17:
time: 135 us
  Pallas kernels  120 us (89%)
  starting transfers between devices  5.14 us (4%)
  local copies, waits for them, and re-layouts  4.67 us (3%)
  other arithmetic  2.24 us (2%)
  waiting for transfers between devices  2.24 us (2%)
    pallas_call x1, Pallas kernels, halo_exchange(): pl.pallas_call(halo_kernel, out_shape=(whole, whole, whole), in_specs=[an...  58.3 us
    pallas_call x1, Pallas kernels, square_products(): pl.pallas_call(functools.partial(square_kernel, n_own, n_inner, len(piece...  37.3 us
    pallas_call x1, Pallas kernels, block_products(): pl.pallas_call(functools.partial(product_kernel, n_out, n_inner, len(piec...  24.8 us
    ppermute x2, starting transfers between devices, shifted(): return lax.ppermute(value, axis, pairs)  5.14 us
  transfers between devices with their start and end apart: 2, of which 1 were waited for; matrix products, arithmetic and copies ran while one was open for 5% of the time, Pallas kernels for 28%

profile of v17, /device:TPU:8, one launch (start us, length us, event | category | flops | bytes accessed | tf_op | source)
XLA Modules:
  0.0 134.9 jit_solution(3522882585733364919)
XLA Ops:
  0.0 58.3 %shard_map.37 = (bf16[8,16,128,128]{3,2,1,0:T(8,128)(2,1)}, bf16[8,16,128,128]{3,2,1,0:T(8,128)(2,1)}, bf16[8,16,128,128]{3,2,1,0:T(8,128)(2,1)}) custom-call(bf16[8,4,128,128]{3,2,1,0:T(8,128)(2,1)} %blocks_ref.1), custom_call_target="tpu_custom_call" | custom-call | bytes 15728640 | tf_op jit(solution)/shard_map/pallas_call | solution.py:338
  58.3 0.1 collective-permute-start
  58.4 5.1 %collective-permute-start.1 = (bf16[8,16,128,128]{3,2,1,0:T(8,128)(2,1)}, bf16[8,16,128,128]{3,2,1,0:T(8,128)(2,1)}, u32[]{:S(2)}, u32[]{:S(2)}) collective-permute-start(bf16[8,16,128,128]{3,2,1,0:T(8,128)(2,1)} %get-tuple-element.12), channel_id=1, source_target_pairs={{0,252},{4,0},{8,4},{12,8},{16,12},{20,16},{24,20},{28,24},{32,28}... | collective-permute-start | bytes 12582920 | tf_op jit(solution)/shard_map/ppermute | solution.py:14
  63.4 0.9 copy.9
  64.4 0.8 compare_select_fusion.1
  65.1 0.1 reshape.149
  65.2 1.1 gather_fusion
  66.3 0.1 copy.10
  66.4 0.8 fusion.2
  67.2 0.8 constant_dynamic-slice_fusion.3
  68.0 0.8 constant_dynamic-slice_fusion.1
  68.8 0.1 pad_add_fusion
  68.9 0.3 compare_reduce_fusion
  69.2 0.3 fusion
  69.5 0.1 copy.11
  69.7 0.7 select_n.74.idx_ref
  70.4 37.3 %shard_map.38 = (bf16[8,14,128,128]{3,2,1,0:T(8,128)(2,1)}, bf16[8,24,128,128]{3,2,1,0:T(8,128)(2,1)}) custom-call(s32[4480]{0:T(1024)} %select_n.74.idx_ref, bf16[8,16,128,128]{3,2,1,0:T(8,128)(2,1)} %get-tuple-element.10.left_ref, bf16[128,128,128]{2,1,0:T(8,128)(2,1)} %bitcast.13, bf16[128,128,128]{2,1,0:T(8,128)(2,1)} %bitcast.11, ...), custom_call_target="tpu_custom_call" | custom-call | flops 7516192768 | bytes 24659456 | tf_op jit(solution)/shard_map/pallas_call | solution.py:211
  107.7 2.2 %collective-permute-done = bf16[8,16,128,128]{3,2,1,0:T(8,128)(2,1)} collective-permute-done((bf16[8,16,128,128]{3,2,1,0:T(8,128)(2,1)}, bf16[8,16,128,128]{3,2,1,0:T(8,128)(2,1)}, u32[]{:S(2)}, u32[]{:S(2)}) %collective-permute-start) | collective-permute-done | bytes 4194336 | tf_op jit(solution)/shard_map/ppermute | solution.py:14
  109.9 0.0 collective-permute-done.1
  110.0 24.8 %shard_map.39 = bf16[8,6,128,128]{3,2,1,0:T(8,128)(2,1)} custom-call(s32[4480]{0:T(1024)} %select_n.74.idx_ref, bf16[8,24,128,128]{3,2,1,0:T(8,128)(2,1)} %get-tuple-element.13.left_hbm, bf16[128,128,128]{2,1,0:T(8,128)(2,1)} %bitcast.6.rest_0_, bf16[128,128,128]{2,1,0:T(8,128)(2,1)} %bitcast.14, bf16[128,128,128]{2,1,0:T(8,128)(2,1)} %bitcast.12, ...), custom_call_target="tpu_custom_call" | custom-call | flops 4831838208 | bytes 32523776 | tf_op jit(solution)/shard_map/pallas_call | solution.py:85
  (4 shorter events, 0.0 us)
Async XLA Ops:
  58.3 51.6 %collective-permute-start = (bf16[8,16,128,128]{3,2,1,0:T(8,128)(2,1)}, bf16[8,16,128,128]{3,2,1,0:T(8,128)(2,1)}, u32[]{:S(2)}, u32[]{:S(2)}) collective-permute-start(bf16[8,16,128,128]{3,2,1,0:T(8,128)(2,1)} %get-tuple-element.11), channel_id=1, source_target_pairs={{0,4},{4,8},{8,12},{12,16},{16,20},{20,24},{24,28},{28,32},{32,36}... | collective-permute-start | bytes 12582920 | tf_op jit(solution)/shard_map/ppermute | solution.py:14
  58.4 51.6 %collective-permute-start.1 = (bf16[8,16,128,128]{3,2,1,0:T(8,128)(2,1)}, bf16[8,16,128,128]{3,2,1,0:T(8,128)(2,1)}, u32[]{:S(2)}, u32[]{:S(2)}) collective-permute-start(bf16[8,16,128,128]{3,2,1,0:T(8,128)(2,1)} %get-tuple-element.12), channel_id=1, source_target_pairs={{0,252},{4,0},{8,4},{12,8},{16,12},{20,16},{24,20},{28,24},{32,28}... | collective-permute-start | bytes 12582920 | tf_op jit(solution)/shard_map/ppermute | solution.py:14

commit v18 on v17

--- a/solution.py
+++ b/solution.py
@@ -41,17 +41,36 @@
         out_ref, halo, lcat, rcat, left_ref, sems = rest
     edge = left_ref.shape[-1]
     span = pieces[0].shape[0]
-    copies = [pltpu.make_async_copy(left_hbm, left_ref, sems.at[n_pieces])] + [
-        pltpu.make_async_copy(piece, halo.at[pl.ds(k * span, span)], sems.at[k])
-        for k, piece in enumerate(pieces)
-    ]
-    for copy in copies:
-        copy.start()
+    rows = left_ref.shape[0]
+    per_row = span // rows
+    halo_rows = n_pieces * rows
+    reach = (n_pieces - 1) * rows
+
+    def halo_copy(h):
+        piece = pieces[h // rows]
+        return pltpu.make_async_copy(
+            piece.at[pl.ds((h % rows) * per_row, per_row)],
+            halo.at[pl.ds(h * per_row, per_row)],
+            sems.at[h],
+        )
+
+    def left_copy(row):
+        return pltpu.make_async_copy(left_hbm.at[row], left_ref.at[row], sems.at[halo_rows + row])
+
+    def needed(row):
+        first = 0 if row == 0 else min(reach + row, halo_rows)
+        return range(first, min(reach + row + 1, halo_rows))
+
+    for row in range(rows):
+        for h in needed(row):
+            halo_copy(h).start()
+        left_copy(row).start()
     halo[n_pieces * span] = jnp.zeros((edge, edge), halo.dtype)
-    for copy in copies:
-        copy.wait()
 
     for row in range(left_ref.shape[0]):
+        for h in needed(row):
+            halo_copy(h).wait()
+        left_copy(row).wait()
         lbuf, rbuf = lcat.at[row % 2], rcat.at[row % 2]
         for inner in range(n_inner):
             lbuf[:, inner * edge:(inner + 1) * edge] = left_ref[row, inner]
@@ -92,7 +111,7 @@
             pltpu.VMEM((2, edge, n_inner * edge), left.dtype),
             pltpu.VMEM((2, n_inner * edge, n_out * edge), left.dtype),
             pltpu.VMEM(left.shape, left.dtype),
-            pltpu.SemaphoreType.DMA((len(pieces) + 1,)),
+            pltpu.SemaphoreType.DMA((len(pieces) * rows + rows,)),
         ],
         compiler_params=pltpu.CompilerParams(vmem_limit_bytes=62 * 1024 * 1024),
         cost_estimate=pl.CostEstimate(flops=flops, transcendentals=0, bytes_accessed=moved),

time: 135 us -> 134 us (level)
    pallas_call x1, Pallas kernels: 24.8 us -> 23.3 us  [block_products(): pl.pallas_call(functools.partial(product_kernel, n_out, n_inner, len(piec...]
where the time goes in v18:
time: 134 us; the launch traced here: 133 us
  Pallas kernels  119 us (89%)
  starting transfers between devices  5.14 us (4%)
  local copies, waits for them, and re-layouts  4.67 us (3%)
  other arithmetic  2.24 us (2%)
  waiting for transfers between devices  2.24 us (2%)
    pallas_call x1, Pallas kernels, halo_exchange(): pl.pallas_call(halo_kernel, out_shape=(whole, whole, whole), in_specs=[an...  58.3 us
    pallas_call x1, Pallas kernels, square_products(): pl.pallas_call(functools.partial(square_kernel, n_own, n_inner, len(piece...  37.3 us
    pallas_call x1, Pallas kernels, block_products(): pl.pallas_call(functools.partial(product_kernel, n_out, n_inner, len(piec...  23.3 us
    ppermute x2, starting transfers between devices, shifted(): return lax.ppermute(value, axis, pairs)  5.14 us
  transfers between devices with their start and end apart: 2, of which 1 were waited for; matrix products, arithmetic and copies ran while one was open for 5% of the time, Pallas kernels for 28%

profile of v18, /device:TPU:8, one launch (start us, length us, event | category | flops | bytes accessed | tf_op | source)
XLA Modules:
  0.0 133.4 jit_solution(15547784467641040471)
XLA Ops:
  0.0 58.3 %shard_map.37 = (bf16[8,16,128,128]{3,2,1,0:T(8,128)(2,1)}, bf16[8,16,128,128]{3,2,1,0:T(8,128)(2,1)}, bf16[8,16,128,128]{3,2,1,0:T(8,128)(2,1)}) custom-call(bf16[8,4,128,128]{3,2,1,0:T(8,128)(2,1)} %blocks_ref.1), custom_call_target="tpu_custom_call" | custom-call | bytes 15728640 | tf_op jit(solution)/shard_map/pallas_call | solution.py:357
  58.3 0.1 collective-permute-start
  58.4 5.1 %collective-permute-start.1 = (bf16[8,16,128,128]{3,2,1,0:T(8,128)(2,1)}, bf16[8,16,128,128]{3,2,1,0:T(8,128)(2,1)}, u32[]{:S(2)}, u32[]{:S(2)}) collective-permute-start(bf16[8,16,128,128]{3,2,1,0:T(8,128)(2,1)} %get-tuple-element.12), channel_id=1, source_target_pairs={{0,252},{4,0},{8,4},{12,8},{16,12},{20,16},{24,20},{28,24},{32,28}... | collective-permute-start | bytes 12582920 | tf_op jit(solution)/shard_map/ppermute | solution.py:14
  63.4 0.9 copy.9
  64.4 0.8 compare_select_fusion.1
  65.1 0.1 reshape.149
  65.2 1.1 gather_fusion
  66.3 0.1 copy.10
  66.4 0.8 fusion.2
  67.2 0.8 constant_dynamic-slice_fusion.3
  68.0 0.8 constant_dynamic-slice_fusion.1
  68.8 0.1 pad_add_fusion
  68.9 0.3 compare_reduce_fusion
  69.2 0.3 fusion
  69.5 0.1 copy.11
  69.7 0.7 select_n.74.idx_ref
  70.4 37.3 %shard_map.38 = (bf16[8,14,128,128]{3,2,1,0:T(8,128)(2,1)}, bf16[8,24,128,128]{3,2,1,0:T(8,128)(2,1)}) custom-call(s32[4480]{0:T(1024)} %select_n.74.idx_ref, bf16[8,16,128,128]{3,2,1,0:T(8,128)(2,1)} %get-tuple-element.10.left_ref, bf16[128,128,128]{2,1,0:T(8,128)(2,1)} %bitcast.13, bf16[128,128,128]{2,1,0:T(8,128)(2,1)} %bitcast.11, ...), custom_call_target="tpu_custom_call" | custom-call | flops 7516192768 | bytes 24659456 | tf_op jit(solution)/shard_map/pallas_call | solution.py:230
  107.7 2.2 %collective-permute-done = bf16[8,16,128,128]{3,2,1,0:T(8,128)(2,1)} collective-permute-done((bf16[8,16,128,128]{3,2,1,0:T(8,128)(2,1)}, bf16[8,16,128,128]{3,2,1,0:T(8,128)(2,1)}, u32[]{:S(2)}, u32[]{:S(2)}) %collective-permute-start) | collective-permute-done | bytes 4194336 | tf_op jit(solution)/shard_map/ppermute | solution.py:14
  109.9 0.0 collective-permute-done.1
  110.0 23.3 %shard_map.39 = bf16[8,6,128,128]{3,2,1,0:T(8,128)(2,1)} custom-call(s32[4480]{0:T(1024)} %select_n.74.idx_ref, bf16[8,24,128,128]{3,2,1,0:T(8,128)(2,1)} %get-tuple-element.13.left_hbm, bf16[128,128,128]{2,1,0:T(8,128)(2,1)} %bitcast.6.rest_0_, bf16[128,128,128]{2,1,0:T(8,128)(2,1)} %bitcast.14, bf16[128,128,128]{2,1,0:T(8,128)(2,1)} %bitcast.12, ...), custom_call_target="tpu_custom_call" | custom-call | flops 4831838208 | bytes 32523776 | tf_op jit(solution)/shard_map/pallas_call | solution.py:104
  (4 shorter events, 0.0 us)
Async XLA Ops:
  58.3 51.6 %collective-permute-start = (bf16[8,16,128,128]{3,2,1,0:T(8,128)(2,1)}, bf16[8,16,128,128]{3,2,1,0:T(8,128)(2,1)}, u32[]{:S(2)}, u32[]{:S(2)}) collective-permute-start(bf16[8,16,128,128]{3,2,1,0:T(8,128)(2,1)} %get-tuple-element.11), channel_id=1, source_target_pairs={{0,4},{4,8},{8,12},{12,16},{16,20},{20,24},{24,28},{28,32},{32,36}... | collective-permute-start | bytes 12582920 | tf_op jit(solution)/shard_map/ppermute | solution.py:14
  58.4 51.6 %collective-permute-start.1 = (bf16[8,16,128,128]{3,2,1,0:T(8,128)(2,1)}, bf16[8,16,128,128]{3,2,1,0:T(8,128)(2,1)}, u32[]{:S(2)}, u32[]{:S(2)}) collective-permute-start(bf16[8,16,128,128]{3,2,1,0:T(8,128)(2,1)} %get-tuple-element.12), channel_id=1, source_target_pairs={{0,252},{4,0},{8,4},{12,8},{16,12},{20,16},{24,20},{28,24},{32,28}... | collective-permute-start | bytes 12582920 | tf_op jit(solution)/shard_map/ppermute | solution.py:14

commit v19 on v18

--- a/solution.py
+++ b/solution.py
@@ -39,9 +39,9 @@
         own_ref, out_ref, halo, lcat, rcat, left_ref, sems = rest
     else:
         out_ref, halo, lcat, rcat, left_ref, sems = rest
-    edge = left_ref.shape[-1]
+    edge = left_hbm.shape[-1]
     span = pieces[0].shape[0]
-    rows = left_ref.shape[0]
+    rows = left_hbm.shape[0]
     per_row = span // rows
     halo_rows = n_pieces * rows
     reach = (n_pieces - 1) * rows
@@ -54,26 +54,30 @@
             sems.at[h],
         )
 
-    def left_copy(row):
-        return pltpu.make_async_copy(left_hbm.at[row], left_ref.at[row], sems.at[halo_rows + row])
+    def left_copy(row, inner):
+        return pltpu.make_async_copy(
+            left_hbm.at[row, inner],
+            left_ref.at[row, :, pl.ds(inner * edge, edge)],
+            sems.at[halo_rows + row * n_inner + inner],
+        )
 
     def needed(row):
         first = 0 if row == 0 else min(reach + row, halo_rows)
         return range(first, min(reach + row + 1, halo_rows))
 
     for row in range(rows):
+        for inner in range(n_inner):
+            left_copy(row, inner).start()
         for h in needed(row):
             halo_copy(h).start()
-        left_copy(row).start()
     halo[n_pieces * span] = jnp.zeros((edge, edge), halo.dtype)
 
-    for row in range(left_ref.shape[0]):
+    for row in range(rows):
         for h in needed(row):
             halo_copy(h).wait()
-        left_copy(row).wait()
-        lbuf, rbuf = lcat.at[row % 2], rcat.at[row % 2]
         for inner in range(n_inner):
-            lbuf[:, inner * edge:(inner + 1) * edge] = left_ref[row, inner]
+            left_copy(row, inner).wait()
+        lbuf, rbuf = left_ref.at[row], rcat.at[row % 2]
 
         for col in range(n_out):
             for inner in range(n_inner):
@@ -108,10 +112,10 @@
         out_specs=vmem,
         scratch_shapes=[
             pltpu.VMEM((len(pieces) * span + 1, edge, edge), left.dtype),
-            pltpu.VMEM((2, edge, n_inner * edge), left.dtype),
+            pltpu.VMEM((1, 1), left.dtype),
             pltpu.VMEM((2, n_inner * edge, n_out * edge), left.dtype),
-            pltpu.VMEM(left.shape, left.dtype),
-            pltpu.SemaphoreType.DMA((len(pieces) * rows + rows,)),
+            pltpu.VMEM((rows, edge, n_inner * edge), left.dtype),
+            pltpu.SemaphoreType.DMA((len(pieces) * rows + rows * n_inner,)),
         ],
         compiler_params=pltpu.CompilerParams(vmem_limit_bytes=62 * 1024 * 1024),
         cost_estimate=pl.CostEstimate(flops=flops, transcendentals=0, bytes_accessed=moved),

time: 134 us -> 135 us (level)
  no operation moved by 1% of the time
where the time goes in v19:
time: 135 us
  Pallas kernels  120 us (89%)
  starting transfers between devices  5.14 us (4%)
  local copies, waits for them, and re-layouts  4.67 us (3%)
  other arithmetic  2.24 us (2%)
  waiting for transfers between devices  2.24 us (2%)
    pallas_call x1, Pallas kernels, halo_exchange(): pl.pallas_call(halo_kernel, out_shape=(whole, whole, whole), in_specs=[an...  58.3 us
    pallas_call x1, Pallas kernels, square_products(): pl.pallas_call(functools.partial(square_kernel, n_own, n_inner, len(piece...  37.3 us
    pallas_call x1, Pallas kernels, block_products(): pl.pallas_call(functools.partial(product_kernel, n_out, n_inner, len(piec...  24.4 us
    ppermute x2, starting transfers between devices, shifted(): return lax.ppermute(value, axis, pairs)  5.14 us
  transfers between devices with their start and end apart: 2, of which 1 were waited for; matrix products, arithmetic and copies ran while one was open for 5% of the time, Pallas kernels for 28%

profile of v19, /device:TPU:8, one launch (start us, length us, event | category | flops | bytes accessed | tf_op | source)
XLA Modules:
  0.0 134.5 jit_solution(18426351183006582694)
XLA Ops:
  0.0 58.3 %shard_map.37 = (bf16[8,16,128,128]{3,2,1,0:T(8,128)(2,1)}, bf16[8,16,128,128]{3,2,1,0:T(8,128)(2,1)}, bf16[8,16,128,128]{3,2,1,0:T(8,128)(2,1)}) custom-call(bf16[8,4,128,128]{3,2,1,0:T(8,128)(2,1)} %blocks_ref.1), custom_call_target="tpu_custom_call" | custom-call | bytes 15728640 | tf_op jit(solution)/shard_map/pallas_call | solution.py:361
  58.3 0.1 collective-permute-start
  58.4 5.1 %collective-permute-start.1 = (bf16[8,16,128,128]{3,2,1,0:T(8,128)(2,1)}, bf16[8,16,128,128]{3,2,1,0:T(8,128)(2,1)}, u32[]{:S(2)}, u32[]{:S(2)}) collective-permute-start(bf16[8,16,128,128]{3,2,1,0:T(8,128)(2,1)} %get-tuple-element.12), channel_id=1, source_target_pairs={{0,252},{4,0},{8,4},{12,8},{16,12},{20,16},{24,20},{28,24},{32,28}... | collective-permute-start | bytes 12582920 | tf_op jit(solution)/shard_map/ppermute | solution.py:14
  63.4 0.9 copy.9
  64.4 0.8 compare_select_fusion.1
  65.1 0.1 reshape.149
  65.2 1.1 gather_fusion
  66.3 0.1 copy.10
  66.4 0.8 fusion.2
  67.2 0.8 constant_dynamic-slice_fusion.3
  68.0 0.8 constant_dynamic-slice_fusion.1
  68.8 0.1 pad_add_fusion
  68.9 0.3 compare_reduce_fusion
  69.2 0.3 fusion
  69.5 0.1 copy.11
  69.7 0.7 select_n.74.idx_ref
  70.4 37.3 %shard_map.38 = (bf16[8,14,128,128]{3,2,1,0:T(8,128)(2,1)}, bf16[8,24,128,128]{3,2,1,0:T(8,128)(2,1)}) custom-call(s32[4480]{0:T(1024)} %select_n.74.idx_ref, bf16[8,16,128,128]{3,2,1,0:T(8,128)(2,1)} %get-tuple-element.10.left_ref, bf16[128,128,128]{2,1,0:T(8,128)(2,1)} %bitcast.13, bf16[128,128,128]{2,1,0:T(8,128)(2,1)} %bitcast.11, ...), custom_call_target="tpu_custom_call" | custom-call | flops 7516192768 | bytes 24659456 | tf_op jit(solution)/shard_map/pallas_call | solution.py:234
  107.7 2.2 %collective-permute-done = bf16[8,16,128,128]{3,2,1,0:T(8,128)(2,1)} collective-permute-done((bf16[8,16,128,128]{3,2,1,0:T(8,128)(2,1)}, bf16[8,16,128,128]{3,2,1,0:T(8,128)(2,1)}, u32[]{:S(2)}, u32[]{:S(2)}) %collective-permute-start) | collective-permute-done | bytes 4194336 | tf_op jit(solution)/shard_map/ppermute | solution.py:14
  109.9 0.0 collective-permute-done.1
  110.0 24.4 %shard_map.39 = bf16[8,6,128,128]{3,2,1,0:T(8,128)(2,1)} custom-call(s32[4480]{0:T(1024)} %select_n.74.idx_ref, bf16[8,24,128,128]{3,2,1,0:T(8,128)(2,1)} %get-tuple-element.13.left_hbm, bf16[128,128,128]{2,1,0:T(8,128)(2,1)} %bitcast.6.rest_0_, bf16[128,128,128]{2,1,0:T(8,128)(2,1)} %bitcast.14, bf16[128,128,128]{2,1,0:T(8,128)(2,1)} %bitcast.12, ...), custom_call_target="tpu_custom_call" | custom-call | flops 4831838208 | bytes 32523776 | tf_op jit(solution)/shard_map/pallas_call | solution.py:108
  (4 shorter events, 0.0 us)
Async XLA Ops:
  58.3 51.6 %collective-permute-start = (bf16[8,16,128,128]{3,2,1,0:T(8,128)(2,1)}, bf16[8,16,128,128]{3,2,1,0:T(8,128)(2,1)}, u32[]{:S(2)}, u32[]{:S(2)}) collective-permute-start(bf16[8,16,128,128]{3,2,1,0:T(8,128)(2,1)} %get-tuple-element.11), channel_id=1, source_target_pairs={{0,4},{4,8},{8,12},{12,16},{16,20},{20,24},{24,28},{28,32},{32,36}... | collective-permute-start | bytes 12582920 | tf_op jit(solution)/shard_map/ppermute | solution.py:14
  58.4 51.6 %collective-permute-start.1 = (bf16[8,16,128,128]{3,2,1,0:T(8,128)(2,1)}, bf16[8,16,128,128]{3,2,1,0:T(8,128)(2,1)}, u32[]{:S(2)}, u32[]{:S(2)}) collective-permute-start(bf16[8,16,128,128]{3,2,1,0:T(8,128)(2,1)} %get-tuple-element.12), channel_id=1, source_target_pairs={{0,252},{4,0},{8,4},{12,8},{16,12},{20,16},{24,20},{28,24},{32,28}... | collective-permute-start | bytes 12582920 | tf_op jit(solution)/shard_map/ppermute | solution.py:14

commit v20 on v18

--- a/solution.py
+++ b/solution.py
@@ -36,9 +36,9 @@
     pieces = rest[:n_pieces]
     rest = rest[n_pieces:]
     if final:
-        own_ref, out_ref, halo, lcat, rcat, left_ref, sems = rest
+        own_ref, out_hbm, halo, lcat, rcat, left_ref, out_ref, sems = rest
     else:
-        out_ref, halo, lcat, rcat, left_ref, sems = rest
+        out_hbm, halo, lcat, rcat, left_ref, out_ref, sems = rest
     edge = left_ref.shape[-1]
     span = pieces[0].shape[0]
     rows = left_ref.shape[0]
@@ -56,6 +56,11 @@
 
     def left_copy(row):
         return pltpu.make_async_copy(left_hbm.at[row], left_ref.at[row], sems.at[halo_rows + row])
+
+    def out_copy(row):
+        return pltpu.make_async_copy(
+            out_ref.at[row], out_hbm.at[row], sems.at[halo_rows + rows + row]
+        )
 
     def needed(row):
         first = 0 if row == 0 else min(reach + row, halo_rows)
@@ -87,6 +92,9 @@
             else:
                 value = part
             out_ref[row, col] = value.astype(out_ref.dtype)
+        out_copy(row).start()
+    for row in range(rows):
+        out_copy(row).wait()
 
 
 def block_products(table, left, pieces, n_out, view, own=None):
@@ -105,13 +113,14 @@
         functools.partial(product_kernel, n_out, n_inner, len(pieces), final, view),
         out_shape=jax.ShapeDtypeStruct((rows, n_out, edge, edge), jnp.bfloat16),
         in_specs=in_specs,
-        out_specs=vmem,
+        out_specs=anywhere,
         scratch_shapes=[
             pltpu.VMEM((len(pieces) * span + 1, edge, edge), left.dtype),
             pltpu.VMEM((2, edge, n_inner * edge), left.dtype),
             pltpu.VMEM((2, n_inner * edge, n_out * edge), left.dtype),
             pltpu.VMEM(left.shape, left.dtype),
-            pltpu.SemaphoreType.DMA((len(pieces) * rows + rows,)),
+            pltpu.VMEM((rows, n_out, edge, edge), jnp.bfloat16),
+            pltpu.SemaphoreType.DMA((len(pieces) * rows + 2 * rows,)),
         ],
         compiler_params=pltpu.CompilerParams(vmem_limit_bytes=62 * 1024 * 1024),
         cost_estimate=pl.CostEstimate(flops=flops, transcendentals=0, bytes_accessed=moved),

time: 134 us -> 133 us (level)
  no operation moved by 1% of the time
where the time goes in v20:
time: 133 us
  Pallas kernels  118 us (89%)
  starting transfers between devices  5.14 us (4%)
  local copies, waits for them, and re-layouts  4.67 us (4%)
  other arithmetic  2.24 us (2%)
  waiting for transfers between devices  2.24 us (2%)
    pallas_call x1, Pallas kernels, halo_exchange(): pl.pallas_call(halo_kernel, out_shape=(whole, whole, whole), in_specs=[an...  58.3 us
    pallas_call x1, Pallas kernels, square_products(): pl.pallas_call(functools.partial(square_kernel, n_own, n_inner, len(piece...  37.3 us
    pallas_call x1, Pallas kernels, block_products(): pl.pallas_call(functools.partial(product_kernel, n_out, n_inner, len(piec...  22.9 us
    ppermute x2, starting transfers between devices, shifted(): return lax.ppermute(value, axis, pairs)  5.14 us
  transfers between devices with their start and end apart: 2, of which 1 were waited for; matrix products, arithmetic and copies ran while one was open for 5% of the time, Pallas kernels for 28%

profile of v20, /device:TPU:8, one launch (start us, length us, event | category | flops | bytes accessed | tf_op | source)
XLA Modules:
  0.0 133.0 jit_solution(14285700267856646034)
XLA Ops:
  0.0 58.3 %shard_map.37 = (bf16[8,16,128,128]{3,2,1,0:T(8,128)(2,1)}, bf16[8,16,128,128]{3,2,1,0:T(8,128)(2,1)}, bf16[8,16,128,128]{3,2,1,0:T(8,128)(2,1)}) custom-call(bf16[8,4,128,128]{3,2,1,0:T(8,128)(2,1)} %blocks_ref.1), custom_call_target="tpu_custom_call" | custom-call | bytes 15728640 | tf_op jit(solution)/shard_map/pallas_call | solution.py:366
  58.3 0.1 collective-permute-start
  58.4 5.1 %collective-permute-start.1 = (bf16[8,16,128,128]{3,2,1,0:T(8,128)(2,1)}, bf16[8,16,128,128]{3,2,1,0:T(8,128)(2,1)}, u32[]{:S(2)}, u32[]{:S(2)}) collective-permute-start(bf16[8,16,128,128]{3,2,1,0:T(8,128)(2,1)} %get-tuple-element.12), channel_id=1, source_target_pairs={{0,252},{4,0},{8,4},{12,8},{16,12},{20,16},{24,20},{28,24},{32,28}... | collective-permute-start | bytes 12582920 | tf_op jit(solution)/shard_map/ppermute | solution.py:14
  63.4 0.9 copy.9
  64.4 0.8 compare_select_fusion.1
  65.1 0.1 reshape.149
  65.2 1.1 gather_fusion
  66.3 0.1 copy.10
  66.4 0.8 fusion.2
  67.2 0.8 constant_dynamic-slice_fusion.3
  68.0 0.8 constant_dynamic-slice_fusion.1
  68.8 0.1 pad_add_fusion
  68.9 0.3 compare_reduce_fusion
  69.2 0.3 fusion
  69.5 0.1 copy.11
  69.7 0.7 select_n.74.idx_ref
  70.4 37.3 %shard_map.38 = (bf16[8,14,128,128]{3,2,1,0:T(8,128)(2,1)}, bf16[8,24,128,128]{3,2,1,0:T(8,128)(2,1)}) custom-call(s32[4480]{0:T(1024)} %select_n.74.idx_ref, bf16[8,16,128,128]{3,2,1,0:T(8,128)(2,1)} %get-tuple-element.10.left_ref, bf16[128,128,128]{2,1,0:T(8,128)(2,1)} %bitcast.13, bf16[128,128,128]{2,1,0:T(8,128)(2,1)} %bitcast.11, ...), custom_call_target="tpu_custom_call" | custom-call | flops 7516192768 | bytes 24659456 | tf_op jit(solution)/shard_map/pallas_call | solution.py:239
  107.7 2.2 %collective-permute-done = bf16[8,16,128,128]{3,2,1,0:T(8,128)(2,1)} collective-permute-done((bf16[8,16,128,128]{3,2,1,0:T(8,128)(2,1)}, bf16[8,16,128,128]{3,2,1,0:T(8,128)(2,1)}, u32[]{:S(2)}, u32[]{:S(2)}) %collective-permute-start) | collective-permute-done | bytes 4194336 | tf_op jit(solution)/shard_map/ppermute | solution.py:14
  109.9 0.0 collective-permute-done.1
  110.0 22.9 %shard_map.39 = bf16[8,6,128,128]{3,2,1,0:T(8,128)(2,1)} custom-call(s32[4480]{0:T(1024)} %select_n.74.idx_ref, bf16[8,24,128,128]{3,2,1,0:T(8,128)(2,1)} %get-tuple-element.13.left_hbm, bf16[128,128,128]{2,1,0:T(8,128)(2,1)} %bitcast.6.rest_0_, bf16[128,128,128]{2,1,0:T(8,128)(2,1)} %bitcast.14, bf16[128,128,128]{2,1,0:T(8,128)(2,1)} %bitcast.12, ...), custom_call_target="tpu_custom_call" | custom-call | flops 4831838208 | bytes 32523776 | tf_op jit(solution)/shard_map/pallas_call | solution.py:112
  (4 shorter events, 0.0 us)
Async XLA Ops:
  58.3 51.6 %collective-permute-start = (bf16[8,16,128,128]{3,2,1,0:T(8,128)(2,1)}, bf16[8,16,128,128]{3,2,1,0:T(8,128)(2,1)}, u32[]{:S(2)}, u32[]{:S(2)}) collective-permute-start(bf16[8,16,128,128]{3,2,1,0:T(8,128)(2,1)} %get-tuple-element.11), channel_id=1, source_target_pairs={{0,4},{4,8},{8,12},{12,16},{16,20},{20,24},{24,28},{28,32},{32,36}... | collective-permute-start | bytes 12582920 | tf_op jit(solution)/shard_map/ppermute | solution.py:14
  58.4 51.6 %collective-permute-start.1 = (bf16[8,16,128,128]{3,2,1,0:T(8,128)(2,1)}, bf16[8,16,128,128]{3,2,1,0:T(8,128)(2,1)}, u32[]{:S(2)}, u32[]{:S(2)}) collective-permute-start(bf16[8,16,128,128]{3,2,1,0:T(8,128)(2,1)} %get-tuple-element.12), channel_id=1, source_target_pairs={{0,252},{4,0},{8,4},{12,8},{16,12},{20,16},{24,20},{28,24},{32,28}... | collective-permute-start | bytes 12582920 | tf_op jit(solution)/shard_map/ppermute | solution.py:14
